TPU v7x, 768 devices: a whole 4x8x12 slice. The times are simulated.
768 devices in a mesh: elem: 96 (over z_lo, y, core), band: 8 (over z_hi, x).
Axes of the slice: x: 4, y: 8, z: 12 (z_hi: 2, z_lo: 6; z = z_hi * 6 + z_lo), core: 2. Of those that a mesh axis runs over, the one named last changes fastest.
Arguments:
- orbitals: bfloat16 [96, 512, 13824], P('elem', 'band'), may hold values from -6 to 6
- potential: float32 [96, 13824], P('elem'), may hold values from 0 to 1.9
- basis_count: int32 [96], P('elem'), may hold values from 256 to 512, as said below
- states: bfloat16 [96, 512, 1024], P('elem', None, 'band'), may hold values from -6 to 6
Outputs:
- filtered_states: bfloat16 [96, 512, 1024], P('elem', None, 'band')
Inputs may be any that keep to these rules, and one draw needn't show every extreme that they name: `basis_count`: some element keeps all 512 basis functions and some element keeps 512 // 2 of them in every draw.
All inputs are finite; a program needn't handle non-finite values.
Results may differ from a plain program's by a relative error of at most 0.03.
Values may be sent and summed in bfloat16 or wider, within the bound.
No kernel may reach another device: no remote copies, remote signals or barrier semaphores. Data moves between devices by JAX's collectives and lax.ppermute only.
A program may use at most 32 MiB of HBM per device.

v0:
```python
import jax
import jax.numpy as jnp
from jax import lax
from jax.sharding import PartitionSpec as P

P_SIZE = 24
G = 13824
EB = 4


LOW_EDGE = 4.0
HIGH_EDGE = 14.0
PENALTY = 1.0
SHIFT_CENTER = 4.0
HALF_WIDTH = 6.0
HIGHEST = lax.Precision.HIGHEST


def with_halo(value, sides, width):
    for axis, dim in sides:
        devices, length = (lax.axis_size(axis), value.shape[dim])
        up = [(i, (i + 1) % devices) for i in range(devices - 1)]
        down = [(j, i) for i, j in up]
        last = lax.slice_in_dim(value, length - width, length, axis=dim)
        initial = lax.slice_in_dim(value, 0, width, axis=dim)
        before = lax.ppermute(last, axis, up)
        after = lax.ppermute(initial, axis, down)
        value = jnp.concatenate([before, value, after], axis=dim)
    return value


def from_behind(value, axis, by):
    devices = lax.axis_size(axis)
    return lax.ppermute(value, axis, [(i, (i + by) % devices) for i in range(devices)])


def side_masks(length):
    where = jnp.arange(length, dtype=jnp.int32)
    zpos = where % P_SIZE
    ypos = where // P_SIZE % P_SIZE
    return (
        (zpos < P_SIZE - 1).astype(jnp.float32),
        (zpos > 0).astype(jnp.float32),
        (ypos < P_SIZE - 1).astype(jnp.float32),
        (ypos > 0).astype(jnp.float32),
    )


def flat_stencil(padded, length, masks):
    plane = P_SIZE * P_SIZE
    values = padded[:, plane : plane + length]
    beside = padded[:, 2 * plane : 2 * plane + length] + padded[:, 0:length]
    beside = beside + masks[0] * padded[:, plane + 1 : plane + 1 + length]
    beside = beside + masks[1] * padded[:, plane - 1 : plane - 1 + length]
    beside = beside + masks[2] * padded[:, plane + P_SIZE : plane + P_SIZE + length]
    beside = beside + masks[3] * padded[:, plane - P_SIZE : plane - P_SIZE + length]
    return (values, 6.0 * values - beside)


def flat_hamiltonian(values, potential, masks):
    plane = P_SIZE * P_SIZE
    padded = jnp.pad(values, ((0, 0), (plane, plane)))
    middle_values, laplace = flat_stencil(padded, values.shape[1], masks)
    return laplace + potential * middle_values


def filtered_basis(orbitals, potential, kept_count, start_index):
    orbital_count = orbitals.shape[0]
    masks = side_masks(G)
    middle = 0.5 * (HIGH_EDGE + LOW_EDGE)
    spread = 0.5 * (HIGH_EDGE - LOW_EDGE)
    previous = orbitals.astype(jnp.float32)
    current = (flat_hamiltonian(previous, potential, masks) - middle * previous) / spread
    following = (
        2.0 * (flat_hamiltonian(current, potential, masks) - middle * current) / spread - previous
    )
    previous, current = (current, following)
    magnitude = jnp.sqrt(jnp.mean(current * current, axis=1, keepdims=True) + 1e-06)
    active = start_index + jnp.arange(orbital_count, dtype=jnp.int32) < kept_count
    return jnp.where(active[:, None], current / magnitude, 0.0).astype(jnp.bfloat16)


def slab_applied(slab_rows, slab_potential):
    length = slab_rows.shape[1]
    padded = with_halo(slab_rows, (("band", 1),), P_SIZE * P_SIZE).astype(jnp.float32)
    values, laplace = flat_stencil(padded, length, side_masks(length))
    return (laplace + slab_potential * values).astype(jnp.bfloat16)


def face_pair(gridded, axis_place, upper):
    extent = gridded.shape[axis_place]
    surface = lax.index_in_dim(gridded, extent - 1 if upper else 0, axis_place, keepdims=False)
    beneath = lax.index_in_dim(gridded, extent - 2 if upper else 1, axis_place, keepdims=False)
    return (surface, beneath)


def face_terms(own_surface, own_beneath, other_surface, other_beneath):
    own_slope = own_surface - own_beneath
    other_slope = other_surface - other_beneath
    leading = jnp.concatenate(
        [-PENALTY * own_surface + 0.5 * own_slope, 0.5 * own_surface], axis=-1
    )
    trailing = jnp.concatenate([other_surface, other_slope], axis=-1)
    return (leading, trailing)


def apply_blocks(terms, current):
    offsets = [0, 1, -1, EB, -EB]
    running = jnp.zeros((terms[0][0].shape[0], current.shape[1]), jnp.float32)
    for position, offset in enumerate(offsets):
        matrix, contract = terms[position]
        if offset == 0:
            source = current
        else:
            source = from_behind(current, "elem", -offset)
        running = running + lax.dot_general(
            matrix, source, (((contract,), (0,)), ((), ())), preferred_element_type=jnp.float32
        )
    return running


def scaled(terms, current):
    return (apply_blocks(terms, current) - SHIFT_CENTER * current.astype(jnp.float32)) / HALF_WIDTH


def on_device(orbitals, potential, basis_count, states):
    per_device = orbitals.shape[1]
    band_place = lax.axis_index("band")
    start_index = band_place * per_device
    basis = filtered_basis(orbitals[0], potential[0], basis_count[0], start_index)
    basis_rows = lax.all_to_all(basis, "band", split_axis=1, concat_axis=0, tiled=True)
    orbital_count = basis_rows.shape[0]
    slab_length = basis_rows.shape[1]
    planes = slab_length // (P_SIZE * P_SIZE)
    slab_potential = lax.dynamic_slice_in_dim(
        potential[0], band_place * slab_length, slab_length, 0
    )
    applied_rows = slab_applied(basis_rows, slab_potential)
    interior = lax.dot_general(
        basis_rows, applied_rows, (((1,), (1,)), ((), ())), preferred_element_type=jnp.float32
    ) * (1.0 / G)
    half_grid = basis_rows.reshape(orbital_count, planes, P_SIZE, P_SIZE)
    directions = [
        (1, 1, True, False),
        (-1, 1, False, True),
        (EB, 0, True, False),
        (-EB, 0, False, True),
    ]
    partials = [interior]
    for offset, axis_code, own_upper, other_upper in directions:
        outgoing = jnp.stack(face_pair(half_grid, 2 + axis_code, other_upper))
        received = from_behind(outgoing, "elem", -offset)
        own_surface, own_beneath = face_pair(half_grid, 2 + axis_code, own_upper)
        leading, trailing = face_terms(
            own_surface.reshape(orbital_count, -1).astype(jnp.float32),
            own_beneath.reshape(orbital_count, -1).astype(jnp.float32),
            received[0].reshape(orbital_count, -1).astype(jnp.float32),
            received[1].reshape(orbital_count, -1).astype(jnp.float32),
        )
        partials.append(
            lax.dot_general(
                leading,
                trailing,
                (((1,), (1,)), ((), ())),
                precision=HIGHEST,
                preferred_element_type=jnp.float32,
            )
            * (1.0 / (P_SIZE * P_SIZE))
        )
    rounded = jnp.stack(partials).astype(jnp.bfloat16).astype(jnp.float32)
    summed = lax.psum(rounded.astype(jnp.bfloat16), "band")
    terms = [(summed[position], 1) for position in range(5)]
    start_states = states[0]
    first_term = scaled(terms, start_states).astype(jnp.bfloat16)
    second_term = (2.0 * scaled(terms, first_term) - start_states.astype(jnp.float32)).astype(
        jnp.bfloat16
    )
    third_term = 2.0 * scaled(terms, second_term) - first_term.astype(jnp.float32)
    magnitude = jnp.sqrt(jnp.mean(third_term * third_term, axis=0, keepdims=True) + 1e-06)
    return (third_term / magnitude).astype(jnp.bfloat16)[None]


def solution(mesh):
    placed = (P("elem", "band", None), P("elem", None), P("elem"), P("elem", None, "band"))
    return jax.shard_map(
        on_device, mesh=mesh, in_specs=placed, out_specs=P("elem", None, "band"), check_vma=False
    )
```

profile of v0, /device:TPU:6, one launch (start us, length us, event | category | flops | bytes accessed | tf_op | source)
XLA Modules:
  0.0 511.5 jit_solution(13479355668238107868)
XLA Ops:
  6.6 3.6 bitcast_convert_fusion
  10.4 14.1 %broadcast_multiply_fusion = (f32[64,13824]{1,0:T(8,128)S(1)}, f32[64,13824]{1,0:T(8,128)S(1)}) fusion(f32[13824]{0:T(1024)S(1)} %reduce, f32[13824]{0:T(1024)S(1)} %get-tuple-element.39, f32[13824]{0:T(1024)S(1)} %get-tuple-element.40, f32[13824]{0:T(1024)S(1)} %get-tuple-element.38, f32[13824]{0:T(1024)S(1)} %get-tuple-element.37, ...), kind=kLoop, calls=%fused_computation.35 | loop fusion | flops 15040512 | bytes 12662784 | tf_op jit(solution)/shard_map/div | solution.py:73
  24.5 7.0 %multiply_reduce_fusion = (f32[64]{0:T(128)S(1)}, f32[64,13824]{1,0:T(8,128)}) fusion(bf16[1,64,13824]{2,1,0:T(8,128)(2,1)S(1)} %copy-done.1, f32[64,13824]{1,0:T(8,128)S(1)} %get-tuple-element.8, f32[13824]{0:T(1024)S(1)} %broadcast_multiply_fusion.1, f32[13824]{0:T(1024)S(1)} %get-tuple-element.39, f32[13824]{0:T(1024)S(1)} %get-tuple-element.40, ...), kind=kLoop, calls=%fused_computation.20 | loop fusion | flops 17694656 | bytes 12663040 | tf_op jit(solution)/shard_map/reduce_sum | solution.py:78
  32.2 3.6 select_convert_fusion
  35.8 3.2 all_to_all.14
  39.1 1.6 copy.21
  40.6 17.4 %all-to-all-start = ((bf16[64,8,1728]{2,0,1:T(8,128)(2,1)}), bf16[64,8,1728]{2,0,1:T(8,128)(2,1)S(1)}, u32[]{:S(2)}, u32[]{:S(2)}) async-start(bf16[64,8,1728]{2,0,1:T(8,128)(2,1)} %copy.21), calls=%async_computation | async-start | bytes 3670016 | tf_op jit(solution)/shard_map/all_to_all | solution.py:131
  58.2 29.9 %all-to-all-done = bf16[64,8,1728]{2,0,1:T(8,128)(2,1)S(1)} async-done(((bf16[64,8,1728]{2,0,1:T(8,128)(2,1)}), bf16[64,8,1728]{2,0,1:T(8,128)(2,1)S(1)}, u32[]{:S(2)}, u32[]{:S(2)}) %all-to-all-start) | async-done | bytes 1769504 | tf_op jit(solution)/shard_map/all_to_all | solution.py:131
  88.1 4.1 copy.26
  92.1 5.8 %reshape.166 = bf16[512,3,24,24]{0,3,2,1:T(8,128)(2,1)} reshape(bf16[8,64,1728]{1,0,2:T(8,128)(2,1)} %copy.26) | data formatting | bytes 3538944 | tf_op jit(solution)/shard_map/reshape | solution.py:142
  98.0 3.2 multiply_add_fusion
  101.2 2.9 fusion.124
  104.1 1.8 fusion.93
  105.9 1.7 slice_bitcast_fusion.23
  107.7 1.1 copy.22
  108.8 2.5 collective-permute-start
  111.3 1.1 copy.23
  112.4 3.5 collective-permute-start.1
  115.9 1.6 copy.28
  117.5 1.6 copy.27
  119.1 0.9 copy.41
  120.0 0.9 copy.42
  121.0 27.4 %collective-permute-start.2 = (bf16[2,512,3,24]{1,3,2,0:T(8,128)(2,1)S(1)}, bf16[2,512,3,24]{1,3,2,0:T(8,128)(2,1)S(1)}, u32[]{:S(2)}, u32[]{:S(2)}) collective-permute-start(bf16[2,512,3,24]{1,3,2,0:T(8,128)(2,1)S(1)} %pad_maximum_fusion), channel_id=1, source_target_pairs={{0,760},{8,0},{16,8},{24,16},{32,24},{40,32},{48,40},{56,48},{64,5... | collective-permute-start | bytes 442376 | tf_op jit(solution)/shard_map/ppermute | solution.py:34
  148.4 1.6 copy.32
  150.0 0.7 copy.31
  150.7 0.9 copy.39
  151.6 1.9 collective-permute-start.3
  153.6 0.9 pad_maximum_fusion.2
  154.5 19.6 %collective-permute-start.4 = (bf16[2,512,3,24]{1,3,2,0:T(8,128)(2,1)S(1)}, bf16[2,512,3,24]{1,3,2,0:T(8,128)(2,1)S(1)}, u32[]{:S(2)}, u32[]{:S(2)}) collective-permute-start(bf16[2,512,3,24]{1,3,2,0:T(8,128)(2,1)S(1)} %pad_maximum_fusion.2), channel_id=1, source_target_pairs={{0,736},{8,744},{16,752},{24,760},{32,0},{40,8},{48,16},{56,24},{6... | collective-permute-start | bytes 442376 | tf_op jit(solution)/shard_map/ppermute | solution.py:34
  174.1 0.9 pad_maximum_fusion.3
  175.0 1.9 collective-permute-start.5
  177.1 0.7 convert_subtract_fusion.5
  177.8 0.7 bitcast_convert_fusion.3
  178.5 0.7 bitcast_convert_fusion.2
  179.2 13.4 %collective-permute-done.5 = bf16[2,512,3,24]{1,3,2,0:T(8,128)(2,1)S(1)} collective-permute-done((bf16[2,512,3,24]{1,3,2,0:T(8,128)(2,1)S(1)}, bf16[2,512,3,24]{1,3,2,0:T(8,128)(2,1)S(1)}, u32[]{:S(2)}, u32[]{:S(2)}) %collective-permute-start.5) | collective-permute-done | bytes 147488 | tf_op jit(solution)/shard_map/ppermute | solution.py:34
  193.3 0.7 convert_subtract_fusion.4
  195.0 1.4 copy.25
  196.3 4.5 concatenate.27
  200.9 2.3 convert_element_type.192
  203.2 6.2 %fusion.31 = bf16[5,512,512]{2,1,0:T(8,128)(2,1)} fusion(bf16[512,1728]{1,0:T(8,128)(2,1)S(1)} %bitcast.146, f32[512,2880]{1,0:T(8,128)S(1)} %convert_element_type.192, f32[1728]{0:T(1024)S(1)} %dynamic-slice_reduce_fusion, f32[1728]{0:T(1024)S(1)} %get-tuple-element.43, f32[1728]{0:T(1024)S(1)} %get-tuple-element.44, f32[1728]{0:T(1024)S(1)} %get-tuple-element.42, ...), kind=kOutput, calls=%fused_computation.47 | convolution fusion | flops 918880256 | bytes 28090368 | tf_op jit(solution)/shard_map/dot_general | solution.py:139
  209.5 1.9 fusion.41
  211.5 1.9 fusion.39
  213.4 1.9 fusion.37
  215.3 1.9 fusion.35
  217.3 1.9 collective-permute-start.9
  219.2 11.7 %collective-permute-start.8 = (bf16[512,128]{1,0:T(8,128)(2,1)S(1)}, bf16[512,128]{1,0:T(8,128)(2,1)S(1)}, u32[]{:S(2)}, u32[]{:S(2)}) collective-permute-start(bf16[512,128]{1,0:T(8,128)(2,1)S(1)} %bitcast.148), channel_id=1, source_target_pairs={{0,736},{8,744},{16,752},{24,760},{32,0},{40,8},{48,16},{56,24},{6... | collective-permute-start | bytes 393224 | tf_op jit(solution)/shard_map/ppermute | solution.py:34
  231.0 1.9 collective-permute-start.6
  232.9 2.4 collective-permute-start.7
  235.3 204.6 %all-reduce.4.cloned.1.call-done = bf16[5,512,512]{2,1,0:T(8,128)(2,1)} async-done(((bf16[5,512,512]{2,1,0:T(8,128)(2,1)}), bf16[5,512,512]{2,1,0:T(8,128)(2,1)}) %all-reduce.4.cloned.1.call-update) | async-done | bytes 2621456 | tf_op jit(solution)/shard_map/psum | solution.py:171
  439.9 1.5 fusion.60
  441.4 1.3 convolution_add_fusion.5
  442.7 1.3 fusion.66
  444.1 1.3 fusion.63
  445.7 4.3 collective-permute-start.13
  450.1 9.3 %collective-permute-start.12 = (bf16[512,128]{1,0:T(8,128)(2,1)S(1)}, bf16[512,128]{1,0:T(8,128)(2,1)S(1)}, u32[]{:S(2)}, u32[]{:S(2)}) collective-permute-start(bf16[512,128]{1,0:T(8,128)(2,1)S(1)} %fusion.57), channel_id=1, source_target_pairs={{0,736},{8,744},{16,752},{24,760},{32,0},{40,8},{48,16},{56,24},{6... | collective-permute-start | bytes 393224 | tf_op jit(solution)/shard_map/ppermute | solution.py:34
  459.4 1.9 collective-permute-start.10
  461.3 2.4 collective-permute-start.11
  465.0 9.6 %collective-permute-done.11 = bf16[512,128]{1,0:T(8,128)(2,1)S(1)} collective-permute-done((bf16[512,128]{1,0:T(8,128)(2,1)S(1)}, bf16[512,128]{1,0:T(8,128)(2,1)S(1)}, u32[]{:S(2)}, u32[]{:S(2)}) %collective-permute-start.11) | collective-permute-done | bytes 131104 | tf_op jit(solution)/shard_map/ppermute | solution.py:34
  474.8 1.9 collective-permute-start.17
  476.8 11.7 %collective-permute-start.16 = (bf16[512,128]{1,0:T(8,128)(2,1)S(1)}, bf16[512,128]{1,0:T(8,128)(2,1)S(1)}, u32[]{:S(2)}, u32[]{:S(2)}) collective-permute-start(bf16[512,128]{1,0:T(8,128)(2,1)S(1)} %fusion.56), channel_id=1, source_target_pairs={{0,736},{8,744},{16,752},{24,760},{32,0},{40,8},{48,16},{56,24},{6... | collective-permute-start | bytes 393224 | tf_op jit(solution)/shard_map/ppermute | solution.py:34
  488.5 1.9 collective-permute-start.14
  490.4 2.4 collective-permute-start.15
  494.1 9.6 %collective-permute-done.15 = bf16[512,128]{1,0:T(8,128)(2,1)S(1)} collective-permute-done((bf16[512,128]{1,0:T(8,128)(2,1)S(1)}, bf16[512,128]{1,0:T(8,128)(2,1)S(1)}, u32[]{:S(2)}, u32[]{:S(2)}) %collective-permute-start.15) | collective-permute-done | bytes 131104 | tf_op jit(solution)/shard_map/ppermute | solution.py:34
  504.0 0.7 fusion.95
  (87 shorter events, 5.7 us)
Async XLA Ops:
  6.5 3.8 copy-start.1
  6.5 3.7 copy-start.17
  40.6 47.4 %all-to-all-start = ((bf16[64,8,1728]{2,0,1:T(8,128)(2,1)}), bf16[64,8,1728]{2,0,1:T(8,128)(2,1)S(1)}, u32[]{:S(2)}, u32[]{:S(2)}) async-start(bf16[64,8,1728]{2,0,1:T(8,128)(2,1)} %copy.21), calls=%async_computation | async-start | bytes 3670016 | tf_op jit(solution)/shard_map/all_to_all | solution.py:131
  58.1 381.8 %all-reduce.4.cloned.1.call-start = ((), (), s32[]{:S(2)}) async-start(), calls=%async_computation.1 | async-start | bytes 5242880 | tf_op jit(solution)/shard_map/psum | solution.py:171
  108.8 85.9 %collective-permute-start = (bf16[512,576]{0,1:T(8,128)(2,1)}, bf16[512,576]{0,1:T(8,128)(2,1)S(1)}, u32[]{:S(2)}, u32[]{:S(2)}) collective-permute-start(bf16[512,576]{0,1:T(8,128)(2,1)} %copy.22), channel_id=1, source_target_pairs={{0,1},{1,2},{2,3},{3,4},{4,5},{5,6},{6,7},{8,9},{9,10},{10,11},{11... | collective-permute-start | bytes 1769480 | tf_op jit(solution)/shard_map/ppermute | solution.py:26
  112.4 82.5 %collective-permute-start.1 = (bf16[512,576]{0,1:T(8,128)(2,1)}, bf16[512,576]{0,1:T(8,128)(2,1)}, u32[]{:S(2)}, u32[]{:S(2)}) collective-permute-start(bf16[512,576]{0,1:T(8,128)(2,1)} %copy.23), channel_id=1, source_target_pairs={{1,0},{2,1},{3,2},{4,3},{5,4},{6,5},{7,6},{9,8},{10,9},{11,10},{12... | collective-permute-start | bytes 1769480 | tf_op jit(solution)/shard_map/ppermute | solution.py:27
  121.0 54.1 %collective-permute-start.2 = (bf16[2,512,3,24]{1,3,2,0:T(8,128)(2,1)S(1)}, bf16[2,512,3,24]{1,3,2,0:T(8,128)(2,1)S(1)}, u32[]{:S(2)}, u32[]{:S(2)}) collective-permute-start(bf16[2,512,3,24]{1,3,2,0:T(8,128)(2,1)S(1)} %pad_maximum_fusion), channel_id=1, source_target_pairs={{0,760},{8,0},{16,8},{24,16},{32,24},{40,32},{48,40},{56,48},{64,5... | collective-permute-start | bytes 442376 | tf_op jit(solution)/shard_map/ppermute | solution.py:34
  151.6 25.4 %collective-permute-start.3 = (bf16[2,512,3,24]{1,3,2,0:T(8,128)(2,1)S(1)}, bf16[2,512,3,24]{1,3,2,0:T(8,128)(2,1)S(1)}, u32[]{:S(2)}, u32[]{:S(2)}) collective-permute-start(bf16[2,512,3,24]{1,3,2,0:T(8,128)(2,1)S(1)} %pad_maximum_fusion.1), channel_id=1, source_target_pairs={{0,8},{8,16},{16,24},{24,32},{32,40},{40,48},{48,56},{56,64},{64,7... | collective-permute-start | bytes 442376 | tf_op jit(solution)/shard_map/ppermute | solution.py:34
  154.5 24.0 %collective-permute-start.4 = (bf16[2,512,3,24]{1,3,2,0:T(8,128)(2,1)S(1)}, bf16[2,512,3,24]{1,3,2,0:T(8,128)(2,1)S(1)}, u32[]{:S(2)}, u32[]{:S(2)}) collective-permute-start(bf16[2,512,3,24]{1,3,2,0:T(8,128)(2,1)S(1)} %pad_maximum_fusion.2), channel_id=1, source_target_pairs={{0,736},{8,744},{16,752},{24,760},{32,0},{40,8},{48,16},{56,24},{6... | collective-permute-start | bytes 442376 | tf_op jit(solution)/shard_map/ppermute | solution.py:34
  175.0 17.6 %collective-permute-start.5 = (bf16[2,512,3,24]{1,3,2,0:T(8,128)(2,1)S(1)}, bf16[2,512,3,24]{1,3,2,0:T(8,128)(2,1)S(1)}, u32[]{:S(2)}, u32[]{:S(2)}) collective-permute-start(bf16[2,512,3,24]{1,3,2,0:T(8,128)(2,1)S(1)} %pad_maximum_fusion.3), channel_id=1, source_target_pairs={{0,32},{8,40},{16,48},{24,56},{32,64},{40,72},{48,80},{56,88},{64,... | collective-permute-start | bytes 442376 | tf_op jit(solution)/shard_map/ppermute | solution.py:34
  203.1 6.4 %copy-start.7 = (f32[512,3,24,1]{0,2,3,1:T(8,128)S(1)}, f32[512,3,24,1]{0,2,3,1:T(8,128)}, u32[]{:S(2)}) copy-start(f32[512,3,24,1]{0,2,3,1:T(8,128)} %copy.28) | copy-start | bytes 442372
  203.2 6.4 %copy-start.8 = (f32[512,3,24,1]{0,2,3,1:T(8,128)S(1)}, f32[512,3,24,1]{0,2,3,1:T(8,128)}, u32[]{:S(2)}) copy-start(f32[512,3,24,1]{0,2,3,1:T(8,128)} %copy.27) | copy-start | bytes 442372
  203.2 8.3 %copy-start.9 = (f32[512,3,24,1]{0,2,3,1:T(8,128)S(1)}, f32[512,3,24,1]{0,2,3,1:T(8,128)}, u32[]{:S(2)}) copy-start(f32[512,3,24,1]{0,2,3,1:T(8,128)} %copy.32) | copy-start | bytes 442372
  203.2 8.3 %copy-start.10 = (f32[512,3,24,1]{0,2,3,1:T(8,128)S(1)}, f32[512,3,24,1]{0,2,3,1:T(8,128)}, u32[]{:S(2)}) copy-start(f32[512,3,24,1]{0,2,3,1:T(8,128)} %copy.31) | copy-start | bytes 442372
  203.2 8.3 %copy-start.11 = (f32[512,72]{0,1:T(8,128)S(1)}, f32[512,72]{0,1:T(8,128)}, u32[]{:S(2)}) copy-start(f32[512,72]{0,1:T(8,128)} %convert_subtract_fusion.5) | copy-start | bytes 442372
  203.2 8.3 %copy-start.12 = (f32[512,72]{0,1:T(8,128)S(1)}, f32[512,72]{0,1:T(8,128)}, u32[]{:S(2)}) copy-start(f32[512,72]{0,1:T(8,128)} %bitcast_convert_fusion.3) | copy-start | bytes 442372
  203.2 10.2 %copy-start.5 = (f32[512,3,1,24]{0,3,2,1:T(8,128)S(1)}, f32[512,3,1,24]{0,3,2,1:T(8,128)}, u32[]{:S(2)}) copy-start(f32[512,3,1,24]{0,3,2,1:T(8,128)} %get-tuple-element.16) | copy-start | bytes 442372
  203.2 10.2 %copy-start.6 = (f32[512,3,1,24]{0,3,2,1:T(8,128)S(1)}, f32[512,3,1,24]{0,3,2,1:T(8,128)}, u32[]{:S(2)}) copy-start(f32[512,3,1,24]{0,3,2,1:T(8,128)} %get-tuple-element.18) | copy-start | bytes 442372
  203.2 10.2 %copy-start.13 = (f32[512,72]{0,1:T(8,128)S(1)}, f32[512,72]{0,1:T(8,128)}, u32[]{:S(2)}) copy-start(f32[512,72]{0,1:T(8,128)} %bitcast_convert_fusion.2) | copy-start | bytes 442372
  203.2 10.2 %copy-start.16 = (f32[512,72]{0,1:T(8,128)S(1)}, f32[512,72]{0,1:T(8,128)}, u32[]{:S(2)}) copy-start(f32[512,72]{0,1:T(8,128)} %convert_subtract_fusion.4) | copy-start | bytes 442372
  209.5 5.8 %copy-start.3 = (f32[512,3,1,24]{0,3,2,1:T(8,128)S(1)}, f32[512,3,1,24]{0,3,2,1:T(8,128)}, u32[]{:S(2)}) copy-start(f32[512,3,1,24]{0,3,2,1:T(8,128)} %get-tuple-element.15) | copy-start | bytes 442372
  209.5 5.8 %copy-start.4 = (f32[512,3,1,24]{0,3,2,1:T(8,128)S(1)}, f32[512,3,1,24]{0,3,2,1:T(8,128)}, u32[]{:S(2)}) copy-start(f32[512,3,1,24]{0,3,2,1:T(8,128)} %get-tuple-element.17) | copy-start | bytes 442372
  209.5 5.8 %copy-start.14 = (f32[512,72]{0,1:T(8,128)S(1)}, f32[512,72]{0,1:T(8,128)}, u32[]{:S(2)}) copy-start(f32[512,72]{0,1:T(8,128)} %bitcast_convert_fusion.1) | copy-start | bytes 442372
  209.5 5.8 %copy-start.15 = (f32[512,72]{0,1:T(8,128)S(1)}, f32[512,72]{0,1:T(8,128)}, u32[]{:S(2)}) copy-start(f32[512,72]{0,1:T(8,128)} %convert_subtract_fusion.3) | copy-start | bytes 442372
  211.5 5.8 %copy-start.2 = (bf16[1,512,128]{2,1,0:T(8,128)(2,1)S(1)}, bf16[1,512,128]{2,1,0:T(8,128)(2,1)}, u32[]{:S(2)}) copy-start(bf16[1,512,128]{2,1,0:T(8,128)(2,1)} %param.7) | copy-start | bytes 393220
  217.3 225.4 %collective-permute-start.9 = (bf16[512,128]{1,0:T(8,128)(2,1)S(1)}, bf16[512,128]{1,0:T(8,128)(2,1)S(1)}, u32[]{:S(2)}, u32[]{:S(2)}) collective-permute-start(bf16[512,128]{1,0:T(8,128)(2,1)S(1)} %bitcast.147), channel_id=1, source_target_pairs={{0,32},{8,40},{16,48},{24,56},{32,64},{40,72},{48,80},{56,88},{64,... | collective-permute-start | bytes 393224 | tf_op jit(solution)/shard_map/ppermute | solution.py:34
  219.2 224.8 %collective-permute-start.8 = (bf16[512,128]{1,0:T(8,128)(2,1)S(1)}, bf16[512,128]{1,0:T(8,128)(2,1)S(1)}, u32[]{:S(2)}, u32[]{:S(2)}) collective-permute-start(bf16[512,128]{1,0:T(8,128)(2,1)S(1)} %bitcast.148), channel_id=1, source_target_pairs={{0,736},{8,744},{16,752},{24,760},{32,0},{40,8},{48,16},{56,24},{6... | collective-permute-start | bytes 393224 | tf_op jit(solution)/shard_map/ppermute | solution.py:34
  231.0 210.4 %collective-permute-start.6 = (bf16[512,128]{1,0:T(8,128)(2,1)S(1)}, bf16[512,128]{1,0:T(8,128)(2,1)S(1)}, u32[]{:S(2)}, u32[]{:S(2)}) collective-permute-start(bf16[512,128]{1,0:T(8,128)(2,1)S(1)} %bitcast.149), channel_id=1, source_target_pairs={{0,760},{8,0},{16,8},{24,16},{32,24},{40,32},{48,40},{56,48},{64,5... | collective-permute-start | bytes 393224 | tf_op jit(solution)/shard_map/ppermute | solution.py:34
  232.9 212.5 %collective-permute-start.7 = (bf16[512,128]{1,0:T(8,128)(2,1)S(1)}, bf16[512,128]{1,0:T(8,128)(2,1)S(1)}, u32[]{:S(2)}, u32[]{:S(2)}) collective-permute-start(bf16[512,128]{1,0:T(8,128)(2,1)S(1)} %bitcast.150), channel_id=1, source_target_pairs={{0,8},{8,16},{16,24},{24,32},{32,40},{40,48},{48,56},{56,64},{64,7... | collective-permute-start | bytes 393224 | tf_op jit(solution)/shard_map/ppermute | solution.py:34
  439.9 5.5 %copy-start = (bf16[5,512,512]{2,1,0:T(8,128)(2,1)S(1)}, bf16[5,512,512]{2,1,0:T(8,128)(2,1)}, u32[]{:S(2)}) copy-start(bf16[5,512,512]{2,1,0:T(8,128)(2,1)} %all-reduce.4.cloned.1.call-done) | copy-start | bytes 7864324
  445.7 18.6 %collective-permute-start.13 = (bf16[512,128]{1,0:T(8,128)(2,1)S(1)}, bf16[512,128]{1,0:T(8,128)(2,1)S(1)}, u32[]{:S(2)}, u32[]{:S(2)}) collective-permute-start(bf16[512,128]{1,0:T(8,128)(2,1)S(1)} %fusion.57), channel_id=1, source_target_pairs={{0,32},{8,40},{16,48},{24,56},{32,64},{40,72},{48,80},{56,88},{64,... | collective-permute-start | bytes 393224 | tf_op jit(solution)/shard_map/ppermute | solution.py:34
  450.1 14.6 %collective-permute-start.12 = (bf16[512,128]{1,0:T(8,128)(2,1)S(1)}, bf16[512,128]{1,0:T(8,128)(2,1)S(1)}, u32[]{:S(2)}, u32[]{:S(2)}) collective-permute-start(bf16[512,128]{1,0:T(8,128)(2,1)S(1)} %fusion.57), channel_id=1, source_target_pairs={{0,736},{8,744},{16,752},{24,760},{32,0},{40,8},{48,16},{56,24},{6... | collective-permute-start | bytes 393224 | tf_op jit(solution)/shard_map/ppermute | solution.py:34
  459.4 4.6 collective-permute-start.10
  461.3 13.2 %collective-permute-start.11 = (bf16[512,128]{1,0:T(8,128)(2,1)S(1)}, bf16[512,128]{1,0:T(8,128)(2,1)S(1)}, u32[]{:S(2)}, u32[]{:S(2)}) collective-permute-start(bf16[512,128]{1,0:T(8,128)(2,1)S(1)} %fusion.57), channel_id=1, source_target_pairs={{0,8},{8,16},{16,24},{24,32},{32,40},{40,48},{48,56},{56,64},{64,7... | collective-permute-start | bytes 393224 | tf_op jit(solution)/shard_map/ppermute | solution.py:34
  474.8 18.6 %collective-permute-start.17 = (bf16[512,128]{1,0:T(8,128)(2,1)S(1)}, bf16[512,128]{1,0:T(8,128)(2,1)S(1)}, u32[]{:S(2)}, u32[]{:S(2)}) collective-permute-start(bf16[512,128]{1,0:T(8,128)(2,1)S(1)} %fusion.56), channel_id=1, source_target_pairs={{0,32},{8,40},{16,48},{24,56},{32,64},{40,72},{48,80},{56,88},{64,... | collective-permute-start | bytes 393224 | tf_op jit(solution)/shard_map/ppermute | solution.py:34
  476.8 17.0 %collective-permute-start.16 = (bf16[512,128]{1,0:T(8,128)(2,1)S(1)}, bf16[512,128]{1,0:T(8,128)(2,1)S(1)}, u32[]{:S(2)}, u32[]{:S(2)}) collective-permute-start(bf16[512,128]{1,0:T(8,128)(2,1)S(1)} %fusion.56), channel_id=1, source_target_pairs={{0,736},{8,744},{16,752},{24,760},{32,0},{40,8},{48,16},{56,24},{6... | collective-permute-start | bytes 393224 | tf_op jit(solution)/shard_map/ppermute | solution.py:34
  488.5 4.6 collective-permute-start.14
  490.4 13.2 %collective-permute-start.15 = (bf16[512,128]{1,0:T(8,128)(2,1)S(1)}, bf16[512,128]{1,0:T(8,128)(2,1)S(1)}, u32[]{:S(2)}, u32[]{:S(2)}) collective-permute-start(bf16[512,128]{1,0:T(8,128)(2,1)S(1)} %fusion.56), channel_id=1, source_target_pairs={{0,8},{8,16},{16,24},{24,32},{32,40},{40,48},{48,56},{56,64},{64,7... | collective-permute-start | bytes 393224 | tf_op jit(solution)/shard_map/ppermute | solution.py:34
Sparse Core Ops, SparseCore 0:
  217.4 222.4 all-reduce.3
where the time goes:
time: 513 us; the launch traced here: 512 us
  waiting for transfers between devices  267 us (52%)
  starting transfers between devices  128 us (25%)
  other arithmetic  42.6 us (8%)
  local copies, waits for them, and re-layouts  36.2 us (7%)
  matrix products  22.7 us (4%)
  between operations  14.7 us (3%)
    psum x1, waiting for transfers between devices, on_device(): summed = lax.psum(rounded.astype(jnp.bfloat16), 'band')  205 us
    ppermute x16, starting transfers between devices, from_behind(): lax.ppermute(value, axis, [(i, (i + by) % devices) for i in range(devices)])  105 us
    ppermute x16, waiting for transfers between devices, from_behind(): lax.ppermute(value, axis, [(i, (i + by) % devices) for i in range(devices)])  32.6 us
    all_to_all x1, waiting for transfers between devices, on_device(): lax.all_to_all(basis, 'band', split_axis=1, concat_axis=0, tiled=True)  29.9 us
    all_to_all x1, starting transfers between devices, on_device(): lax.all_to_all(basis, 'band', split_axis=1, concat_axis=0, tiled=True)  17.4 us
    div x1, other arithmetic, filtered_basis(): (flat_hamiltonian(previous, potential, masks) - middle * previous) / spread  14.1 us
  transfers between devices with their start and end apart: 20, of which 5 were waited for; matrix products, arithmetic and copies ran while one was open for 5% of the time, Pallas kernels for 0%

commit v1 on v0

v1 whole, which is shorter than its diff:
```python
import jax
import jax.numpy as jnp
import numpy as np
from jax import lax
from jax.sharding import Mesh, PartitionSpec as P

P_SIZE = 24
PLANE = P_SIZE * P_SIZE
G = 13824
EB = 4
HALVES = 2
SLABS = 4
CHUNKS = 4

LOW_EDGE = 4.0
HIGH_EDGE = 14.0
SHIFT_CENTER = 4.0
HALF_WIDTH = 6.0
MIDDLE = 0.5 * (HIGH_EDGE + LOW_EDGE)
SPREAD = 0.5 * (HIGH_EDGE - LOW_EDGE)


def from_behind(value, axis, by):
    devices = lax.axis_size(axis)
    return lax.ppermute(value, axis, [(i, (i + by) % devices) for i in range(devices)])


def swap_halves(value):
    return lax.ppermute(value, "half", [(0, 1), (1, 0)])


def side_masks(length):
    where = jnp.arange(length, dtype=jnp.int32)
    zpos = where % P_SIZE
    ypos = where // P_SIZE % P_SIZE
    return (
        (zpos < P_SIZE - 1).astype(jnp.float32),
        (zpos > 0).astype(jnp.float32),
        (ypos < P_SIZE - 1).astype(jnp.float32),
        (ypos > 0).astype(jnp.float32),
    )


def flat_hamiltonian(padded, length, potential, masks):
    values = padded[:, PLANE : PLANE + length]
    beside = padded[:, 2 * PLANE : 2 * PLANE + length] + padded[:, 0:length]
    beside = beside + masks[0] * padded[:, PLANE + 1 : PLANE + 1 + length]
    beside = beside + masks[1] * padded[:, PLANE - 1 : PLANE - 1 + length]
    beside = beside + masks[2] * padded[:, PLANE + P_SIZE : PLANE + P_SIZE + length]
    beside = beside + masks[3] * padded[:, PLANE - P_SIZE : PLANE - P_SIZE + length]
    return 6.0 * values - beside + potential * values


def whole_hamiltonian(values, potential, masks):
    padded = jnp.pad(values, ((0, 0), (PLANE, PLANE)))
    return flat_hamiltonian(padded, values.shape[1], potential, masks)


def filtered_basis(orbitals, potential, kept_count, start_index):
    orbital_count = orbitals.shape[0]
    masks = side_masks(G)
    previous = orbitals.astype(jnp.float32)
    current = (whole_hamiltonian(previous, potential, masks) - MIDDLE * previous) / SPREAD
    current = (
        2.0 * (whole_hamiltonian(current, potential, masks) - MIDDLE * current) / SPREAD - previous
    )
    magnitude = jnp.sqrt(jnp.mean(current * current, axis=1, keepdims=True) + 1e-06)
    active = start_index + jnp.arange(orbital_count, dtype=jnp.int32) < kept_count
    return jnp.where(active[:, None], current / magnitude, 0.0).astype(jnp.bfloat16)


def face_selector(planes):
    grid = np.arange(planes * PLANE, dtype=np.int32).reshape(planes, P_SIZE, P_SIZE)
    last = P_SIZE - 1
    groups = [
        grid[:, :, 0], grid[:, :, 1], grid[:, 0, :], grid[:, 1, :],
        grid[:, :, last - 1], grid[:, :, last], grid[:, last - 1, :], grid[:, last, :],
    ]
    chosen = jnp.asarray(np.concatenate([g.reshape(-1) for g in groups]))
    points = jnp.arange(planes * PLANE, dtype=jnp.int32)
    return (chosen[:, None] == points[None, :]).astype(jnp.bfloat16)


def slab_rows(orbitals, potential, kept_count, half, band):
    per_device = orbitals.shape[0]
    step = per_device // CHUNKS
    half_points = G // HALVES
    slab_points = half_points // SLABS
    taken = half_points + PLANE
    arrived = []
    for chunk in range(CHUNKS):
        basis = filtered_basis(
            orbitals[chunk * step : (chunk + 1) * step],
            potential,
            kept_count,
            band * per_device + chunk * step,
        )
        padded = jnp.pad(basis, ((0, 0), (0, PLANE)))
        lower, upper = padded[:, :taken], padded[:, half_points:]
        kept = jnp.where(half == 0, lower, upper)
        other = swap_halves(jnp.where(half == 0, upper, lower))
        ordered = jnp.stack(
            [jnp.where(half == 0, kept, other), jnp.where(half == 0, other, kept)]
        )
        pieces = jnp.stack(
            [
                ordered[:, :, s * slab_points : (s + 1) * slab_points + PLANE]
                for s in range(SLABS)
            ]
        )
        arrived.append(lax.all_to_all(pieces, "slab", 0, 0, tiled=True))
    rows = jnp.stack(arrived, axis=2)
    return jnp.swapaxes(rows, 0, 1).reshape(-1, slab_points + PLANE)


def transposed_dot(a, b, contract_a, contract_b):
    return lax.dot_general(
        a, b, (((contract_a,), (contract_b,)), ((), ())), preferred_element_type=jnp.float32
    )


def apply_blocks(h_self, h_z, h_y, current):
    ahead_z = from_behind(current, "elem", -1)
    ahead_y = from_behind(current, "elem", -EB)
    back_z = transposed_dot(h_z, current, 0, 0).astype(jnp.bfloat16)
    back_y = transposed_dot(h_y, current, 0, 0).astype(jnp.bfloat16)
    behind_z = from_behind(back_z, "elem", 1)
    behind_y = from_behind(back_y, "elem", EB)
    running = transposed_dot(h_self, current, 1, 0)
    running = running + transposed_dot(h_z, ahead_z, 1, 0)
    running = running + transposed_dot(h_y, ahead_y, 1, 0)
    return running + behind_z.astype(jnp.float32) + behind_y.astype(jnp.float32)


def scaled(blocks, current):
    return (apply_blocks(*blocks, current) - SHIFT_CENTER * current.astype(jnp.float32)) / HALF_WIDTH


def on_device(orbitals, potential, basis_count, states):
    half = lax.axis_index("half")
    slab = lax.axis_index("slab")
    band = half * SLABS + slab
    extended = slab_rows(orbitals[0], potential[0], basis_count[0], half, band)
    total = extended.shape[0]
    length = extended.shape[1] - PLANE
    planes = length // PLANE
    own = extended[:, :length]

    faces = transposed_dot(face_selector(planes), own, 1, 1).astype(jnp.bfloat16)
    width = 2 * planes * P_SIZE
    other_z = from_behind(faces[:width], "elem", -1)
    other_y = from_behind(faces[width : 2 * width], "elem", -EB)

    slab_potential = lax.dynamic_slice_in_dim(potential[0], band * length, length, 0)
    padded = jnp.pad(extended.astype(jnp.float32), ((0, 0), (PLANE, 0)))
    applied = flat_hamiltonian(padded, length, slab_potential, side_masks(length))
    applied = jnp.concatenate(
        [applied.astype(jnp.bfloat16), -own[:, length - PLANE :]], axis=1
    )
    h_self = transposed_dot(extended, applied, 1, 1) * (1.0 / G)
    weight = -0.5 / PLANE
    h_z = transposed_dot(faces[2 * width : 3 * width], other_z, 0, 0) * weight
    h_y = transposed_dot(faces[3 * width :], other_y, 0, 0) * weight

    partial = jnp.stack([h_self, h_z, h_y], axis=0).astype(jnp.bfloat16)
    partial = partial.reshape(3, SLABS, total // SLABS, total).swapaxes(0, 1)
    pieces = lax.all_to_all(partial, "slab", 0, 0, tiled=True)
    summed = jnp.sum(pieces.astype(jnp.float32), axis=0).astype(jnp.bfloat16)
    swapped = swap_halves(summed)
    summed = (summed.astype(jnp.float32) + swapped.astype(jnp.float32)).astype(jnp.bfloat16)
    blocks = lax.all_gather(summed, "slab", axis=1, tiled=True)
    blocks = (blocks[0], blocks[1], blocks[2])

    start = states[0]
    first = scaled(blocks, start).astype(jnp.bfloat16)
    second = (2.0 * scaled(blocks, first) - start.astype(jnp.float32)).astype(jnp.bfloat16)
    third = 2.0 * scaled(blocks, second) - first.astype(jnp.float32)
    magnitude = jnp.sqrt(jnp.mean(third * third, axis=0, keepdims=True) + 1e-06)
    return (third / magnitude).astype(jnp.bfloat16)[None]


def solution(mesh):
    elems, bands = mesh.devices.shape
    inner = Mesh(mesh.devices.reshape(elems, HALVES, bands // HALVES), ("elem", "half", "slab"))
    both = ("half", "slab")
    placed = (P("elem", both, None), P("elem", None), P("elem"), P("elem", None, both))
    return jax.shard_map(
        on_device, mesh=inner, in_specs=placed, out_specs=P("elem", None, both), check_vma=False
    )
```

time: 513 us -> 344 us (0.67)
  waiting for transfers between devices: 267 us -> 131 us
  local copies, waits for them, and re-layouts: 36.2 us -> 1.13 us
  blocking collectives: 0 us -> 23.8 us
  starting transfers between devices: 128 us -> 114 us
  matrix products: 22.7 us -> 11.4 us
    psum x1 -> x0, waiting for transfers between devices: 205 us -> none  [on_device(): summed = lax.psum(rounded.astype(jnp.bfloat16), 'band')]
    ppermute x16 -> x14, starting transfers between devices: 105 us -> 51.2 us  [from_behind(): lax.ppermute(value, axis, [(i, (i + by) % devices) for i in range(devices)])]
    ppermute x2 -> x5, waiting for transfers between devices: 0.01 us -> 41.4 us  [swap_halves(): return lax.ppermute(value, 'half', [(0, 1), (1, 0)])]
    all_gather x0 -> x1, waiting for transfers between devices: none -> 36.4 us  [on_device(): blocks = lax.all_gather(summed, 'slab', axis=1, tiled=True)]
    ppermute x2 -> x5, starting transfers between devices: 6 us -> 39 us  [swap_halves(): return lax.ppermute(value, 'half', [(0, 1), (1, 0)])]
    all_to_all x0 -> x1, blocking collectives: none -> 23.8 us  [on_device(): pieces = lax.all_to_all(partial, 'slab', 0, 0, tiled=True)]
    all_to_all x1 -> x4, waiting for transfers between devices: 29.9 us -> 16.3 us  [slab_rows(): arrived.append(lax.all_to_all(pieces, 'slab', 0, 0, tiled=True))]
    dot_general x20 -> x19, matrix products: 22.7 us -> 11.4 us  [transposed_dot(): lax.dot_general(a, b, (((contract_a,), (contract_b,)), ((), ())), preferr...]
  transfers between devices with their start and end apart: 20 -> 24, of which waited for: 5 -> 14; matrix products, arithmetic and copies ran while one was open for 5% -> 7% of each run, Pallas kernels for 0% -> 0%
where the time goes in v1:
time: 344 us; the launch traced here: 339 us
  waiting for transfers between devices  131 us (38%)
  starting transfers between devices  114 us (33%)
  other arithmetic  43.2 us (13%)
  blocking collectives  23.8 us (7%)
  between operations  14.8 us (4%)
  matrix products  11.4 us (3%)
    ppermute x14, starting transfers between devices, from_behind(): lax.ppermute(value, axis, [(i, (i + by) % devices) for i in range(devices)])  51.2 us
    ppermute x5, waiting for transfers between devices, swap_halves(): return lax.ppermute(value, 'half', [(0, 1), (1, 0)])  41.4 us
    ppermute x5, starting transfers between devices, swap_halves(): return lax.ppermute(value, 'half', [(0, 1), (1, 0)])  39 us
    ppermute x14, waiting for transfers between devices, from_behind(): lax.ppermute(value, axis, [(i, (i + by) % devices) for i in range(devices)])  36.9 us
    all_gather x1, waiting for transfers between devices, on_device(): blocks = lax.all_gather(summed, 'slab', axis=1, tiled=True)  36.4 us
    all_to_all x1, blocking collectives, on_device(): pieces = lax.all_to_all(partial, 'slab', 0, 0, tiled=True)  23.8 us
    all_to_all x4, starting transfers between devices, slab_rows(): arrived.append(lax.all_to_all(pieces, 'slab', 0, 0, tiled=True))  23.8 us
    all_to_all x4, waiting for transfers between devices, slab_rows(): arrived.append(lax.all_to_all(pieces, 'slab', 0, 0, tiled=True))  16.3 us
  transfers between devices with their start and end apart: 24, of which 14 were waited for; matrix products, arithmetic and copies ran while one was open for 7% of the time, Pallas kernels for 0%

profile of v1, /device:TPU:6, one launch (start us, length us, event | category | flops | bytes accessed | tf_op | source)
XLA Modules:
  0.0 339.5 jit_solution(11061878583048122836)
XLA Ops:
  7.2 0.7 compare_convert_fusion
  7.9 3.0 bitcast_convert_fusion.3
  10.9 1.6 reduce.1
  12.5 0.8 broadcast_multiply_fusion.4
  13.4 9.0 %broadcast_multiply_fusion.3 = (f32[16,13824]{1,0:T(8,128)S(1)}, f32[16,13824]{1,0:T(8,128)S(1)}, f32[16,13824]{1,0:T(8,128)S(1)}, f32[16,13824]{1,0:T(8,128)S(1...) fusion(f32[13824]{0:T(1024)} %reduce.1, ...), kind=kLoop, calls=%fused_computation.192 | loop fusion | flops 15040512 | bytes 12662784 | tf_op jit(solution)/shard_map/div | solution.py:63
  22.4 6.8 %multiply_reduce_fusion.3 = (f32[16]{0:T(128)S(1)}, f32[16,13824]{1,0:T(8,128)}, f32[16]{0:T(128)S(1)}, f32[16,13824]{1,0:T(8,128)}, f32[16]{0:T(128)S(1)}, /*in...) fusion(bf16[1,64,13824]{2,1,0:T(8,128)(2,1)S(1)} %copy-done, f32[16,13824]{1,0:T(8,128)S(1)} %get-tuple-element.8, ...), kind=kLoop, calls=%fused_computation.131 | loop fusion | flops 17694656 | bytes 12663040 | tf_op jit(solution)/shard_map/reduce_sum | solution.py:67
  30.0 1.3 select_convert_fusion.3
  31.3 0.8 broadcast_select_fusion.6
  32.1 15.1 %collective-permute-start = (bf16[16,7488]{1,0:T(8,128)(2,1)}, bf16[16,7488]{1,0:T(8,128)(2,1)}, u32[]{:S(2)}, u32[]{:S(2)}) collective-permute-start(bf16[16,7488]{1,0:T(8,128)(2,1)} %broadcast_select_fusion.6), channel_id=1, source_target_pairs={{0,4},{4,0},{1,5},{5,1},{2,6},{6,2},{3,7},{7,3},{8,12},{12,8},{9,1... | collective-permute-start | bytes 718856 | tf_op jit(solution)/shard_map/ppermute | solution.py:29
  47.4 0.8 broadcast_select_fusion.4
  48.2 1.9 collective-permute-start.1
  50.3 0.8 broadcast_select_fusion.2
  51.0 10.2 %collective-permute-start.2 = (bf16[16,7488]{1,0:T(8,128)(2,1)}, bf16[16,7488]{1,0:T(8,128)(2,1)}, u32[]{:S(2)}, u32[]{:S(2)}) collective-permute-start(bf16[16,7488]{1,0:T(8,128)(2,1)} %broadcast_select_fusion.2), channel_id=1, source_target_pairs={{0,4},{4,0},{1,5},{5,1},{2,6},{6,2},{3,7},{7,3},{8,12},{12,8},{9,1... | collective-permute-start | bytes 718856 | tf_op jit(solution)/shard_map/ppermute | solution.py:29
  61.5 1.9 collective-permute-start.3
  63.4 1.1 select_bitcast_fusion.7
  64.7 0.9 pad_maximum_fusion.1
  65.5 8.0 %all-to-all-start = ((bf16[4,2,16,2304]{3,2,1,0:T(8,128)(2,1)}), bf16[4,2,16,2304]{3,2,1,0:T(8,128)(2,1)S(1)}, u32[]{:S(2)}, u32[]{:S(2)}) async-start(bf16[4,2,16,2304]{3,2,1,0:T(8,128)(2,1)} %pad_maximum_fusion.1), calls=%async_computation | async-start | bytes 1179648 | tf_op jit(solution)/shard_map/all_to_all | solution.py:111
  73.5 2.7 collective-permute-done.1
  76.4 15.8 %collective-permute-done.2 = bf16[16,7488]{1,0:T(8,128)(2,1)} collective-permute-done((bf16[16,7488]{1,0:T(8,128)(2,1)}, bf16[16,7488]{1,0:T(8,128)(2,1)}, u32[]{:S(2)}, u32[]{:S(2)}) %collective-permute-start.2) | collective-permute-done | bytes 239648 | tf_op jit(solution)/shard_map/ppermute | solution.py:29
  92.1 1.1 select_bitcast_fusion.3
  93.2 13.4 %collective-permute-done.3 = bf16[16,7488]{1,0:T(8,128)(2,1)} collective-permute-done((bf16[16,7488]{1,0:T(8,128)(2,1)S(1)}, bf16[16,7488]{1,0:T(8,128)(2,1)}, u32[]{:S(2)}, u32[]{:S(2)}) %collective-permute-start.3) | collective-permute-done | bytes 239648 | tf_op jit(solution)/shard_map/ppermute | solution.py:29
  106.6 1.1 select_bitcast_fusion.1
  107.8 0.9 pad_maximum_fusion.2
  108.8 4.8 %all-to-all-start.1 = ((bf16[4,2,16,2304]{3,2,1,0:T(8,128)(2,1)}), bf16[4,2,16,2304]{3,2,1,0:T(8,128)(2,1)S(1)}, u32[]{:S(2)}, u32[]{:S(2)}) async-start(bf16[4,2,16,2304]{3,2,1,0:T(8,128)(2,1)} %pad_maximum_fusion.2), calls=%async_computation.1 | async-start | bytes 1179648 | tf_op jit(solution)/shard_map/all_to_all | solution.py:111
  113.7 0.9 pad_maximum_fusion.3
  114.6 5.7 %all-to-all-done.1 = bf16[4,2,16,2304]{3,2,1,0:T(8,128)(2,1)S(1)} async-done(((bf16[4,2,16,2304]{3,2,1,0:T(8,128)(2,1)}), bf16[4,2,16,2304]{3,2,1,0:T(8,128)(2,1)S(1)}, u32[]{:S(2)}, u32[]{:S(2)}) %all-to-all-start.1) | async-done | bytes 589856 | tf_op jit(solution)/shard_map/all_to_all | solution.py:111
  120.3 5.5 %all-to-all-start.2 = ((bf16[4,2,16,2304]{3,2,1,0:T(8,128)(2,1)}), bf16[4,2,16,2304]{3,2,1,0:T(8,128)(2,1)S(1)}, u32[]{:S(2)}, u32[]{:S(2)}) async-start(bf16[4,2,16,2304]{3,2,1,0:T(8,128)(2,1)} %pad_maximum_fusion.3), calls=%async_computation.2 | async-start | bytes 1179648 | tf_op jit(solution)/shard_map/all_to_all | solution.py:111
  125.9 0.9 pad_maximum_fusion.4
  126.9 5.3 %all-to-all-done.2 = bf16[4,2,16,2304]{3,2,1,0:T(8,128)(2,1)S(1)} async-done(((bf16[4,2,16,2304]{3,2,1,0:T(8,128)(2,1)}), bf16[4,2,16,2304]{3,2,1,0:T(8,128)(2,1)S(1)}, u32[]{:S(2)}, u32[]{:S(2)}) %all-to-all-start.2) | async-done | bytes 589856 | tf_op jit(solution)/shard_map/all_to_all | solution.py:111
  132.1 5.5 %all-to-all-start.3 = ((bf16[4,2,16,2304]{3,2,1,0:T(8,128)(2,1)}), bf16[4,2,16,2304]{3,2,1,0:T(8,128)(2,1)S(1)}, u32[]{:S(2)}, u32[]{:S(2)}) async-start(bf16[4,2,16,2304]{3,2,1,0:T(8,128)(2,1)} %pad_maximum_fusion.4), calls=%async_computation.3 | async-start | bytes 1179648 | tf_op jit(solution)/shard_map/all_to_all | solution.py:111
  137.6 0.8 dynamic-slice_reduce_fusion
  138.6 5.4 %all-to-all-done.3 = bf16[4,2,16,2304]{3,2,1,0:T(8,128)(2,1)S(1)} async-done(((bf16[4,2,16,2304]{3,2,1,0:T(8,128)(2,1)}), bf16[4,2,16,2304]{3,2,1,0:T(8,128)(2,1)S(1)}, u32[]{:S(2)}, u32[]{:S(2)}) %all-to-all-start.3) | async-done | bytes 589856 | tf_op jit(solution)/shard_map/all_to_all | solution.py:111
  145.0 1.3 fusion.20
  146.3 1.9 collective-permute-start.4
  148.3 9.7 %collective-permute-start.5 = (bf16[144,512]{1,0:T(8,128)(2,1)S(1)}, bf16[144,512]{1,0:T(8,128)(2,1)S(1)}, u32[]{:S(2)}, u32[]{:S(2)}) collective-permute-start(bf16[144,512]{1,0:T(8,128)(2,1)S(1)} %get-tuple-element.46), channel_id=1, source_target_pairs={{0,736},{8,744},{16,752},{24,760},{32,0},{40,8},{48,16},{56,24},{6... | collective-permute-start | bytes 442376 | tf_op jit(solution)/shard_map/ppermute | solution.py:25
  157.9 5.9 %fusion.8 = bf16[512,1728]{1,0:T(8,128)(2,1)S(1)} fusion(f32[512,2304]{1,0:T(8,128)S(1)} %bitcast_convert_fusion.4, f32[1728]{0:T(1024)S(1)} %dynamic-slice_reduce_fusion, f32[1728]{0:T(1024)S(1)} %get-tuple-element.73, f32[1728]{0:T(1024)S(1)} %get-tuple-element.74, f32[1728]{0:T(1024)S(1)} %get-tuple-element.72, f32[1728]{0:T(1024)S(1)} %get-tuple-element.71), kind=kLoop, calls=%fused_computation.12 | loop fusion | flops 12386304 | bytes 21209088 | tf_op jit(solution)/shard_map/convert_element_type | solution.py:158
  163.9 1.4 fusion.23
  166.2 23.8 %all_to_all.25 = bf16[4,3,128,512]{3,2,1,0:T(8,128)(2,1)S(1)} all-to-all(bf16[4,3,128,512]{3,2,1,0:T(8,128)(2,1)S(1)} %maximum_bitcast_fusion), channel_id=1, replica_groups=mesh['elem'=96,'half'=2,'slab'=4] {'slab'}, dimensions={0} | all-to-all | bytes 3145728 | tf_op jit(solution)/shard_map/all_to_all | solution.py:167
  190.4 9.9 %collective-permute-start.6 = (bf16[3,128,512]{2,1,0:T(8,128)(2,1)S(1)}, bf16[3,128,512]{2,1,0:T(8,128)(2,1)S(1)}, u32[]{:S(2)}, u32[]{:S(2)}) collective-permute-start(bf16[3,128,512]{2,1,0:T(8,128)(2,1)S(1)} %reduce_sum.61), channel_id=1, source_target_pairs={{0,4},{4,0},{1,5},{5,1},{2,6},{6,2},{3,7},{7,3},{8,12},{12,8},{9,1... | collective-permute-start | bytes 1179656 | tf_op jit(solution)/shard_map/ppermute | solution.py:29
  200.3 9.5 %collective-permute-done.6 = bf16[3,128,512]{2,1,0:T(8,128)(2,1)S(1)} collective-permute-done((bf16[3,128,512]{2,1,0:T(8,128)(2,1)S(1)}, bf16[3,128,512]{2,1,0:T(8,128)(2,1)S(1)}, u32[]{:S(2)}, u32[]{:S(2)}) %collective-permute-start.6) | collective-permute-done | bytes 393248 | tf_op jit(solution)/shard_map/ppermute | solution.py:29
  209.8 0.8 add_convert_fusion
  210.7 3.8 %collective-permute-start.7 = (bf16[512,128]{1,0:T(8,128)(2,1)S(1)}, bf16[512,128]{1,0:T(8,128)(2,1)S(1)}, u32[]{:S(2)}, u32[]{:S(2)}) collective-permute-start(bf16[512,128]{1,0:T(8,128)(2,1)S(1)} %bitcast.166), channel_id=1, source_target_pairs={{0,760},{8,0},{16,8},{24,16},{32,24},{40,32},{48,40},{56,48},{64,5... | collective-permute-start | bytes 393224 | tf_op jit(solution)/shard_map/ppermute | solution.py:25
  214.5 8.1 %collective-permute-start.8 = (bf16[512,128]{1,0:T(8,128)(2,1)S(1)}, bf16[512,128]{1,0:T(8,128)(2,1)S(1)}, u32[]{:S(2)}, u32[]{:S(2)}) collective-permute-start(bf16[512,128]{1,0:T(8,128)(2,1)S(1)} %bitcast.167), channel_id=1, source_target_pairs={{0,736},{8,744},{16,752},{24,760},{32,0},{40,8},{48,16},{56,24},{6... | collective-permute-start | bytes 393224 | tf_op jit(solution)/shard_map/ppermute | solution.py:25
  222.6 36.4 %all-gather.2.cloned.1.call-done = bf16[3,512,512]{2,1,0:T(8,128)(2,1)} async-done(((bf16[3,128,512]{2,1,0:T(8,128)(2,1)}), bf16[3,512,512]{2,1,0:T(8,128)(2,1)}) %all-gather.2.cloned.1.call-update) | async-done | bytes 1572880 | tf_op jit(solution)/shard_map/all_gather | solution.py:171
  259.0 1.5 convolution_convert_fusion.4
  260.5 4.3 %collective-permute-start.10 = (bf16[512,128]{1,0:T(8,128)(2,1)S(1)}, bf16[512,128]{1,0:T(8,128)(2,1)S(1)}, u32[]{:S(2)}, u32[]{:S(2)}) collective-permute-start(bf16[512,128]{1,0:T(8,128)(2,1)S(1)} %convolution_convert_fusion.4), channel_id=1, source_target_pairs={{0,32},{8,40},{16,48},{24,56},{32,64},{40,72},{48,80},{56,88},{64,... | collective-permute-start | bytes 393224 | tf_op jit(solution)/shard_map/ppermute | solution.py:25
  264.8 1.4 convolution_convert_fusion.5
  266.2 1.9 collective-permute-start.9
  268.1 1.3 fusion.82
  269.8 7.8 %collective-permute-done.10 = bf16[512,128]{1,0:T(8,128)(2,1)S(1)} collective-permute-done((bf16[512,128]{1,0:T(8,128)(2,1)S(1)}, bf16[512,128]{1,0:T(8,128)(2,1)S(1)}, u32[]{:S(2)}, u32[]{:S(2)}) %collective-permute-start.10) | collective-permute-done | bytes 131104 | tf_op jit(solution)/shard_map/ppermute | solution.py:25
  277.6 1.8 collective-permute-done.9
  279.7 1.9 collective-permute-start.11
  281.6 4.1 %collective-permute-start.12 = (bf16[512,128]{1,0:T(8,128)(2,1)S(1)}, bf16[512,128]{1,0:T(8,128)(2,1)S(1)}, u32[]{:S(2)}, u32[]{:S(2)}) collective-permute-start(bf16[512,128]{1,0:T(8,128)(2,1)S(1)} %fusion.43), channel_id=1, source_target_pairs={{0,736},{8,744},{16,752},{24,760},{32,0},{40,8},{48,16},{56,24},{6... | collective-permute-start | bytes 393224 | tf_op jit(solution)/shard_map/ppermute | solution.py:25
  286.0 2.1 collective-permute-start.13
  288.5 2.7 collective-permute-start.14
  291.8 7.4 %collective-permute-done.13 = bf16[512,128]{1,0:T(8,128)(2,1)S(1)} collective-permute-done((bf16[512,128]{1,0:T(8,128)(2,1)S(1)}, bf16[512,128]{1,0:T(8,128)(2,1)S(1)}, u32[]{:S(2)}, u32[]{:S(2)}) %collective-permute-start.13) | collective-permute-done | bytes 131104 | tf_op jit(solution)/shard_map/ppermute | solution.py:25
  299.2 6.8 %collective-permute-done.14 = bf16[512,128]{1,0:T(8,128)(2,1)S(1)} collective-permute-done((bf16[512,128]{1,0:T(8,128)(2,1)S(1)}, bf16[512,128]{1,0:T(8,128)(2,1)S(1)}, u32[]{:S(2)}, u32[]{:S(2)}) %collective-permute-start.14) | collective-permute-done | bytes 131104 | tf_op jit(solution)/shard_map/ppermute | solution.py:25
  306.4 1.9 collective-permute-start.15
  308.3 1.9 collective-permute-start.16
  310.6 2.4 collective-permute-start.17
  313.4 4.5 %collective-permute-start.18 = (bf16[512,128]{1,0:T(8,128)(2,1)S(1)}, bf16[512,128]{1,0:T(8,128)(2,1)S(1)}, u32[]{:S(2)}, u32[]{:S(2)}) collective-permute-start(bf16[512,128]{1,0:T(8,128)(2,1)S(1)} %convolution_convert_fusion), channel_id=1, source_target_pairs={{0,32},{8,40},{16,48},{24,56},{32,64},{40,72},{48,80},{56,88},{64,... | collective-permute-start | bytes 393224 | tf_op jit(solution)/shard_map/ppermute | solution.py:25
  318.5 5.3 %collective-permute-done.17 = bf16[512,128]{1,0:T(8,128)(2,1)S(1)} collective-permute-done((bf16[512,128]{1,0:T(8,128)(2,1)S(1)}, bf16[512,128]{1,0:T(8,128)(2,1)S(1)}, u32[]{:S(2)}, u32[]{:S(2)}) %collective-permute-start.17) | collective-permute-done | bytes 131104 | tf_op jit(solution)/shard_map/ppermute | solution.py:25
  323.8 7.8 %collective-permute-done.18 = bf16[512,128]{1,0:T(8,128)(2,1)S(1)} collective-permute-done((bf16[512,128]{1,0:T(8,128)(2,1)S(1)}, bf16[512,128]{1,0:T(8,128)(2,1)S(1)}, u32[]{:S(2)}, u32[]{:S(2)}) %collective-permute-start.18) | collective-permute-done | bytes 131104 | tf_op jit(solution)/shard_map/ppermute | solution.py:25
  331.9 0.7 fusion.113
  (78 shorter events, 8.3 us)
Async XLA Ops:
  7.9 5.4 %copy-start = (bf16[1,64,13824]{2,1,0:T(8,128)(2,1)S(1)}, bf16[1,64,13824]{2,1,0:T(8,128)(2,1)}, u32[]{:S(2)}) copy-start(bf16[1,64,13824]{2,1,0:T(8,128)(2,1)} %param.5) | copy-start | bytes 5308420
  13.3 9.0 %copy-start.5 = (f32[13824]{0:T(1024)S(1)}, f32[13824]{0:T(1024)}, u32[]{:S(2)}) copy-start(f32[13824]{0:T(1024)} %get-tuple-element.65) | copy-start | bytes 165892
  13.3 9.0 %copy-start.6 = (f32[13824]{0:T(1024)S(1)}, f32[13824]{0:T(1024)}, u32[]{:S(2)}) copy-start(f32[13824]{0:T(1024)} %get-tuple-element.66) | copy-start | bytes 165892
  13.3 9.0 %copy-start.7 = (f32[13824]{0:T(1024)S(1)}, f32[13824]{0:T(1024)}, u32[]{:S(2)}) copy-start(f32[13824]{0:T(1024)} %get-tuple-element.67) | copy-start | bytes 165892
  13.3 9.0 %copy-start.8 = (f32[13824]{0:T(1024)S(1)}, f32[13824]{0:T(1024)}, u32[]{:S(2)}) copy-start(f32[13824]{0:T(1024)} %get-tuple-element.68) | copy-start | bytes 165892
  29.2 18.0 %copy-start.2 = (f32[16,13824]{1,0:T(8,128)S(1)}, f32[16,13824]{1,0:T(8,128)}, u32[]{:S(2)}) copy-start(f32[16,13824]{1,0:T(8,128)} %get-tuple-element.22) | copy-start | bytes 2654212
  32.1 31.3 %collective-permute-start = (bf16[16,7488]{1,0:T(8,128)(2,1)}, bf16[16,7488]{1,0:T(8,128)(2,1)}, u32[]{:S(2)}, u32[]{:S(2)}) collective-permute-start(bf16[16,7488]{1,0:T(8,128)(2,1)} %broadcast_select_fusion.6), channel_id=1, source_target_pairs={{0,4},{4,0},{1,5},{5,1},{2,6},{6,2},{3,7},{7,3},{8,12},{12,8},{9,1... | collective-permute-start | bytes 718856 | tf_op jit(solution)/shard_map/ppermute | solution.py:29
  48.2 28.1 %collective-permute-start.1 = (bf16[16,7488]{1,0:T(8,128)(2,1)}, bf16[16,7488]{1,0:T(8,128)(2,1)S(1)}, u32[]{:S(2)}, u32[]{:S(2)}) collective-permute-start(bf16[16,7488]{1,0:T(8,128)(2,1)} %broadcast_select_fusion.4), channel_id=1, source_target_pairs={{0,4},{4,0},{1,5},{5,1},{2,6},{6,2},{3,7},{7,3},{8,12},{12,8},{9,1... | collective-permute-start | bytes 718856 | tf_op jit(solution)/shard_map/ppermute | solution.py:29
  51.0 41.1 %collective-permute-start.2 = (bf16[16,7488]{1,0:T(8,128)(2,1)}, bf16[16,7488]{1,0:T(8,128)(2,1)}, u32[]{:S(2)}, u32[]{:S(2)}) collective-permute-start(bf16[16,7488]{1,0:T(8,128)(2,1)} %broadcast_select_fusion.2), channel_id=1, source_target_pairs={{0,4},{4,0},{1,5},{5,1},{2,6},{6,2},{3,7},{7,3},{8,12},{12,8},{9,1... | collective-permute-start | bytes 718856 | tf_op jit(solution)/shard_map/ppermute | solution.py:29
  61.5 45.1 %collective-permute-start.3 = (bf16[16,7488]{1,0:T(8,128)(2,1)S(1)}, bf16[16,7488]{1,0:T(8,128)(2,1)}, u32[]{:S(2)}, u32[]{:S(2)}) collective-permute-start(bf16[16,7488]{1,0:T(8,128)(2,1)S(1)} %broadcast_select_fusion), channel_id=1, source_target_pairs={{0,4},{4,0},{1,5},{5,1},{2,6},{6,2},{3,7},{7,3},{8,12},{12,8},{9,1... | collective-permute-start | bytes 718856 | tf_op jit(solution)/shard_map/ppermute | solution.py:29
  65.5 43.2 %all-to-all-start = ((bf16[4,2,16,2304]{3,2,1,0:T(8,128)(2,1)}), bf16[4,2,16,2304]{3,2,1,0:T(8,128)(2,1)S(1)}, u32[]{:S(2)}, u32[]{:S(2)}) async-start(bf16[4,2,16,2304]{3,2,1,0:T(8,128)(2,1)} %pad_maximum_fusion.1), calls=%async_computation | async-start | bytes 1179648 | tf_op jit(solution)/shard_map/all_to_all | solution.py:111
  108.8 17.2 %copy-start.3 = (bf16[4,2,16,2304]{3,2,1,0:T(8,128)(2,1)}, bf16[4,2,16,2304]{3,2,1,0:T(8,128)(2,1)S(1)}, u32[]{:S(2)}) copy-start(bf16[4,2,16,2304]{3,2,1,0:T(8,128)(2,1)S(1)} %all-to-all-done) | copy-start | bytes 1769476
  108.8 11.5 %all-to-all-start.1 = ((bf16[4,2,16,2304]{3,2,1,0:T(8,128)(2,1)}), bf16[4,2,16,2304]{3,2,1,0:T(8,128)(2,1)S(1)}, u32[]{:S(2)}, u32[]{:S(2)}) async-start(bf16[4,2,16,2304]{3,2,1,0:T(8,128)(2,1)} %pad_maximum_fusion.2), calls=%async_computation.1 | async-start | bytes 1179648 | tf_op jit(solution)/shard_map/all_to_all | solution.py:111
  120.3 11.8 %all-to-all-start.2 = ((bf16[4,2,16,2304]{3,2,1,0:T(8,128)(2,1)}), bf16[4,2,16,2304]{3,2,1,0:T(8,128)(2,1)S(1)}, u32[]{:S(2)}, u32[]{:S(2)}) async-start(bf16[4,2,16,2304]{3,2,1,0:T(8,128)(2,1)} %pad_maximum_fusion.3), calls=%async_computation.2 | async-start | bytes 1179648 | tf_op jit(solution)/shard_map/all_to_all | solution.py:111
  125.9 12.6 %copy-start.4 = (bf16[4,2,16,2304]{3,2,1,0:T(8,128)(2,1)S(1)}, bf16[4,2,16,2304]{3,2,1,0:T(8,128)(2,1)}, u32[]{:S(2)}) copy-start(bf16[4,2,16,2304]{3,2,1,0:T(8,128)(2,1)} %copy-done.3) | copy-start | bytes 1769476
  132.1 11.9 %all-to-all-start.3 = ((bf16[4,2,16,2304]{3,2,1,0:T(8,128)(2,1)}), bf16[4,2,16,2304]{3,2,1,0:T(8,128)(2,1)S(1)}, u32[]{:S(2)}, u32[]{:S(2)}) async-start(bf16[4,2,16,2304]{3,2,1,0:T(8,128)(2,1)} %pad_maximum_fusion.4), calls=%async_computation.3 | async-start | bytes 1179648 | tf_op jit(solution)/shard_map/all_to_all | solution.py:111
  137.6 121.3 %all-gather.2.cloned.1.call-start = ((), (), s32[]{:S(2)}) async-start(), calls=%async_computation.5 | async-start | bytes 1966080 | tf_op jit(solution)/shard_map/all_gather | solution.py:171
  144.3 0.7 copy-start.10
  146.3 19.0 %collective-permute-start.4 = (bf16[144,512]{1,0:T(8,128)(2,1)S(1)}, bf16[144,512]{1,0:T(8,128)(2,1)S(1)}, u32[]{:S(2)}, u32[]{:S(2)}) collective-permute-start(bf16[144,512]{1,0:T(8,128)(2,1)S(1)} %get-tuple-element.45), channel_id=1, source_target_pairs={{0,760},{8,0},{16,8},{24,16},{32,24},{40,32},{48,40},{56,48},{64,5... | collective-permute-start | bytes 442376 | tf_op jit(solution)/shard_map/ppermute | solution.py:25
  148.3 17.4 %collective-permute-start.5 = (bf16[144,512]{1,0:T(8,128)(2,1)S(1)}, bf16[144,512]{1,0:T(8,128)(2,1)S(1)}, u32[]{:S(2)}, u32[]{:S(2)}) collective-permute-start(bf16[144,512]{1,0:T(8,128)(2,1)S(1)} %get-tuple-element.46), channel_id=1, source_target_pairs={{0,736},{8,744},{16,752},{24,760},{32,0},{40,8},{48,16},{56,24},{6... | collective-permute-start | bytes 442376 | tf_op jit(solution)/shard_map/ppermute | solution.py:25
  190.0 20.7 %copy-start.9 = (bf16[1,512,128]{2,1,0:T(8,128)(2,1)S(1)}, bf16[1,512,128]{2,1,0:T(8,128)(2,1)}, u32[]{:S(2)}) copy-start(bf16[1,512,128]{2,1,0:T(8,128)(2,1)} %param.8) | copy-start | bytes 393220
  190.4 19.4 %collective-permute-start.6 = (bf16[3,128,512]{2,1,0:T(8,128)(2,1)S(1)}, bf16[3,128,512]{2,1,0:T(8,128)(2,1)S(1)}, u32[]{:S(2)}, u32[]{:S(2)}) collective-permute-start(bf16[3,128,512]{2,1,0:T(8,128)(2,1)S(1)} %reduce_sum.61), channel_id=1, source_target_pairs={{0,4},{4,0},{1,5},{5,1},{2,6},{6,2},{3,7},{7,3},{8,12},{12,8},{9,1... | collective-permute-start | bytes 1179656 | tf_op jit(solution)/shard_map/ppermute | solution.py:29
  210.7 58.8 %collective-permute-start.7 = (bf16[512,128]{1,0:T(8,128)(2,1)S(1)}, bf16[512,128]{1,0:T(8,128)(2,1)S(1)}, u32[]{:S(2)}, u32[]{:S(2)}) collective-permute-start(bf16[512,128]{1,0:T(8,128)(2,1)S(1)} %bitcast.166), channel_id=1, source_target_pairs={{0,760},{8,0},{16,8},{24,16},{32,24},{40,32},{48,40},{56,48},{64,5... | collective-permute-start | bytes 393224 | tf_op jit(solution)/shard_map/ppermute | solution.py:25
  214.5 55.3 %collective-permute-start.8 = (bf16[512,128]{1,0:T(8,128)(2,1)S(1)}, bf16[512,128]{1,0:T(8,128)(2,1)S(1)}, u32[]{:S(2)}, u32[]{:S(2)}) collective-permute-start(bf16[512,128]{1,0:T(8,128)(2,1)S(1)} %bitcast.167), channel_id=1, source_target_pairs={{0,736},{8,744},{16,752},{24,760},{32,0},{40,8},{48,16},{56,24},{6... | collective-permute-start | bytes 393224 | tf_op jit(solution)/shard_map/ppermute | solution.py:25
  259.0 10.5 %copy-start.1 = (bf16[3,512,512]{2,1,0:T(8,128)(2,1)S(1)}, bf16[3,512,512]{2,1,0:T(8,128)(2,1)}, u32[]{:S(2)}) copy-start(bf16[3,512,512]{2,1,0:T(8,128)(2,1)} %all-gather.2.cloned.1.call-done) | copy-start | bytes 4718596
  260.5 17.2 %collective-permute-start.10 = (bf16[512,128]{1,0:T(8,128)(2,1)S(1)}, bf16[512,128]{1,0:T(8,128)(2,1)S(1)}, u32[]{:S(2)}, u32[]{:S(2)}) collective-permute-start(bf16[512,128]{1,0:T(8,128)(2,1)S(1)} %convolution_convert_fusion.4), channel_id=1, source_target_pairs={{0,32},{8,40},{16,48},{24,56},{32,64},{40,72},{48,80},{56,88},{64,... | collective-permute-start | bytes 393224 | tf_op jit(solution)/shard_map/ppermute | solution.py:25
  266.2 13.2 %collective-permute-start.9 = (bf16[512,128]{1,0:T(8,128)(2,1)S(1)}, bf16[512,128]{1,0:T(8,128)(2,1)S(1)}, u32[]{:S(2)}, u32[]{:S(2)}) collective-permute-start(bf16[512,128]{1,0:T(8,128)(2,1)S(1)} %convolution_convert_fusion.5), channel_id=1, source_target_pairs={{0,8},{8,16},{16,24},{24,32},{32,40},{40,48},{48,56},{56,64},{64,7... | collective-permute-start | bytes 393224 | tf_op jit(solution)/shard_map/ppermute | solution.py:25
  279.7 11.8 %collective-permute-start.11 = (bf16[512,128]{1,0:T(8,128)(2,1)S(1)}, bf16[512,128]{1,0:T(8,128)(2,1)S(1)}, u32[]{:S(2)}, u32[]{:S(2)}) collective-permute-start(bf16[512,128]{1,0:T(8,128)(2,1)S(1)} %fusion.43), channel_id=1, source_target_pairs={{0,760},{8,0},{16,8},{24,16},{32,24},{40,32},{48,40},{56,48},{64,5... | collective-permute-start | bytes 393224 | tf_op jit(solution)/shard_map/ppermute | solution.py:25
  281.6 24.4 %collective-permute-start.12 = (bf16[512,128]{1,0:T(8,128)(2,1)S(1)}, bf16[512,128]{1,0:T(8,128)(2,1)S(1)}, u32[]{:S(2)}, u32[]{:S(2)}) collective-permute-start(bf16[512,128]{1,0:T(8,128)(2,1)S(1)} %fusion.43), channel_id=1, source_target_pairs={{0,736},{8,744},{16,752},{24,760},{32,0},{40,8},{48,16},{56,24},{6... | collective-permute-start | bytes 393224 | tf_op jit(solution)/shard_map/ppermute | solution.py:25
  286.0 13.2 %collective-permute-start.13 = (bf16[512,128]{1,0:T(8,128)(2,1)S(1)}, bf16[512,128]{1,0:T(8,128)(2,1)S(1)}, u32[]{:S(2)}, u32[]{:S(2)}) collective-permute-start(bf16[512,128]{1,0:T(8,128)(2,1)S(1)} %convolution_convert_fusion.3), channel_id=1, source_target_pairs={{0,8},{8,16},{16,24},{24,32},{32,40},{40,48},{48,56},{56,64},{64,7... | collective-permute-start | bytes 393224 | tf_op jit(solution)/shard_map/ppermute | solution.py:25
  288.5 17.5 %collective-permute-start.14 = (bf16[512,128]{1,0:T(8,128)(2,1)S(1)}, bf16[512,128]{1,0:T(8,128)(2,1)S(1)}, u32[]{:S(2)}, u32[]{:S(2)}) collective-permute-start(bf16[512,128]{1,0:T(8,128)(2,1)S(1)} %convolution_convert_fusion.2), channel_id=1, source_target_pairs={{0,32},{8,40},{16,48},{24,56},{32,64},{40,72},{48,80},{56,88},{64,... | collective-permute-start | bytes 393224 | tf_op jit(solution)/shard_map/ppermute | solution.py:25
  306.4 11.8 %collective-permute-start.15 = (bf16[512,128]{1,0:T(8,128)(2,1)S(1)}, bf16[512,128]{1,0:T(8,128)(2,1)S(1)}, u32[]{:S(2)}, u32[]{:S(2)}) collective-permute-start(bf16[512,128]{1,0:T(8,128)(2,1)S(1)} %fusion.42), channel_id=1, source_target_pairs={{0,760},{8,0},{16,8},{24,16},{32,24},{40,32},{48,40},{56,48},{64,5... | collective-permute-start | bytes 393224 | tf_op jit(solution)/shard_map/ppermute | solution.py:25
  308.3 23.3 %collective-permute-start.16 = (bf16[512,128]{1,0:T(8,128)(2,1)S(1)}, bf16[512,128]{1,0:T(8,128)(2,1)S(1)}, u32[]{:S(2)}, u32[]{:S(2)}) collective-permute-start(bf16[512,128]{1,0:T(8,128)(2,1)S(1)} %fusion.42), channel_id=1, source_target_pairs={{0,736},{8,744},{16,752},{24,760},{32,0},{40,8},{48,16},{56,24},{6... | collective-permute-start | bytes 393224 | tf_op jit(solution)/shard_map/ppermute | solution.py:25
  310.6 13.2 %collective-permute-start.17 = (bf16[512,128]{1,0:T(8,128)(2,1)S(1)}, bf16[512,128]{1,0:T(8,128)(2,1)S(1)}, u32[]{:S(2)}, u32[]{:S(2)}) collective-permute-start(bf16[512,128]{1,0:T(8,128)(2,1)S(1)} %convolution_convert_fusion.1), channel_id=1, source_target_pairs={{0,8},{8,16},{16,24},{24,32},{32,40},{40,48},{48,56},{56,64},{64,7... | collective-permute-start | bytes 393224 | tf_op jit(solution)/shard_map/ppermute | solution.py:25
  313.4 18.2 %collective-permute-start.18 = (bf16[512,128]{1,0:T(8,128)(2,1)S(1)}, bf16[512,128]{1,0:T(8,128)(2,1)S(1)}, u32[]{:S(2)}, u32[]{:S(2)}) collective-permute-start(bf16[512,128]{1,0:T(8,128)(2,1)S(1)} %convolution_convert_fusion), channel_id=1, source_target_pairs={{0,32},{8,40},{16,48},{24,56},{32,64},{40,72},{48,80},{56,88},{64,... | collective-permute-start | bytes 393224 | tf_op jit(solution)/shard_map/ppermute | solution.py:25
Sparse Core Ops, SparseCore 0:
  210.8 48.0 all-gather.1

commit v2 on v1

--- a/solution.py
+++ b/solution.py
@@ -81,24 +81,40 @@
     return (chosen[:, None] == points[None, :]).astype(jnp.bfloat16)
 
 
-def slab_rows(orbitals, potential, kept_count, half, band):
+def transposed_dot(a, b, contract_a, contract_b):
+    return lax.dot_general(
+        a, b, (((contract_a,), (contract_b,)), ((), ())), preferred_element_type=jnp.float32
+    )
+
+
+def slab_applied(rows, length, slab_potential):
+    padded = jnp.pad(rows.astype(jnp.float32), ((0, 0), (PLANE, 0)))
+    applied = flat_hamiltonian(padded, length, slab_potential, side_masks(length))
+    return jnp.concatenate(
+        [applied.astype(jnp.bfloat16), -rows[:, length - PLANE : length]], axis=1
+    )
+
+
+def slab_rows(orbitals, potential, kept_count, slab_potential, half, band):
     per_device = orbitals.shape[0]
     step = per_device // CHUNKS
     half_points = G // HALVES
     slab_points = half_points // SLABS
     taken = half_points + PLANE
-    arrived = []
+    arrived, applied = [], []
+    tied = None
     for chunk in range(CHUNKS):
+        source = orbitals[chunk * step : (chunk + 1) * step]
+        if tied is not None:
+            source, tied = lax.optimization_barrier((source, tied))
         basis = filtered_basis(
-            orbitals[chunk * step : (chunk + 1) * step],
-            potential,
-            kept_count,
-            band * per_device + chunk * step,
+            source, potential, kept_count, band * per_device + chunk * step
         )
         padded = jnp.pad(basis, ((0, 0), (0, PLANE)))
         lower, upper = padded[:, :taken], padded[:, half_points:]
         kept = jnp.where(half == 0, lower, upper)
-        other = swap_halves(jnp.where(half == 0, upper, lower))
+        leaving = tied = jnp.where(half == 0, upper, lower)
+        other = swap_halves(leaving)
         ordered = jnp.stack(
             [jnp.where(half == 0, kept, other), jnp.where(half == 0, other, kept)]
         )
@@ -108,55 +124,85 @@
                 for s in range(SLABS)
             ]
         )
-        arrived.append(lax.all_to_all(pieces, "slab", 0, 0, tiled=True))
-    rows = jnp.stack(arrived, axis=2)
-    return jnp.swapaxes(rows, 0, 1).reshape(-1, slab_points + PLANE)
-
-
-def transposed_dot(a, b, contract_a, contract_b):
-    return lax.dot_general(
-        a, b, (((contract_a,), (contract_b,)), ((), ())), preferred_element_type=jnp.float32
-    )
-
-
-def apply_blocks(h_self, h_z, h_y, current):
-    ahead_z = from_behind(current, "elem", -1)
-    ahead_y = from_behind(current, "elem", -EB)
+        rows = lax.all_to_all(pieces, "slab", 0, 0, tiled=True)
+        rows = lax.optimization_barrier(rows.reshape(-1, slab_points + PLANE))
+        applied.append(lax.optimization_barrier(slab_applied(rows, slab_points, slab_potential)))
+        arrived.append(rows)
+    return jnp.concatenate(arrived), jnp.concatenate(applied)
+
+
+def arrival_order(rows):
+    columns = rows.shape[1]
+    split = rows.reshape(HALVES, SLABS, CHUNKS, -1, columns)
+    return split.transpose(2, 1, 0, 3, 4).reshape(-1, columns)
+
+
+def natural_order(rows):
+    columns = rows.shape[1]
+    split = rows.reshape(CHUNKS, SLABS, HALVES, -1, columns)
+    return split.transpose(2, 1, 0, 3, 4).reshape(-1, columns)
+
+
+def pair_swap(value, by, odd):
+    devices = lax.axis_size("elem")
+    low = [i for i in range(devices) if (i // by) % 2 == odd]
+    pairs = [(i, (i + by) % devices) for i in low]
+    return lax.ppermute(value, "elem", pairs + [(j, i) for i, j in pairs])
+
+
+def exchange(value, product, by):
+    even = (lax.axis_index("elem") // by) % 2 == 0
+    from_odd = pair_swap(jnp.where(even, value, product), by, 1)
+    from_even = pair_swap(jnp.where(even, product, value), by, 0)
+    ahead = jnp.where(even, from_even, from_odd)
+    behind = jnp.where(even, from_odd, from_even)
+    return ahead, behind
+
+
+def neighbours_of(current, back_z, back_y):
+    ahead_y, behind_y = exchange(current, back_y, EB)
+    ahead_z, behind_z = exchange(current, back_z, 1)
+    return ahead_z, ahead_y, behind_z, behind_y
+
+
+def scaled(blocks, current, ahead=None):
+    h_self, h_z, h_y = blocks
+    back_y = transposed_dot(h_y, current, 0, 0).astype(jnp.bfloat16)
     back_z = transposed_dot(h_z, current, 0, 0).astype(jnp.bfloat16)
-    back_y = transposed_dot(h_y, current, 0, 0).astype(jnp.bfloat16)
-    behind_z = from_behind(back_z, "elem", 1)
-    behind_y = from_behind(back_y, "elem", EB)
+    if ahead is None:
+        ahead_z, ahead_y, behind_z, behind_y = neighbours_of(current, back_z, back_y)
+    else:
+        ahead_z, ahead_y = ahead
+        behind_y = from_behind(back_y, "elem", EB)
+        behind_z = from_behind(back_z, "elem", 1)
     running = transposed_dot(h_self, current, 1, 0)
     running = running + transposed_dot(h_z, ahead_z, 1, 0)
     running = running + transposed_dot(h_y, ahead_y, 1, 0)
-    return running + behind_z.astype(jnp.float32) + behind_y.astype(jnp.float32)
-
-
-def scaled(blocks, current):
-    return (apply_blocks(*blocks, current) - SHIFT_CENTER * current.astype(jnp.float32)) / HALF_WIDTH
-
-
-def on_device(orbitals, potential, basis_count, states):
+    running = running + behind_z.astype(jnp.float32) + behind_y.astype(jnp.float32)
+    return (running - SHIFT_CENTER * current.astype(jnp.float32)) / HALF_WIDTH
+
+
+def device_body(orbitals, potential, basis_count, states):
     half = lax.axis_index("half")
     slab = lax.axis_index("slab")
     band = half * SLABS + slab
-    extended = slab_rows(orbitals[0], potential[0], basis_count[0], half, band)
+    length = G // (HALVES * SLABS)
+    planes = length // PLANE
+    slab_potential = lax.dynamic_slice_in_dim(potential[0], band * length, length, 0)
+
+    start = arrival_order(states[0])
+    ahead = (from_behind(start, "elem", -1), from_behind(start, "elem", -EB))
+
+    extended, applied = slab_rows(
+        orbitals[0], potential[0], basis_count[0], slab_potential, half, band
+    )
     total = extended.shape[0]
-    length = extended.shape[1] - PLANE
-    planes = length // PLANE
-    own = extended[:, :length]
-
-    faces = transposed_dot(face_selector(planes), own, 1, 1).astype(jnp.bfloat16)
+
+    faces = transposed_dot(face_selector(planes), extended[:, :length], 1, 1)
+    faces = faces.astype(jnp.bfloat16)
     width = 2 * planes * P_SIZE
+    other_y = from_behind(faces[width : 2 * width], "elem", -EB)
     other_z = from_behind(faces[:width], "elem", -1)
-    other_y = from_behind(faces[width : 2 * width], "elem", -EB)
-
-    slab_potential = lax.dynamic_slice_in_dim(potential[0], band * length, length, 0)
-    padded = jnp.pad(extended.astype(jnp.float32), ((0, 0), (PLANE, 0)))
-    applied = flat_hamiltonian(padded, length, slab_potential, side_masks(length))
-    applied = jnp.concatenate(
-        [applied.astype(jnp.bfloat16), -own[:, length - PLANE :]], axis=1
-    )
     h_self = transposed_dot(extended, applied, 1, 1) * (1.0 / G)
     weight = -0.5 / PLANE
     h_z = transposed_dot(faces[2 * width : 3 * width], other_z, 0, 0) * weight
@@ -168,15 +214,16 @@
     summed = jnp.sum(pieces.astype(jnp.float32), axis=0).astype(jnp.bfloat16)
     swapped = swap_halves(summed)
     summed = (summed.astype(jnp.float32) + swapped.astype(jnp.float32)).astype(jnp.bfloat16)
-    blocks = lax.all_gather(summed, "slab", axis=1, tiled=True)
+    copies = jnp.broadcast_to(summed[None], (SLABS,) + summed.shape)
+    blocks = lax.all_to_all(copies, "slab", 0, 0, tiled=True)
+    blocks = blocks.swapaxes(0, 1).reshape(3, total, total)
     blocks = (blocks[0], blocks[1], blocks[2])
 
-    start = states[0]
-    first = scaled(blocks, start).astype(jnp.bfloat16)
+    first = scaled(blocks, start, ahead).astype(jnp.bfloat16)
     second = (2.0 * scaled(blocks, first) - start.astype(jnp.float32)).astype(jnp.bfloat16)
     third = 2.0 * scaled(blocks, second) - first.astype(jnp.float32)
     magnitude = jnp.sqrt(jnp.mean(third * third, axis=0, keepdims=True) + 1e-06)
-    return (third / magnitude).astype(jnp.bfloat16)[None]
+    return natural_order((third / magnitude).astype(jnp.bfloat16))[None]
 
 
 def solution(mesh):
@@ -185,5 +232,5 @@
     both = ("half", "slab")
     placed = (P("elem", both, None), P("elem", None), P("elem"), P("elem", None, both))
     return jax.shard_map(
-        on_device, mesh=inner, in_specs=placed, out_specs=P("elem", None, both), check_vma=False
-    )
+        device_body, mesh=inner, in_specs=placed, out_specs=P("elem", None, both), check_vma=False
+    )

time: 344 us -> 314 us (0.913)
  between operations: 14.8 us -> 1.47 us
  waiting for transfers between devices: 131 us -> 119 us
    all_gather x1 -> x0, waiting for transfers between devices: 36.4 us -> none  [on_device(): blocks = lax.all_gather(summed, 'slab', axis=1, tiled=True)]
    ppermute x14 -> x6, starting transfers between devices: 51.2 us -> 25.5 us  [from_behind(): lax.ppermute(value, axis, [(i, (i + by) % devices) for i in range(devices)])]
    ppermute x0 -> x8, waiting for transfers between devices: none -> 24.4 us  [pair_swap(): return lax.ppermute(value, 'elem', pairs + [(j, i) for i, j in pairs])]
    ppermute x0 -> x8, starting transfers between devices: none -> 22.7 us  [pair_swap(): return lax.ppermute(value, 'elem', pairs + [(j, i) for i, j in pairs])]
    ppermute x14 -> x6, waiting for transfers between devices: 36.9 us -> 15 us  [from_behind(): lax.ppermute(value, axis, [(i, (i + by) % devices) for i in range(devices)])]
    ppermute x5, waiting for transfers between devices: 41.4 us -> 56.2 us  [swap_halves(): return lax.ppermute(value, 'half', [(0, 1), (1, 0)])]
    all_to_all x4 -> x5, waiting for transfers between devices: 16.3 us -> 23.9 us  [the longest x4 15 us: slab_rows(): rows = lax.all_to_all(pieces, 'slab', 0, 0, tiled=True)]
    ppermute x5, starting transfers between devices: 39 us -> 31.8 us  [swap_halves(): return lax.ppermute(value, 'half', [(0, 1), (1, 0)])]
  transfers between devices with their start and end apart: 24 -> 24, of which waited for: 14 -> 16; matrix products, arithmetic and copies ran while one was open for 7% -> 9% of each run, Pallas kernels for 0% -> 0%
where the time goes in v2:
time: 314 us; the launch traced here: 312 us
  waiting for transfers between devices  119 us (38%)
  starting transfers between devices  111 us (35%)
  other arithmetic  43.4 us (14%)
  blocking collectives  22.6 us (7%)
  matrix products  10.6 us (3%)
  local copies, waits for them, and re-layouts  3.24 us (1%)
    ppermute x5, waiting for transfers between devices, swap_halves(): return lax.ppermute(value, 'half', [(0, 1), (1, 0)])  56.2 us
    ppermute x5, starting transfers between devices, swap_halves(): return lax.ppermute(value, 'half', [(0, 1), (1, 0)])  31.8 us
    ppermute x6, starting transfers between devices, from_behind(): lax.ppermute(value, axis, [(i, (i + by) % devices) for i in range(devices)])  25.5 us
    all_to_all x4, starting transfers between devices, slab_rows(): rows = lax.all_to_all(pieces, 'slab', 0, 0, tiled=True)  25.1 us
    ppermute x8, waiting for transfers between devices, pair_swap(): return lax.ppermute(value, 'elem', pairs + [(j, i) for i, j in pairs])  24.4 us
    ppermute x8, starting transfers between devices, pair_swap(): return lax.ppermute(value, 'elem', pairs + [(j, i) for i, j in pairs])  22.7 us
    all_to_all x1, blocking collectives, device_body(): pieces = lax.all_to_all(partial, 'slab', 0, 0, tiled=True)  22.6 us
    all_to_all x4, waiting for transfers between devices, slab_rows(): rows = lax.all_to_all(pieces, 'slab', 0, 0, tiled=True)  15 us
  transfers between devices with their start and end apart: 24, of which 16 were waited for; matrix products, arithmetic and copies ran while one was open for 9% of the time, Pallas kernels for 0%

profile of v2, /device:TPU:6, one launch (start us, length us, event | category | flops | bytes accessed | tf_op | source)
XLA Modules:
  0.0 311.8 jit_solution(3938730442235189686)
XLA Ops:
  0.1 2.8 bitcast_convert_fusion
  3.1 4.5 %broadcast_multiply_fusion.3 = (f32[16,13824]{1,0:T(8,128)S(1)}, f32[16,13824]{1,0:T(8,128)S(1)}) fusion(f32[13824]{0:T(1024)S(1)} %reduce.1, f32[13824]{0:T(1024)S(1)} %get-tuple-element.80, f32[13824]{0:T(1024)S(1)} %get-tuple-element.81, f32[13824]{0:T(1024)S(1)} %get-tuple-element.79, f32[13824]{0:T(1024)S(1)} %get-tuple-element.78, ...), kind=kLoop, calls=%fused_computation.242 | loop fusion | flops 3760128 | bytes 3373056 | tf_op jit(solution)/shard_map/div | solution.py:63
  7.6 2.5 multiply_reduce_fusion.3
  10.8 1.3 select_convert_fusion.3
  12.9 15.1 %collective-permute-start = (bf16[16,7488]{1,0:T(8,128)(2,1)}, bf16[16,7488]{1,0:T(8,128)(2,1)S(1)}, u32[]{:S(2)}, u32[]{:S(2)}) collective-permute-start(bf16[16,7488]{1,0:T(8,128)(2,1)} %broadcast_select_fusion.6), channel_id=1, source_target_pairs={{0,4},{4,0},{1,5},{5,1},{2,6},{6,2},{3,7},{7,3},{8,12},{12,8},{9,1... | collective-permute-start | bytes 718856 | tf_op jit(solution)/shard_map/ppermute | solution.py:29
  28.1 1.4 broadcast_multiply_fusion.2
  29.5 1.5 multiply_reduce_fusion.2
  32.0 1.9 collective-permute-start.1
  34.0 1.4 broadcast_multiply_fusion.1
  35.4 1.5 multiply_reduce_fusion.1
  37.2 10.4 %collective-permute-start.2 = (bf16[16,7488]{1,0:T(8,128)(2,1)S(1)}, bf16[16,7488]{1,0:T(8,128)(2,1)S(1)}, u32[]{:S(2)}, u32[]{:S(2)}) collective-permute-start(bf16[16,7488]{1,0:T(8,128)(2,1)S(1)} %broadcast_select_fusion.2), channel_id=1, source_target_pairs={{0,4},{4,0},{1,5},{5,1},{2,6},{6,2},{3,7},{7,3},{8,12},{12,8},{9,1... | collective-permute-start | bytes 718856 | tf_op jit(solution)/shard_map/ppermute | solution.py:29
  47.7 1.4 broadcast_multiply_fusion
  49.1 1.5 multiply_reduce_fusion
  50.9 1.9 collective-permute-start.3
  55.3 8.0 %all-to-all-start = ((bf16[4,2,16,2304]{3,2,1,0:T(8,128)(2,1)}), bf16[4,2,16,2304]{3,2,1,0:T(8,128)(2,1)S(1)}, u32[]{:S(2)}, u32[]{:S(2)}) async-start(bf16[4,2,16,2304]{3,2,1,0:T(8,128)(2,1)} %pad_maximum_fusion), calls=%async_computation | async-start | bytes 1179648 | tf_op jit(solution)/shard_map/all_to_all | solution.py:127
  63.3 24.4 %collective-permute-done.1 = bf16[16,7488]{1,0:T(8,128)(2,1)} collective-permute-done((bf16[16,7488]{1,0:T(8,128)(2,1)}, bf16[16,7488]{1,0:T(8,128)(2,1)}, u32[]{:S(2)}, u32[]{:S(2)}) %collective-permute-start.1) | collective-permute-done | bytes 239648 | tf_op jit(solution)/shard_map/ppermute | solution.py:29
  87.7 1.1 select_bitcast_fusion.5
  88.8 4.0 %collective-permute-done.2 = bf16[16,7488]{1,0:T(8,128)(2,1)S(1)} collective-permute-done((bf16[16,7488]{1,0:T(8,128)(2,1)S(1)}, bf16[16,7488]{1,0:T(8,128)(2,1)S(1)}, u32[]{:S(2)}, u32[]{:S(2)}) %collective-permute-start.2) | collective-permute-done | bytes 239648 | tf_op jit(solution)/shard_map/ppermute | solution.py:29
  93.1 4.8 %collective-permute-done.3 = bf16[16,7488]{1,0:T(8,128)(2,1)S(1)} collective-permute-done((bf16[16,7488]{1,0:T(8,128)(2,1)S(1)}, bf16[16,7488]{1,0:T(8,128)(2,1)S(1)}, u32[]{:S(2)}, u32[]{:S(2)}) %collective-permute-start.3) | collective-permute-done | bytes 239648 | tf_op jit(solution)/shard_map/ppermute | solution.py:29
  98.2 0.9 pad_maximum_fusion.1
  99.1 4.8 %all-to-all-start.1 = ((bf16[4,2,16,2304]{3,2,1,0:T(8,128)(2,1)}), bf16[4,2,16,2304]{3,2,1,0:T(8,128)(2,1)S(1)}, u32[]{:S(2)}, u32[]{:S(2)}) async-start(bf16[4,2,16,2304]{3,2,1,0:T(8,128)(2,1)} %pad_maximum_fusion.1), calls=%async_computation.1 | async-start | bytes 1179648 | tf_op jit(solution)/shard_map/all_to_all | solution.py:127
  104.0 0.9 pad_maximum_fusion.2
  104.9 7.2 %all-to-all-done.1 = bf16[4,2,16,2304]{3,2,1,0:T(8,128)(2,1)S(1)} async-done(((bf16[4,2,16,2304]{3,2,1,0:T(8,128)(2,1)}), bf16[4,2,16,2304]{3,2,1,0:T(8,128)(2,1)S(1)}, u32[]{:S(2)}, u32[]{:S(2)}) %all-to-all-start.1) | async-done | bytes 589856 | tf_op jit(solution)/shard_map/all_to_all | solution.py:127
  112.1 6.2 %all-to-all-start.2 = ((bf16[4,2,16,2304]{3,2,1,0:T(8,128)(2,1)}), bf16[4,2,16,2304]{3,2,1,0:T(8,128)(2,1)}, u32[]{:S(2)}, u32[]{:S(2)}) async-start(bf16[4,2,16,2304]{3,2,1,0:T(8,128)(2,1)} %pad_maximum_fusion.2), calls=%async_computation.2 | async-start | bytes 1179648 | tf_op jit(solution)/shard_map/all_to_all | solution.py:127
  120.0 5.7 %all-to-all-done.2 = bf16[4,2,16,2304]{3,2,1,0:T(8,128)(2,1)} async-done(((bf16[4,2,16,2304]{3,2,1,0:T(8,128)(2,1)}), bf16[4,2,16,2304]{3,2,1,0:T(8,128)(2,1)}, u32[]{:S(2)}, u32[]{:S(2)}) %all-to-all-start.2) | async-done | bytes 589856 | tf_op jit(solution)/shard_map/all_to_all | solution.py:127
  125.8 6.2 %all-to-all-start.3 = ((bf16[4,2,16,2304]{3,2,1,0:T(8,128)(2,1)}), bf16[4,2,16,2304]{3,2,1,0:T(8,128)(2,1)}, u32[]{:S(2)}, u32[]{:S(2)}) async-start(bf16[4,2,16,2304]{3,2,1,0:T(8,128)(2,1)} %pad_maximum_fusion.3), calls=%async_computation.3 | async-start | bytes 1179648 | tf_op jit(solution)/shard_map/all_to_all | solution.py:127
  131.9 1.1 convert_element_type.324
  133.1 1.6 slice_negate_fusion.2
  134.7 1.6 slice_negate_fusion.1
  136.3 2.1 all-to-all-done.3
  138.4 1.2 convert_element_type.326
  139.6 0.9 slice_negate_fusion
  140.6 2.8 fusion.52
  143.7 2.8 fusion.72
  147.7 2.4 fusion.24
  150.2 1.9 collective-permute-start.4
  152.1 6.0 %collective-permute-start.5 = (bf16[144,512]{1,0:T(8,128)(2,1)S(1)}, bf16[144,512]{1,0:T(8,128)(2,1)S(1)}, u32[]{:S(2)}, u32[]{:S(2)}) collective-permute-start(bf16[144,512]{1,0:T(8,128)(2,1)S(1)} %get-tuple-element.43), channel_id=1, source_target_pairs={{0,736},{8,744},{16,752},{24,760},{32,0},{40,8},{48,16},{56,24},{6... | collective-permute-start | bytes 442376 | tf_op jit(solution)/shard_map/ppermute | solution.py:25
  158.1 2.7 multiply_convert_fusion
  161.1 4.3 %collective-permute-done.5 = bf16[144,512]{1,0:T(8,128)(2,1)S(1)} collective-permute-done((bf16[144,512]{1,0:T(8,128)(2,1)S(1)}, bf16[144,512]{1,0:T(8,128)(2,1)S(1)}, u32[]{:S(2)}, u32[]{:S(2)}) %collective-permute-start.5) | collective-permute-done | bytes 147488 | tf_op jit(solution)/shard_map/ppermute | solution.py:25
  166.0 22.6 %all_to_all.30 = bf16[4,3,128,512]{3,2,1,0:T(8,128)(2,1)S(1)} all-to-all(bf16[4,3,128,512]{3,2,1,0:T(8,128)(2,1)S(1)} %maximum_bitcast_fusion), channel_id=1, replica_groups=mesh['elem'=96,'half'=2,'slab'=4] {'slab'}, dimensions={0} | all-to-all | bytes 3145728 | tf_op jit(solution)/shard_map/all_to_all | solution.py:213
  189.0 2.5 collective-permute-start.6
  191.5 23.0 %collective-permute-done.6 = bf16[3,128,512]{2,1,0:T(8,128)(2,1)S(1)} collective-permute-done((bf16[3,128,512]{2,1,0:T(8,128)(2,1)S(1)}, bf16[3,128,512]{2,1,0:T(8,128)(2,1)S(1)}, u32[]{:S(2)}, u32[]{:S(2)}) %collective-permute-start.6) | collective-permute-done | bytes 393248 | tf_op jit(solution)/shard_map/ppermute | solution.py:29
  214.6 1.3 broadcast_in_dim.37
  215.9 5.7 %all-to-all-start.5 = ((bf16[4,3,128,512]{3,2,1,0:T(8,128)(2,1)}), bf16[4,3,128,512]{3,2,1,0:T(8,128)(2,1)S(1)}, u32[]{:S(2)}, u32[]{:S(2)}) async-start(bf16[4,3,128,512]{3,2,1,0:T(8,128)(2,1)} %broadcast_in_dim.37), calls=%async_computation.5 | async-start | bytes 3145728 | tf_op jit(solution)/shard_map/all_to_all | solution.py:218
  221.7 2.0 collective-permute-start.7
  223.7 7.8 %collective-permute-start.8 = (bf16[512,128]{1,0:T(8,128)(2,1)S(1)}, bf16[512,128]{1,0:T(8,128)(2,1)S(1)}, u32[]{:S(2)}, u32[]{:S(2)}) collective-permute-start(bf16[512,128]{1,0:T(8,128)(2,1)S(1)} %bitcast.137), channel_id=1, source_target_pairs={{0,736},{8,744},{16,752},{24,760},{32,0},{40,8},{48,16},{56,24},{6... | collective-permute-start | bytes 393224 | tf_op jit(solution)/shard_map/ppermute | solution.py:25
  231.5 8.9 %all-to-all-done.5 = bf16[4,3,128,512]{3,2,1,0:T(8,128)(2,1)S(1)} async-done(((bf16[4,3,128,512]{3,2,1,0:T(8,128)(2,1)}), bf16[4,3,128,512]{3,2,1,0:T(8,128)(2,1)S(1)}, u32[]{:S(2)}, u32[]{:S(2)}) %all-to-all-start.5) | async-done | bytes 1572896 | tf_op jit(solution)/shard_map/all_to_all | solution.py:218
  240.9 5.9 %collective-permute-start.10 = (bf16[512,128]{1,0:T(8,128)(2,1)S(1)}, bf16[512,128]{1,0:T(8,128)(2,1)S(1)}, u32[]{:S(2)}, u32[]{:S(2)}) collective-permute-start(bf16[512,128]{1,0:T(8,128)(2,1)S(1)} %convolution_convert_fusion.4), channel_id=1, source_target_pairs={{0,32},{8,40},{16,48},{24,56},{32,64},{40,72},{48,80},{56,88},{64,... | collective-permute-start | bytes 393224 | tf_op jit(solution)/shard_map/ppermute | solution.py:25
  247.1 1.9 collective-permute-start.9
  249.7 7.2 %collective-permute-done.10 = bf16[512,128]{1,0:T(8,128)(2,1)S(1)} collective-permute-done((bf16[512,128]{1,0:T(8,128)(2,1)S(1)}, bf16[512,128]{1,0:T(8,128)(2,1)S(1)}, u32[]{:S(2)}, u32[]{:S(2)}) %collective-permute-start.10) | collective-permute-done | bytes 131104 | tf_op jit(solution)/shard_map/ppermute | solution.py:25
  256.9 3.5 %collective-permute-done.9 = bf16[512,128]{1,0:T(8,128)(2,1)S(1)} collective-permute-done((bf16[512,128]{1,0:T(8,128)(2,1)S(1)}, bf16[512,128]{1,0:T(8,128)(2,1)S(1)}, u32[]{:S(2)}, u32[]{:S(2)}) %collective-permute-start.9) | collective-permute-done | bytes 131104 | tf_op jit(solution)/shard_map/ppermute | solution.py:25
  261.3 1.9 collective-permute-start.11
  263.3 1.9 collective-permute-start.12
  265.2 1.9 collective-permute-start.13
  267.1 4.5 %collective-permute-start.14 = (bf16[512,128]{1,0:T(8,128)(2,1)S(1)}, bf16[512,128]{1,0:T(8,128)(2,1)S(1)}, u32[]{:S(2)}, u32[]{:S(2)}) collective-permute-start(bf16[512,128]{1,0:T(8,128)(2,1)S(1)} %get-tuple-element.65), channel_id=1, source_target_pairs={{32,64},{40,72},{48,80},{56,88},{96,128},{104,136},{112,144},{120,... | collective-permute-start | bytes 393224 | tf_op jit(solution)/shard_map/ppermute | solution.py:150
  272.0 4.5 %collective-permute-done.12 = bf16[512,128]{1,0:T(8,128)(2,1)S(1)} collective-permute-done((bf16[512,128]{1,0:T(8,128)(2,1)S(1)}, bf16[512,128]{1,0:T(8,128)(2,1)S(1)}, u32[]{:S(2)}, u32[]{:S(2)}) %collective-permute-start.12) | collective-permute-done | bytes 131104 | tf_op jit(solution)/shard_map/ppermute | solution.py:150
  276.8 7.8 %collective-permute-done.14 = bf16[512,128]{1,0:T(8,128)(2,1)S(1)} collective-permute-done((bf16[512,128]{1,0:T(8,128)(2,1)S(1)}, bf16[512,128]{1,0:T(8,128)(2,1)S(1)}, u32[]{:S(2)}, u32[]{:S(2)}) %collective-permute-start.14) | collective-permute-done | bytes 131104 | tf_op jit(solution)/shard_map/ppermute | solution.py:150
  285.5 1.9 collective-permute-start.15
  287.5 6.7 %collective-permute-start.16 = (bf16[512,128]{1,0:T(8,128)(2,1)S(1)}, bf16[512,128]{1,0:T(8,128)(2,1)S(1)}, u32[]{:S(2)}, u32[]{:S(2)}) collective-permute-start(bf16[512,128]{1,0:T(8,128)(2,1)S(1)} %get-tuple-element.69), channel_id=1, source_target_pairs={{8,16},{24,32},{40,48},{56,64},{72,80},{88,96},{104,112},{120,128}... | collective-permute-start | bytes 393224 | tf_op jit(solution)/shard_map/ppermute | solution.py:150
  294.2 1.9 collective-permute-start.17
  296.1 1.9 collective-permute-start.18
  298.3 2.4 collective-permute-done.16
  301.0 0.9 collective-permute-done.17
  301.9 8.8 %collective-permute-done.18 = bf16[512,128]{1,0:T(8,128)(2,1)S(1)} collective-permute-done((bf16[512,128]{1,0:T(8,128)(2,1)S(1)}, bf16[512,128]{1,0:T(8,128)(2,1)S(1)}, u32[]{:S(2)}, u32[]{:S(2)}) %collective-permute-start.18) | collective-permute-done | bytes 131104 | tf_op jit(solution)/shard_map/ppermute | solution.py:150
  (104 shorter events, 16.0 us)
Async XLA Ops:
  0.1 2.8 copy-start.13
  0.1 3.0 copy-start
  12.9 41.3 %collective-permute-start = (bf16[16,7488]{1,0:T(8,128)(2,1)}, bf16[16,7488]{1,0:T(8,128)(2,1)S(1)}, u32[]{:S(2)}, u32[]{:S(2)}) collective-permute-start(bf16[16,7488]{1,0:T(8,128)(2,1)} %broadcast_select_fusion.6), channel_id=1, source_target_pairs={{0,4},{4,0},{1,5},{5,1},{2,6},{6,2},{3,7},{7,3},{8,12},{12,8},{9,1... | collective-permute-start | bytes 718856 | tf_op jit(solution)/shard_map/ppermute | solution.py:29
  32.0 55.7 %collective-permute-start.1 = (bf16[16,7488]{1,0:T(8,128)(2,1)}, bf16[16,7488]{1,0:T(8,128)(2,1)}, u32[]{:S(2)}, u32[]{:S(2)}) collective-permute-start(bf16[16,7488]{1,0:T(8,128)(2,1)} %broadcast_select_fusion.4), channel_id=1, source_target_pairs={{0,4},{4,0},{1,5},{5,1},{2,6},{6,2},{3,7},{7,3},{8,12},{12,8},{9,1... | collective-permute-start | bytes 718856 | tf_op jit(solution)/shard_map/ppermute | solution.py:29
  36.9 10.7 %copy-start.1 = (bf16[16,13824]{1,0:T(8,128)(2,1)S(1)}, bf16[16,13824]{1,0:T(8,128)(2,1)}, u32[]{:S(2)}) copy-start(bf16[16,13824]{1,0:T(8,128)(2,1)} %get-tuple-element.10) | copy-start | bytes 1327108
  37.2 55.6 %collective-permute-start.2 = (bf16[16,7488]{1,0:T(8,128)(2,1)S(1)}, bf16[16,7488]{1,0:T(8,128)(2,1)S(1)}, u32[]{:S(2)}, u32[]{:S(2)}) collective-permute-start(bf16[16,7488]{1,0:T(8,128)(2,1)S(1)} %broadcast_select_fusion.2), channel_id=1, source_target_pairs={{0,4},{4,0},{1,5},{5,1},{2,6},{6,2},{3,7},{7,3},{8,12},{12,8},{9,1... | collective-permute-start | bytes 718856 | tf_op jit(solution)/shard_map/ppermute | solution.py:29
  50.9 47.0 %collective-permute-start.3 = (bf16[16,7488]{1,0:T(8,128)(2,1)S(1)}, bf16[16,7488]{1,0:T(8,128)(2,1)S(1)}, u32[]{:S(2)}, u32[]{:S(2)}) collective-permute-start(bf16[16,7488]{1,0:T(8,128)(2,1)S(1)} %broadcast_select_fusion), channel_id=1, source_target_pairs={{0,4},{4,0},{1,5},{5,1},{2,6},{6,2},{3,7},{7,3},{8,12},{12,8},{9,1... | collective-permute-start | bytes 718856 | tf_op jit(solution)/shard_map/ppermute | solution.py:29
  55.3 43.7 %all-to-all-start = ((bf16[4,2,16,2304]{3,2,1,0:T(8,128)(2,1)}), bf16[4,2,16,2304]{3,2,1,0:T(8,128)(2,1)S(1)}, u32[]{:S(2)}, u32[]{:S(2)}) async-start(bf16[4,2,16,2304]{3,2,1,0:T(8,128)(2,1)} %pad_maximum_fusion), calls=%async_computation | async-start | bytes 1179648 | tf_op jit(solution)/shard_map/all_to_all | solution.py:127
  99.1 20.3 %copy-start.2 = (bf16[4,2,16,2304]{3,2,1,0:T(8,128)(2,1)}, bf16[4,2,16,2304]{3,2,1,0:T(8,128)(2,1)S(1)}, u32[]{:S(2)}) copy-start(bf16[4,2,16,2304]{3,2,1,0:T(8,128)(2,1)S(1)} %all-to-all-done) | copy-start | bytes 1769476
  99.1 13.0 %all-to-all-start.1 = ((bf16[4,2,16,2304]{3,2,1,0:T(8,128)(2,1)}), bf16[4,2,16,2304]{3,2,1,0:T(8,128)(2,1)S(1)}, u32[]{:S(2)}, u32[]{:S(2)}) async-start(bf16[4,2,16,2304]{3,2,1,0:T(8,128)(2,1)} %pad_maximum_fusion.1), calls=%async_computation.1 | async-start | bytes 1179648 | tf_op jit(solution)/shard_map/all_to_all | solution.py:127
  112.1 7.2 %copy-start.4 = (bf16[4,2,16,2304]{3,2,1,0:T(8,128)(2,1)}, bf16[4,2,16,2304]{3,2,1,0:T(8,128)(2,1)S(1)}, u32[]{:S(2)}) copy-start(bf16[4,2,16,2304]{3,2,1,0:T(8,128)(2,1)S(1)} %all-to-all-done.1) | copy-start | bytes 1769476
  112.1 13.7 %all-to-all-start.2 = ((bf16[4,2,16,2304]{3,2,1,0:T(8,128)(2,1)}), bf16[4,2,16,2304]{3,2,1,0:T(8,128)(2,1)}, u32[]{:S(2)}, u32[]{:S(2)}) async-start(bf16[4,2,16,2304]{3,2,1,0:T(8,128)(2,1)} %pad_maximum_fusion.2), calls=%async_computation.2 | async-start | bytes 1179648 | tf_op jit(solution)/shard_map/all_to_all | solution.py:127
  125.8 12.6 %all-to-all-start.3 = ((bf16[4,2,16,2304]{3,2,1,0:T(8,128)(2,1)}), bf16[4,2,16,2304]{3,2,1,0:T(8,128)(2,1)}, u32[]{:S(2)}, u32[]{:S(2)}) async-start(bf16[4,2,16,2304]{3,2,1,0:T(8,128)(2,1)} %pad_maximum_fusion.3), calls=%async_computation.3 | async-start | bytes 1179648 | tf_op jit(solution)/shard_map/all_to_all | solution.py:127
  138.4 2.1 copy-start.10
  138.4 2.1 copy-start.11
  138.4 2.1 copy-start.12
  140.6 2.8 copy-start.7
  140.6 2.9 copy-start.8
  143.6 2.8 copy-start.6
  146.4 1.1 copy-start.3
  146.4 1.2 copy-start.5
  146.5 1.2 copy-start.14
  150.2 10.6 %collective-permute-start.4 = (bf16[144,512]{1,0:T(8,128)(2,1)S(1)}, bf16[144,512]{1,0:T(8,128)(2,1)S(1)}, u32[]{:S(2)}, u32[]{:S(2)}) collective-permute-start(bf16[144,512]{1,0:T(8,128)(2,1)S(1)} %get-tuple-element.42), channel_id=1, source_target_pairs={{0,760},{8,0},{16,8},{24,16},{32,24},{40,32},{48,40},{56,48},{64,5... | collective-permute-start | bytes 442376 | tf_op jit(solution)/shard_map/ppermute | solution.py:25
  152.1 13.4 %collective-permute-start.5 = (bf16[144,512]{1,0:T(8,128)(2,1)S(1)}, bf16[144,512]{1,0:T(8,128)(2,1)S(1)}, u32[]{:S(2)}, u32[]{:S(2)}) collective-permute-start(bf16[144,512]{1,0:T(8,128)(2,1)S(1)} %get-tuple-element.43), channel_id=1, source_target_pairs={{0,736},{8,744},{16,752},{24,760},{32,0},{40,8},{48,16},{56,24},{6... | collective-permute-start | bytes 442376 | tf_op jit(solution)/shard_map/ppermute | solution.py:25
  189.0 25.5 %collective-permute-start.6 = (bf16[3,128,512]{2,1,0:T(8,128)(2,1)S(1)}, bf16[3,128,512]{2,1,0:T(8,128)(2,1)S(1)}, u32[]{:S(2)}, u32[]{:S(2)}) collective-permute-start(bf16[3,128,512]{2,1,0:T(8,128)(2,1)S(1)} %reduce_sum.61), channel_id=1, source_target_pairs={{0,4},{4,0},{1,5},{5,1},{2,6},{6,2},{3,7},{7,3},{8,12},{12,8},{9,1... | collective-permute-start | bytes 1179656 | tf_op jit(solution)/shard_map/ppermute | solution.py:29
  215.9 5.7 %copy-start.9 = (bf16[1,512,128]{2,1,0:T(8,128)(2,1)S(1)}, bf16[1,512,128]{2,1,0:T(8,128)(2,1)}, u32[]{:S(2)}) copy-start(bf16[1,512,128]{2,1,0:T(8,128)(2,1)} %param.8) | copy-start | bytes 393220
  215.9 24.5 %all-to-all-start.5 = ((bf16[4,3,128,512]{3,2,1,0:T(8,128)(2,1)}), bf16[4,3,128,512]{3,2,1,0:T(8,128)(2,1)S(1)}, u32[]{:S(2)}, u32[]{:S(2)}) async-start(bf16[4,3,128,512]{3,2,1,0:T(8,128)(2,1)} %broadcast_in_dim.37), calls=%async_computation.5 | async-start | bytes 3145728 | tf_op jit(solution)/shard_map/all_to_all | solution.py:218
  221.7 27.7 %collective-permute-start.7 = (bf16[512,128]{1,0:T(8,128)(2,1)S(1)}, bf16[512,128]{1,0:T(8,128)(2,1)S(1)}, u32[]{:S(2)}, u32[]{:S(2)}) collective-permute-start(bf16[512,128]{1,0:T(8,128)(2,1)S(1)} %bitcast.136), channel_id=1, source_target_pairs={{0,760},{8,0},{16,8},{24,16},{32,24},{40,32},{48,40},{56,48},{64,5... | collective-permute-start | bytes 393224 | tf_op jit(solution)/shard_map/ppermute | solution.py:25
  223.7 26.0 %collective-permute-start.8 = (bf16[512,128]{1,0:T(8,128)(2,1)S(1)}, bf16[512,128]{1,0:T(8,128)(2,1)S(1)}, u32[]{:S(2)}, u32[]{:S(2)}) collective-permute-start(bf16[512,128]{1,0:T(8,128)(2,1)S(1)} %bitcast.137), channel_id=1, source_target_pairs={{0,736},{8,744},{16,752},{24,760},{32,0},{40,8},{48,16},{56,24},{6... | collective-permute-start | bytes 393224 | tf_op jit(solution)/shard_map/ppermute | solution.py:25
  240.9 16.0 %collective-permute-start.10 = (bf16[512,128]{1,0:T(8,128)(2,1)S(1)}, bf16[512,128]{1,0:T(8,128)(2,1)S(1)}, u32[]{:S(2)}, u32[]{:S(2)}) collective-permute-start(bf16[512,128]{1,0:T(8,128)(2,1)S(1)} %convolution_convert_fusion.4), channel_id=1, source_target_pairs={{0,32},{8,40},{16,48},{24,56},{32,64},{40,72},{48,80},{56,88},{64,... | collective-permute-start | bytes 393224 | tf_op jit(solution)/shard_map/ppermute | solution.py:25
  247.1 13.2 %collective-permute-start.9 = (bf16[512,128]{1,0:T(8,128)(2,1)S(1)}, bf16[512,128]{1,0:T(8,128)(2,1)S(1)}, u32[]{:S(2)}, u32[]{:S(2)}) collective-permute-start(bf16[512,128]{1,0:T(8,128)(2,1)S(1)} %convolution_convert_fusion.5), channel_id=1, source_target_pairs={{0,8},{8,16},{16,24},{24,32},{32,40},{40,48},{48,56},{56,64},{64,7... | collective-permute-start | bytes 393224 | tf_op jit(solution)/shard_map/ppermute | solution.py:25
  261.3 10.6 %collective-permute-start.11 = (bf16[512,128]{1,0:T(8,128)(2,1)S(1)}, bf16[512,128]{1,0:T(8,128)(2,1)S(1)}, u32[]{:S(2)}, u32[]{:S(2)}) collective-permute-start(bf16[512,128]{1,0:T(8,128)(2,1)S(1)} %get-tuple-element.70), channel_id=1, source_target_pairs={{0,8},{16,24},{32,40},{48,56},{64,72},{80,88},{96,104},{112,120},{... | collective-permute-start | bytes 393224 | tf_op jit(solution)/shard_map/ppermute | solution.py:150
  263.3 13.2 %collective-permute-start.12 = (bf16[512,128]{1,0:T(8,128)(2,1)S(1)}, bf16[512,128]{1,0:T(8,128)(2,1)S(1)}, u32[]{:S(2)}, u32[]{:S(2)}) collective-permute-start(bf16[512,128]{1,0:T(8,128)(2,1)S(1)} %get-tuple-element.71), channel_id=1, source_target_pairs={{8,16},{24,32},{40,48},{56,64},{72,80},{88,96},{104,112},{120,128}... | collective-permute-start | bytes 393224 | tf_op jit(solution)/shard_map/ppermute | solution.py:150
  265.2 11.6 %collective-permute-start.13 = (bf16[512,128]{1,0:T(8,128)(2,1)S(1)}, bf16[512,128]{1,0:T(8,128)(2,1)S(1)}, u32[]{:S(2)}, u32[]{:S(2)}) collective-permute-start(bf16[512,128]{1,0:T(8,128)(2,1)S(1)} %get-tuple-element.64), channel_id=1, source_target_pairs={{0,32},{8,40},{16,48},{24,56},{64,96},{72,104},{80,112},{88,120},{... | collective-permute-start | bytes 393224 | tf_op jit(solution)/shard_map/ppermute | solution.py:150
  267.1 17.4 %collective-permute-start.14 = (bf16[512,128]{1,0:T(8,128)(2,1)S(1)}, bf16[512,128]{1,0:T(8,128)(2,1)S(1)}, u32[]{:S(2)}, u32[]{:S(2)}) collective-permute-start(bf16[512,128]{1,0:T(8,128)(2,1)S(1)} %get-tuple-element.65), channel_id=1, source_target_pairs={{32,64},{40,72},{48,80},{56,88},{96,128},{104,136},{112,144},{120,... | collective-permute-start | bytes 393224 | tf_op jit(solution)/shard_map/ppermute | solution.py:150
  285.5 12.8 %collective-permute-start.15 = (bf16[512,128]{1,0:T(8,128)(2,1)S(1)}, bf16[512,128]{1,0:T(8,128)(2,1)S(1)}, u32[]{:S(2)}, u32[]{:S(2)}) collective-permute-start(bf16[512,128]{1,0:T(8,128)(2,1)S(1)} %get-tuple-element.68), channel_id=1, source_target_pairs={{0,8},{16,24},{32,40},{48,56},{64,72},{80,88},{96,104},{112,120},{... | collective-permute-start | bytes 393224 | tf_op jit(solution)/shard_map/ppermute | solution.py:150
  287.5 13.2 %collective-permute-start.16 = (bf16[512,128]{1,0:T(8,128)(2,1)S(1)}, bf16[512,128]{1,0:T(8,128)(2,1)S(1)}, u32[]{:S(2)}, u32[]{:S(2)}) collective-permute-start(bf16[512,128]{1,0:T(8,128)(2,1)S(1)} %get-tuple-element.69), channel_id=1, source_target_pairs={{8,16},{24,32},{40,48},{56,64},{72,80},{88,96},{104,112},{120,128}... | collective-permute-start | bytes 393224 | tf_op jit(solution)/shard_map/ppermute | solution.py:150
  294.2 7.8 %collective-permute-start.17 = (bf16[512,128]{1,0:T(8,128)(2,1)S(1)}, bf16[512,128]{1,0:T(8,128)(2,1)S(1)}, u32[]{:S(2)}, u32[]{:S(2)}) collective-permute-start(bf16[512,128]{1,0:T(8,128)(2,1)S(1)} %get-tuple-element.60), channel_id=1, source_target_pairs={{0,32},{8,40},{16,48},{24,56},{64,96},{72,104},{80,112},{88,120},{... | collective-permute-start | bytes 393224 | tf_op jit(solution)/shard_map/ppermute | solution.py:150
  296.1 14.7 %collective-permute-start.18 = (bf16[512,128]{1,0:T(8,128)(2,1)S(1)}, bf16[512,128]{1,0:T(8,128)(2,1)S(1)}, u32[]{:S(2)}, u32[]{:S(2)}) collective-permute-start(bf16[512,128]{1,0:T(8,128)(2,1)S(1)} %get-tuple-element.61), channel_id=1, source_target_pairs={{32,64},{40,72},{48,80},{56,88},{96,128},{104,136},{112,144},{120,... | collective-permute-start | bytes 393224 | tf_op jit(solution)/shard_map/ppermute | solution.py:150

commit v3 on v2

v3 whole, which is shorter than its diff:
```python
import jax
import jax.numpy as jnp
import numpy as np
from jax import lax
from jax.sharding import Mesh, PartitionSpec as P

P_SIZE = 24
PLANE = P_SIZE * P_SIZE
G = 13824
EB = 4
HALVES = 2
SLABS = 4
CHUNKS = 4
BOTH = ("half", "slab")

LOW_EDGE = 4.0
HIGH_EDGE = 14.0
SHIFT_CENTER = 4.0
HALF_WIDTH = 6.0
MIDDLE = 0.5 * (HIGH_EDGE + LOW_EDGE)
SPREAD = 0.5 * (HIGH_EDGE - LOW_EDGE)


def from_behind(value, axis, by):
    devices = lax.axis_size(axis)
    return lax.ppermute(value, axis, [(i, (i + by) % devices) for i in range(devices)])


def swap_halves(value):
    return lax.ppermute(value, "half", [(0, 1), (1, 0)])


def side_masks(length):
    where = jnp.arange(length, dtype=jnp.int32)
    zpos = where % P_SIZE
    ypos = where // P_SIZE % P_SIZE
    return (
        (zpos < P_SIZE - 1).astype(jnp.float32),
        (zpos > 0).astype(jnp.float32),
        (ypos < P_SIZE - 1).astype(jnp.float32),
        (ypos > 0).astype(jnp.float32),
    )


def flat_hamiltonian(padded, length, potential, masks):
    values = padded[:, PLANE : PLANE + length]
    beside = padded[:, 2 * PLANE : 2 * PLANE + length] + padded[:, 0:length]
    beside = beside + masks[0] * padded[:, PLANE + 1 : PLANE + 1 + length]
    beside = beside + masks[1] * padded[:, PLANE - 1 : PLANE - 1 + length]
    beside = beside + masks[2] * padded[:, PLANE + P_SIZE : PLANE + P_SIZE + length]
    beside = beside + masks[3] * padded[:, PLANE - P_SIZE : PLANE - P_SIZE + length]
    return 6.0 * values - beside + potential * values


def whole_hamiltonian(values, potential, masks):
    padded = jnp.pad(values, ((0, 0), (PLANE, PLANE)))
    return flat_hamiltonian(padded, values.shape[1], potential, masks)


def filtered_basis(orbitals, potential, kept_count, start_index):
    orbital_count = orbitals.shape[0]
    masks = side_masks(G)
    previous = orbitals.astype(jnp.float32)
    current = (whole_hamiltonian(previous, potential, masks) - MIDDLE * previous) / SPREAD
    current = (
        2.0 * (whole_hamiltonian(current, potential, masks) - MIDDLE * current) / SPREAD - previous
    )
    magnitude = jnp.sqrt(jnp.mean(current * current, axis=1, keepdims=True) + 1e-06)
    active = start_index + jnp.arange(orbital_count, dtype=jnp.int32) < kept_count
    return jnp.where(active[:, None], current / magnitude, 0.0).astype(jnp.bfloat16)


def face_selector(planes):
    grid = np.arange(planes * PLANE, dtype=np.int32).reshape(planes, P_SIZE, P_SIZE)
    last = P_SIZE - 1
    groups = [
        grid[:, :, 0], grid[:, :, 1], grid[:, 0, :], grid[:, 1, :],
        grid[:, :, last - 1], grid[:, :, last], grid[:, last - 1, :], grid[:, last, :],
    ]
    chosen = jnp.asarray(np.concatenate([g.reshape(-1) for g in groups]))
    points = jnp.arange(planes * PLANE, dtype=jnp.int32)
    return (chosen[:, None] == points[None, :]).astype(jnp.bfloat16)


def transposed_dot(a, b, contract_a, contract_b):
    return lax.dot_general(
        a, b, (((contract_a,), (contract_b,)), ((), ())), preferred_element_type=jnp.float32
    )


def owned_basis(orbitals, potential, kept_count, start_index):
    step = orbitals.shape[0] // CHUNKS
    chunks = []
    tied = None
    for chunk in range(CHUNKS):
        source = orbitals[chunk * step : (chunk + 1) * step]
        if tied is not None:
            source, tied = lax.optimization_barrier((source, tied))
            chunks[-1] = tied
        tied = filtered_basis(source, potential, kept_count, start_index + chunk * step)
        chunks.append(tied)
    return chunks


def slab_rows(chunks, length):
    slabs = [
        jnp.concatenate([c[:, s * length : (s + 1) * length] for c in chunks])
        for s in range(HALVES * SLABS)
    ]
    rows = lax.all_to_all(jnp.stack(slabs), BOTH, 0, 0, tiled=True)
    return rows.reshape(-1, length)


def pair_swap(value, by, odd):
    devices = lax.axis_size("elem")
    low = [i for i in range(devices) if (i // by) % 2 == odd]
    pairs = [(i, (i + by) % devices) for i in low]
    return lax.ppermute(value, "elem", pairs + [(j, i) for i, j in pairs])


def exchange(value, product, by):
    even = (lax.axis_index("elem") // by) % 2 == 0
    from_odd = pair_swap(jnp.where(even, value, product), by, 1)
    from_even = pair_swap(jnp.where(even, product, value), by, 0)
    ahead = jnp.where(even, from_even, from_odd)
    behind = jnp.where(even, from_odd, from_even)
    return ahead, behind


def scaled(blocks, current, given=None):
    h_self, h_z, h_y = blocks
    back_z = transposed_dot(h_z, current, 0, 0).astype(jnp.bfloat16)
    back_y = transposed_dot(h_y, current, 0, 0).astype(jnp.bfloat16)
    if given is None:
        ahead_z, behind_z = exchange(current, back_z, 1)
        ahead_y, behind_y = exchange(current, back_y, EB)
        running = transposed_dot(h_self, current, 1, 0)
    else:
        ahead_z, ahead_y, running = given
        behind_z = from_behind(back_z, "elem", 1)
        behind_y = from_behind(back_y, "elem", EB)
    running = running + transposed_dot(h_z, ahead_z, 1, 0)
    running = running + transposed_dot(h_y, ahead_y, 1, 0)
    running = running + behind_z.astype(jnp.float32) + behind_y.astype(jnp.float32)
    return (running - SHIFT_CENTER * current.astype(jnp.float32)) / HALF_WIDTH


def slices_of(partial):
    count, total, columns = partial.shape
    return partial.reshape(count, SLABS, total // SLABS, columns).swapaxes(0, 1)


def sum_over_slabs(partial):
    pieces = lax.all_to_all(slices_of(partial), "slab", 0, 0, tiled=True)
    return jnp.sum(pieces.astype(jnp.float32), axis=0).astype(jnp.bfloat16)


def sum_over_halves(summed):
    swapped = swap_halves(summed)
    return (summed.astype(jnp.float32) + swapped.astype(jnp.float32)).astype(jnp.bfloat16)


def gather_slices(summed):
    count, rows, columns = summed.shape
    copies = jnp.broadcast_to(summed[None], (SLABS,) + summed.shape)
    blocks = lax.all_to_all(copies, "slab", 0, 0, tiled=True)
    return [blocks[:, i].reshape(SLABS * rows, columns) for i in range(count)]


def device_body(orbitals, potential, basis_count, states):
    half = lax.axis_index("half")
    slab = lax.axis_index("slab")
    band = half * SLABS + slab
    length = G // (HALVES * SLABS)
    planes = length // PLANE
    slab_potential = lax.dynamic_slice_in_dim(potential[0], band * length, length, 0)

    start = states[0]
    ahead_z = from_behind(start, "elem", -1)
    ahead_y = from_behind(start, "elem", -EB)
    ahead = lax.optimization_barrier(jnp.concatenate([ahead_z, ahead_y]))
    ahead_z, ahead_y = ahead[: ahead.shape[0] // 2], ahead[ahead.shape[0] // 2 :]

    chunks = owned_basis(
        orbitals[0], potential[0], basis_count[0], band * orbitals.shape[1]
    )
    rows = slab_rows(chunks, length)

    above = lax.ppermute(
        rows[:, :PLANE], BOTH, [(i + 1, i) for i in range(HALVES * SLABS - 1)]
    )
    faces = transposed_dot(face_selector(planes), rows, 1, 1).astype(jnp.bfloat16)
    width = 2 * planes * P_SIZE
    other_z = from_behind(faces[:width], "elem", -1)
    other_y = from_behind(faces[width : 2 * width], "elem", -EB)

    padded = jnp.pad(rows.astype(jnp.float32), ((0, 0), (PLANE, PLANE)))
    applied = flat_hamiltonian(padded, length, slab_potential, side_masks(length))
    last = rows[:, length - PLANE :]
    h_self = transposed_dot(rows, applied.astype(jnp.bfloat16), 1, 1)
    h_self = h_self - transposed_dot(last, above, 1, 1) - transposed_dot(above, last, 1, 1)
    weight = -0.5 / PLANE
    h_z = transposed_dot(faces[2 * width : 3 * width], other_z, 0, 0) * weight
    h_y = transposed_dot(faces[3 * width :], other_y, 0, 0) * weight

    summed_self = sum_over_slabs((h_self * (1.0 / G)).astype(jnp.bfloat16)[None])
    whole_self = sum_over_halves(summed_self)
    summed_faces = sum_over_slabs(jnp.stack([h_z, h_y]).astype(jnp.bfloat16))
    whole_faces = sum_over_halves(summed_faces)
    (block_self,) = gather_slices(whole_self)
    running = transposed_dot(block_self, start, 1, 0)
    block_z, block_y = gather_slices(whole_faces)
    blocks = (block_self, block_z, block_y)

    first = scaled(blocks, start, (ahead_z, ahead_y, running)).astype(jnp.bfloat16)
    second = (2.0 * scaled(blocks, first) - start.astype(jnp.float32)).astype(jnp.bfloat16)
    third = 2.0 * scaled(blocks, second) - first.astype(jnp.float32)
    magnitude = jnp.sqrt(jnp.mean(third * third, axis=0, keepdims=True) + 1e-06)
    return (third / magnitude).astype(jnp.bfloat16)[None]


def solution(mesh):
    elems, bands = mesh.devices.shape
    inner = Mesh(mesh.devices.reshape(elems, HALVES, bands // HALVES), ("elem", "half", "slab"))
    placed = (P("elem", BOTH, None), P("elem", None), P("elem"), P("elem", None, BOTH))
    return jax.shard_map(
        device_body, mesh=inner, in_specs=placed, out_specs=P("elem", None, BOTH), check_vma=False
    )
```

time: 314 us -> 282 us (0.90)
  waiting for transfers between devices: 119 us -> 69.9 us
  starting transfers between devices: 111 us -> 160 us
  blocking collectives: 22.6 us -> 0 us
  other arithmetic: 43.4 us -> 29.4 us
  matrix products: 10.6 us -> 16.1 us
    ppermute x5 -> x2, waiting for transfers between devices: 56.2 us -> 5.21 us  [swap_halves(): return lax.ppermute(value, 'half', [(0, 1), (1, 0)])]
    ppermute x6, starting transfers between devices: 25.5 us -> 56.2 us  [from_behind(): lax.ppermute(value, axis, [(i, (i + by) % devices) for i in range(devices)])]
    all_to_all x1 -> x0, blocking collectives: 22.6 us -> none  [device_body(): pieces = lax.all_to_all(partial, 'slab', 0, 0, tiled=True)]
    ppermute x8, starting transfers between devices: 22.7 us -> 39.1 us  [pair_swap(): return lax.ppermute(value, 'elem', pairs + [(j, i) for i, j in pairs])]
    all_to_all x5, waiting for transfers between devices: 23.9 us -> 39.7 us  [the longest x1 29.9 us: slab_rows(): rows = lax.all_to_all(jnp.stack(slabs), BOTH, 0, 0, tiled=True)]
    ppermute x8, waiting for transfers between devices: 24.4 us -> 8.82 us  [pair_swap(): return lax.ppermute(value, 'elem', pairs + [(j, i) for i, j in pairs])]
    all_to_all x5, starting transfers between devices: 30.9 us -> 39.1 us  [the longest x1 17.4 us: slab_rows(): rows = lax.all_to_all(jnp.stack(slabs), BOTH, 0, 0, tiled=True)]
    ppermute x5 -> x2, starting transfers between devices: 31.8 us -> 24.1 us  [swap_halves(): return lax.ppermute(value, 'half', [(0, 1), (1, 0)])]
  transfers between devices with their start and end apart: 24 -> 22, of which waited for: 16 -> 12; matrix products, arithmetic and copies ran while one was open for 9% -> 6% of each run, Pallas kernels for 0% -> 0%
where the time goes in v3:
time: 282 us; the launch traced here: 280 us
  starting transfers between devices  160 us (57%)
  waiting for transfers between devices  69.9 us (25%)
  other arithmetic  29.4 us (10%)
  matrix products  16.1 us (6%)
  local copies, waits for them, and re-layouts  3.16 us (1%)
    ppermute x6, starting transfers between devices, from_behind(): lax.ppermute(value, axis, [(i, (i + by) % devices) for i in range(devices)])  56.2 us
    ppermute x8, starting transfers between devices, pair_swap(): return lax.ppermute(value, 'elem', pairs + [(j, i) for i, j in pairs])  39.1 us
    all_to_all x1, waiting for transfers between devices, slab_rows(): rows = lax.all_to_all(jnp.stack(slabs), BOTH, 0, 0, tiled=True)  29.9 us
    ppermute x2, starting transfers between devices, swap_halves(): return lax.ppermute(value, 'half', [(0, 1), (1, 0)])  24.1 us
    all_to_all x1, starting transfers between devices, slab_rows(): rows = lax.all_to_all(jnp.stack(slabs), BOTH, 0, 0, tiled=True)  17.4 us
    ppermute x6, waiting for transfers between devices, from_behind(): lax.ppermute(value, axis, [(i, (i + by) % devices) for i in range(devices)])  16.2 us
    dot_general x21, matrix products, transposed_dot(): lax.dot_general(a, b, (((contract_a,), (contract_b,)), ((), ())), preferr...  16.1 us
    all_to_all x2, starting transfers between devices, gather_slices(): blocks = lax.all_to_all(copies, 'slab', 0, 0, tiled=True)  11.6 us
  transfers between devices with their start and end apart: 22, of which 12 were waited for; matrix products, arithmetic and copies ran while one was open for 6% of the time, Pallas kernels for 0%

profile of v3, /device:TPU:6, one launch (start us, length us, event | category | flops | bytes accessed | tf_op | source)
XLA Modules:
  0.0 280.3 jit_solution(7519729970492574600)
XLA Ops:
  0.1 2.6 bitcast_convert_fusion
  2.9 4.7 %broadcast_multiply_fusion.3 = (f32[16,13824]{1,0:T(8,128)S(1)}, f32[16,13824]{1,0:T(8,128)S(1)}) fusion(f32[13824]{0:T(1024)S(1)} %reduce.3, f32[13824]{0:T(1024)S(1)} %get-tuple-element.89, f32[13824]{0:T(1024)S(1)} %get-tuple-element.90, f32[13824]{0:T(1024)S(1)} %get-tuple-element.88, f32[13824]{0:T(1024)S(1)} %get-tuple-element.87, ...), kind=kLoop, calls=%fused_computation.147 | loop fusion | flops 3760128 | bytes 3373056 | tf_op jit(solution)/shard_map/div | solution.py:64
  7.6 2.5 multiply_reduce_fusion.3
  10.8 1.3 select_convert_fusion.3
  12.2 1.4 broadcast_multiply_fusion.2
  13.6 1.5 multiply_reduce_fusion.2
  15.4 1.4 broadcast_multiply_fusion.1
  16.8 1.5 multiply_reduce_fusion.1
  18.6 1.4 broadcast_multiply_fusion
  20.1 1.5 multiply_reduce_fusion
  22.5 0.7 fusion.72
  23.2 0.7 fusion.73
  23.9 0.7 fusion.74
  24.7 0.7 fusion.75
  25.4 0.7 fusion.76
  26.1 0.7 fusion.77
  26.8 0.7 fusion.78
  27.5 0.7 fusion.79
  28.3 17.4 %all-to-all-start = ((bf16[8,64,1728]{2,1,0:T(8,128)(2,1)}), bf16[8,64,1728]{2,1,0:T(8,128)(2,1)S(1)}, u32[]{:S(2)}, u32[]{:S(2)}) async-start(bf16[8,64,1728]{2,1,0:T(8,128)(2,1)} %fusion.79), calls=%async_computation | async-start | bytes 3670016 | tf_op jit(solution)/shard_map/all_to_all | solution.py:110
  45.9 29.9 %all-to-all-done = bf16[8,64,1728]{2,1,0:T(8,128)(2,1)S(1)} async-done(((bf16[8,64,1728]{2,1,0:T(8,128)(2,1)}), bf16[8,64,1728]{2,1,0:T(8,128)(2,1)S(1)}, u32[]{:S(2)}, u32[]{:S(2)}) %all-to-all-start) | async-done | bytes 1769504 | tf_op jit(solution)/shard_map/all_to_all | solution.py:110
  76.0 2.0 collective-permute-start
  78.0 1.3 fusion.17
  79.3 45.4 %collective-permute-start.3 = (bf16[144,512]{1,0:T(8,128)(2,1)S(1)}, bf16[144,512]{1,0:T(8,128)(2,1)}, u32[]{:S(2)}, u32[]{:S(2)}) collective-permute-start(bf16[144,512]{1,0:T(8,128)(2,1)S(1)} %get-tuple-element.40), channel_id=1, source_target_pairs={{0,736},{8,744},{16,752},{24,760},{32,0},{40,8},{48,16},{56,24},{6... | collective-permute-start | bytes 442376 | tf_op jit(solution)/shard_map/ppermute | solution.py:26
  124.7 1.9 collective-permute-start.2
  126.7 0.4 bitcast_convert_fusion.1
  127.1 5.5 %fusion.14 = f32[512,512]{1,0:T(8,128)S(1)} fusion(bf16[512,1728]{1,0:T(8,128)(2,1)S(1)} %bitcast.114, f32[512,1728]{1,0:T(8,128)S(1)} %bitcast_convert_fusion.1, f32[1728]{0:T(1024)S(1)} %dynamic-slice_reduce_fusion, f32[1728]{0:T(1024)S(1)} %get-tuple-element.97, f32[1728]{0:T(1024)S(1)} %get-tuple-element.98, f32[1728]{0:T(1024)S(1)} %get-tuple-element.96, ...), kind=kOutput, calls=%fused_computation.21 | convolution fusion | flops 918355968 | bytes 6391552 | tf_op jit(solution)/shard_map/dot_general | solution.py:86
  132.6 0.6 convolution_subtract_fusion.1
  133.2 1.4 fusion.20
  134.6 4.5 %all-to-all-start.1 = ((bf16[4,1,128,512]{3,2,1,0:T(8,128)(2,1)}), bf16[4,1,128,512]{3,2,1,0:T(8,128)(2,1)S(1)}, u32[]{:S(2)}, u32[]{:S(2)}) async-start(bf16[4,1,128,512]{3,2,1,0:T(8,128)(2,1)} %bitcast.16), calls=%async_computation.1 | async-start | bytes 1048576 | tf_op jit(solution)/shard_map/all_to_all | solution.py:154
  139.1 1.2 fusion.19
  140.4 1.2 fusion.18
  141.6 1.1 maximum_bitcast_fusion
  142.7 4.4 %all-to-all-done.1 = bf16[4,1,128,512]{3,2,1,0:T(8,128)(2,1)S(1)} async-done(((bf16[4,1,128,512]{3,2,1,0:T(8,128)(2,1)}), bf16[4,1,128,512]{3,2,1,0:T(8,128)(2,1)S(1)}, u32[]{:S(2)}, u32[]{:S(2)}) %all-to-all-start.1) | async-done | bytes 524320 | tf_op jit(solution)/shard_map/all_to_all | solution.py:154
  147.2 5.6 %all-to-all-start.3 = ((bf16[4,2,128,512]{3,2,1,0:T(8,128)(2,1)}), bf16[4,2,128,512]{3,2,1,0:T(8,128)(2,1)S(1)}, u32[]{:S(2)}, u32[]{:S(2)}) async-start(bf16[4,2,128,512]{3,2,1,0:T(8,128)(2,1)} %maximum_bitcast_fusion), calls=%async_computation.3 | async-start | bytes 2097152 | tf_op jit(solution)/shard_map/all_to_all | solution.py:154
  152.8 11.9 %collective-permute-start.1 = (bf16[1,128,512]{2,1,0:T(8,128)(2,1)S(1)}, bf16[1,128,512]{2,1,0:T(8,128)(2,1)S(1)}, u32[]{:S(2)}, u32[]{:S(2)}) collective-permute-start(bf16[1,128,512]{2,1,0:T(8,128)(2,1)S(1)} %bitcast.128), channel_id=1, source_target_pairs={{0,4},{4,0},{1,5},{5,1},{2,6},{6,2},{3,7},{7,3},{8,12},{12,8},{9,1... | collective-permute-start | bytes 393224 | tf_op jit(solution)/shard_map/ppermute | solution.py:30
  164.7 0.8 all-to-all-done.3
  165.8 12.2 %collective-permute-start.4 = (bf16[2,128,512]{2,1,0:T(8,128)(2,1)S(1)}, bf16[2,128,512]{2,1,0:T(8,128)(2,1)S(1)}, u32[]{:S(2)}, u32[]{:S(2)}) collective-permute-start(bf16[2,128,512]{2,1,0:T(8,128)(2,1)S(1)} %reduce_sum.77), channel_id=1, source_target_pairs={{0,4},{4,0},{1,5},{5,1},{2,6},{6,2},{3,7},{7,3},{8,12},{12,8},{9,1... | collective-permute-start | bytes 786440 | tf_op jit(solution)/shard_map/ppermute | solution.py:30
  178.1 0.9 broadcast_in_dim.44
  178.9 5.5 %all-to-all-start.2 = ((bf16[4,1,128,512]{3,2,1,0:T(8,128)(2,1)}), bf16[4,1,128,512]{3,2,1,0:T(8,128)(2,1)S(1)}, u32[]{:S(2)}, u32[]{:S(2)}) async-start(bf16[4,1,128,512]{3,2,1,0:T(8,128)(2,1)} %broadcast_in_dim.44), calls=%async_computation.2 | async-start | bytes 1048576 | tf_op jit(solution)/shard_map/all_to_all | solution.py:166
  184.4 5.2 %collective-permute-done.4 = bf16[2,128,512]{2,1,0:T(8,128)(2,1)S(1)} collective-permute-done((bf16[2,128,512]{2,1,0:T(8,128)(2,1)S(1)}, bf16[2,128,512]{2,1,0:T(8,128)(2,1)S(1)}, u32[]{:S(2)}, u32[]{:S(2)}) %collective-permute-start.4) | collective-permute-done | bytes 262176 | tf_op jit(solution)/shard_map/ppermute | solution.py:30
  189.7 1.1 all-to-all-done.2
  190.8 1.1 broadcast_in_dim.45
  191.9 6.1 %all-to-all-start.4 = ((bf16[4,2,128,512]{3,2,1,0:T(8,128)(2,1)}), bf16[4,2,128,512]{3,2,1,0:T(8,128)(2,1)S(1)}, u32[]{:S(2)}, u32[]{:S(2)}) async-start(bf16[4,2,128,512]{3,2,1,0:T(8,128)(2,1)} %broadcast_in_dim.45), calls=%async_computation.4 | async-start | bytes 2097152 | tf_op jit(solution)/shard_map/all_to_all | solution.py:166
  198.0 2.9 %collective-permute-start.6 = (bf16[512,128]{1,0:T(8,128)(2,1)S(1)}, bf16[512,128]{1,0:T(8,128)(2,1)S(1)}, u32[]{:S(2)}, u32[]{:S(2)}) collective-permute-start(bf16[512,128]{1,0:T(8,128)(2,1)S(1)} %bitcast.126), channel_id=1, source_target_pairs={{0,736},{8,744},{16,752},{24,760},{32,0},{40,8},{48,16},{56,24},{6... | collective-permute-start | bytes 393224 | tf_op jit(solution)/shard_map/ppermute | solution.py:26
  200.9 1.9 collective-permute-start.5
  202.9 3.9 %collective-permute-done.6 = bf16[512,128]{1,0:T(8,128)(2,1)S(1)} collective-permute-done((bf16[512,128]{1,0:T(8,128)(2,1)S(1)}, bf16[512,128]{1,0:T(8,128)(2,1)S(1)}, u32[]{:S(2)}, u32[]{:S(2)}) %collective-permute-start.6) | collective-permute-done | bytes 131104 | tf_op jit(solution)/shard_map/ppermute | solution.py:26
  207.1 3.5 %all-to-all-done.4 = bf16[4,2,128,512]{3,2,1,0:T(8,128)(2,1)S(1)} async-done(((bf16[4,2,128,512]{3,2,1,0:T(8,128)(2,1)}), bf16[4,2,128,512]{3,2,1,0:T(8,128)(2,1)S(1)}, u32[]{:S(2)}, u32[]{:S(2)}) %all-to-all-start.4) | async-done | bytes 1048608 | tf_op jit(solution)/shard_map/all_to_all | solution.py:166
  211.0 1.9 collective-permute-start.8
  213.3 2.1 collective-permute-start.7
  215.8 11.8 %collective-permute-done.8 = bf16[512,128]{1,0:T(8,128)(2,1)S(1)} collective-permute-done((bf16[512,128]{1,0:T(8,128)(2,1)S(1)}, bf16[512,128]{1,0:T(8,128)(2,1)S(1)}, u32[]{:S(2)}, u32[]{:S(2)}) %collective-permute-start.8) | collective-permute-done | bytes 131104 | tf_op jit(solution)/shard_map/ppermute | solution.py:26
  227.5 0.4 collective-permute-done.7
  228.7 0.4 broadcast_select_fusion.3
  229.0 1.9 collective-permute-start.9
  230.9 3.0 %collective-permute-start.10 = (bf16[512,128]{1,0:T(8,128)(2,1)S(1)}, bf16[512,128]{1,0:T(8,128)(2,1)S(1)}, u32[]{:S(2)}, u32[]{:S(2)}) collective-permute-start(bf16[512,128]{1,0:T(8,128)(2,1)S(1)} %get-tuple-element.84), channel_id=1, source_target_pairs={{8,16},{24,32},{40,48},{56,64},{72,80},{88,96},{104,112},{120,128}... | collective-permute-start | bytes 393224 | tf_op jit(solution)/shard_map/ppermute | solution.py:118
  234.0 2.8 collective-permute-start.12
  236.7 9.5 %collective-permute-start.11 = (bf16[512,128]{1,0:T(8,128)(2,1)S(1)}, bf16[512,128]{1,0:T(8,128)(2,1)S(1)}, u32[]{:S(2)}, u32[]{:S(2)}) collective-permute-start(bf16[512,128]{1,0:T(8,128)(2,1)S(1)} %get-tuple-element.77), channel_id=1, source_target_pairs={{0,32},{8,40},{16,48},{24,56},{64,96},{72,104},{80,112},{88,120},{... | collective-permute-start | bytes 393224 | tf_op jit(solution)/shard_map/ppermute | solution.py:118
  246.8 3.9 %collective-permute-done.12 = bf16[512,128]{1,0:T(8,128)(2,1)S(1)} collective-permute-done((bf16[512,128]{1,0:T(8,128)(2,1)S(1)}, bf16[512,128]{1,0:T(8,128)(2,1)S(1)}, u32[]{:S(2)}, u32[]{:S(2)}) %collective-permute-start.12) | collective-permute-done | bytes 131104 | tf_op jit(solution)/shard_map/ppermute | solution.py:118
  250.8 1.1 collective-permute-done.11
  252.9 7.7 %collective-permute-start.16 = (bf16[512,128]{1,0:T(8,128)(2,1)S(1)}, bf16[512,128]{1,0:T(8,128)(2,1)S(1)}, u32[]{:S(2)}, u32[]{:S(2)}) collective-permute-start(bf16[512,128]{1,0:T(8,128)(2,1)S(1)} %get-tuple-element.74), channel_id=1, source_target_pairs={{32,64},{40,72},{48,80},{56,88},{96,128},{104,136},{112,144},{120,... | collective-permute-start | bytes 393224 | tf_op jit(solution)/shard_map/ppermute | solution.py:118
  260.6 5.1 %collective-permute-start.15 = (bf16[512,128]{1,0:T(8,128)(2,1)S(1)}, bf16[512,128]{1,0:T(8,128)(2,1)S(1)}, u32[]{:S(2)}, u32[]{:S(2)}) collective-permute-start(bf16[512,128]{1,0:T(8,128)(2,1)S(1)} %get-tuple-element.73), channel_id=1, source_target_pairs={{0,32},{8,40},{16,48},{24,56},{64,96},{72,104},{80,112},{88,120},{... | collective-permute-start | bytes 393224 | tf_op jit(solution)/shard_map/ppermute | solution.py:118
  265.7 7.2 %collective-permute-start.14 = (bf16[512,128]{1,0:T(8,128)(2,1)S(1)}, bf16[512,128]{1,0:T(8,128)(2,1)S(1)}, u32[]{:S(2)}, u32[]{:S(2)}) collective-permute-start(bf16[512,128]{1,0:T(8,128)(2,1)S(1)} %get-tuple-element.82), channel_id=1, source_target_pairs={{8,16},{24,32},{40,48},{56,64},{72,80},{88,96},{104,112},{120,128}... | collective-permute-start | bytes 393224 | tf_op jit(solution)/shard_map/ppermute | solution.py:118
  272.9 1.9 collective-permute-start.13
  275.2 3.8 %collective-permute-done.14 = bf16[512,128]{1,0:T(8,128)(2,1)S(1)} collective-permute-done((bf16[512,128]{1,0:T(8,128)(2,1)S(1)}, bf16[512,128]{1,0:T(8,128)(2,1)S(1)}, u32[]{:S(2)}, u32[]{:S(2)}) %collective-permute-start.14) | collective-permute-done | bytes 131104 | tf_op jit(solution)/shard_map/ppermute | solution.py:118
  279.6 0.7 fusion.89
  (65 shorter events, 7.1 us)
Async XLA Ops:
  0.1 2.6 copy-start.2
  0.1 2.8 copy-start
  28.3 47.4 %all-to-all-start = ((bf16[8,64,1728]{2,1,0:T(8,128)(2,1)}), bf16[8,64,1728]{2,1,0:T(8,128)(2,1)S(1)}, u32[]{:S(2)}, u32[]{:S(2)}) async-start(bf16[8,64,1728]{2,1,0:T(8,128)(2,1)} %fusion.79), calls=%async_computation | async-start | bytes 3670016 | tf_op jit(solution)/shard_map/all_to_all | solution.py:110
  45.7 32.3 %copy-start.3 = (s32[576]{0:T(1024)S(1)}, s32[576]{0:T(1024)}, u32[]{:S(2)}) copy-start(s32[576]{0:T(1024)} %constant.203.clone) | copy-start | bytes 6916
  76.0 56.6 %collective-permute-start = (bf16[512,576]{0,1:T(8,128)(2,1)S(1)}, bf16[512,576]{0,1:T(8,128)(2,1)S(1)}, u32[]{:S(2)}, u32[]{:S(2)}) collective-permute-start(bf16[512,576]{0,1:T(8,128)(2,1)S(1)} %copy.10), channel_id=1, source_target_pairs={{1,0},{2,1},{3,2},{4,3},{5,4},{6,5},{7,6},{9,8},{10,9},{11,10},{12... | collective-permute-start | bytes 1769480 | tf_op jit(solution)/shard_map/ppermute | solution.py:189
  79.3 59.8 %collective-permute-start.3 = (bf16[144,512]{1,0:T(8,128)(2,1)S(1)}, bf16[144,512]{1,0:T(8,128)(2,1)}, u32[]{:S(2)}, u32[]{:S(2)}) collective-permute-start(bf16[144,512]{1,0:T(8,128)(2,1)S(1)} %get-tuple-element.40), channel_id=1, source_target_pairs={{0,736},{8,744},{16,752},{24,760},{32,0},{40,8},{48,16},{56,24},{6... | collective-permute-start | bytes 442376 | tf_op jit(solution)/shard_map/ppermute | solution.py:26
  124.7 15.6 %collective-permute-start.2 = (bf16[144,512]{1,0:T(8,128)(2,1)S(1)}, bf16[144,512]{1,0:T(8,128)(2,1)}, u32[]{:S(2)}, u32[]{:S(2)}) collective-permute-start(bf16[144,512]{1,0:T(8,128)(2,1)S(1)} %get-tuple-element.39), channel_id=1, source_target_pairs={{0,760},{8,0},{16,8},{24,16},{32,24},{40,32},{48,40},{56,48},{64,5... | collective-permute-start | bytes 442376 | tf_op jit(solution)/shard_map/ppermute | solution.py:26
  134.6 12.6 %all-to-all-start.1 = ((bf16[4,1,128,512]{3,2,1,0:T(8,128)(2,1)}), bf16[4,1,128,512]{3,2,1,0:T(8,128)(2,1)S(1)}, u32[]{:S(2)}, u32[]{:S(2)}) async-start(bf16[4,1,128,512]{3,2,1,0:T(8,128)(2,1)} %bitcast.16), calls=%async_computation.1 | async-start | bytes 1048576 | tf_op jit(solution)/shard_map/all_to_all | solution.py:154
  147.2 18.4 %all-to-all-start.3 = ((bf16[4,2,128,512]{3,2,1,0:T(8,128)(2,1)}), bf16[4,2,128,512]{3,2,1,0:T(8,128)(2,1)S(1)}, u32[]{:S(2)}, u32[]{:S(2)}) async-start(bf16[4,2,128,512]{3,2,1,0:T(8,128)(2,1)} %maximum_bitcast_fusion), calls=%async_computation.3 | async-start | bytes 2097152 | tf_op jit(solution)/shard_map/all_to_all | solution.py:154
  152.8 25.2 %collective-permute-start.1 = (bf16[1,128,512]{2,1,0:T(8,128)(2,1)S(1)}, bf16[1,128,512]{2,1,0:T(8,128)(2,1)S(1)}, u32[]{:S(2)}, u32[]{:S(2)}) collective-permute-start(bf16[1,128,512]{2,1,0:T(8,128)(2,1)S(1)} %bitcast.128), channel_id=1, source_target_pairs={{0,4},{4,0},{1,5},{5,1},{2,6},{6,2},{3,7},{7,3},{8,12},{12,8},{9,1... | collective-permute-start | bytes 393224 | tf_op jit(solution)/shard_map/ppermute | solution.py:30
  165.8 23.8 %collective-permute-start.4 = (bf16[2,128,512]{2,1,0:T(8,128)(2,1)S(1)}, bf16[2,128,512]{2,1,0:T(8,128)(2,1)S(1)}, u32[]{:S(2)}, u32[]{:S(2)}) collective-permute-start(bf16[2,128,512]{2,1,0:T(8,128)(2,1)S(1)} %reduce_sum.77), channel_id=1, source_target_pairs={{0,4},{4,0},{1,5},{5,1},{2,6},{6,2},{3,7},{7,3},{8,12},{12,8},{9,1... | collective-permute-start | bytes 786440 | tf_op jit(solution)/shard_map/ppermute | solution.py:30
  178.9 11.9 %all-to-all-start.2 = ((bf16[4,1,128,512]{3,2,1,0:T(8,128)(2,1)}), bf16[4,1,128,512]{3,2,1,0:T(8,128)(2,1)S(1)}, u32[]{:S(2)}, u32[]{:S(2)}) async-start(bf16[4,1,128,512]{3,2,1,0:T(8,128)(2,1)} %broadcast_in_dim.44), calls=%async_computation.2 | async-start | bytes 1048576 | tf_op jit(solution)/shard_map/all_to_all | solution.py:166
  189.7 8.3 %copy-start.1 = (bf16[1,512,128]{2,1,0:T(8,128)(2,1)S(1)}, bf16[1,512,128]{2,1,0:T(8,128)(2,1)}, u32[]{:S(2)}) copy-start(bf16[1,512,128]{2,1,0:T(8,128)(2,1)} %param.8) | copy-start | bytes 393220
  191.9 18.7 %all-to-all-start.4 = ((bf16[4,2,128,512]{3,2,1,0:T(8,128)(2,1)}), bf16[4,2,128,512]{3,2,1,0:T(8,128)(2,1)S(1)}, u32[]{:S(2)}, u32[]{:S(2)}) async-start(bf16[4,2,128,512]{3,2,1,0:T(8,128)(2,1)} %broadcast_in_dim.45), calls=%async_computation.4 | async-start | bytes 2097152 | tf_op jit(solution)/shard_map/all_to_all | solution.py:166
  198.0 8.8 %collective-permute-start.6 = (bf16[512,128]{1,0:T(8,128)(2,1)S(1)}, bf16[512,128]{1,0:T(8,128)(2,1)S(1)}, u32[]{:S(2)}, u32[]{:S(2)}) collective-permute-start(bf16[512,128]{1,0:T(8,128)(2,1)S(1)} %bitcast.126), channel_id=1, source_target_pairs={{0,736},{8,744},{16,752},{24,760},{32,0},{40,8},{48,16},{56,24},{6... | collective-permute-start | bytes 393224 | tf_op jit(solution)/shard_map/ppermute | solution.py:26
  200.9 5.9 %collective-permute-start.5 = (bf16[512,128]{1,0:T(8,128)(2,1)S(1)}, bf16[512,128]{1,0:T(8,128)(2,1)S(1)}, u32[]{:S(2)}, u32[]{:S(2)}) collective-permute-start(bf16[512,128]{1,0:T(8,128)(2,1)S(1)} %bitcast.127), channel_id=1, source_target_pairs={{0,760},{8,0},{16,8},{24,16},{32,24},{40,32},{48,40},{56,48},{64,5... | collective-permute-start | bytes 393224 | tf_op jit(solution)/shard_map/ppermute | solution.py:26
  211.0 16.5 %collective-permute-start.8 = (bf16[512,128]{1,0:T(8,128)(2,1)S(1)}, bf16[512,128]{1,0:T(8,128)(2,1)S(1)}, u32[]{:S(2)}, u32[]{:S(2)}) collective-permute-start(bf16[512,128]{1,0:T(8,128)(2,1)S(1)} %convolution_convert_fusion.4), channel_id=1, source_target_pairs={{0,32},{8,40},{16,48},{24,56},{32,64},{40,72},{48,80},{56,88},{64,... | collective-permute-start | bytes 393224 | tf_op jit(solution)/shard_map/ppermute | solution.py:26
  213.3 14.7 %collective-permute-start.7 = (bf16[512,128]{1,0:T(8,128)(2,1)S(1)}, bf16[512,128]{1,0:T(8,128)(2,1)S(1)}, u32[]{:S(2)}, u32[]{:S(2)}) collective-permute-start(bf16[512,128]{1,0:T(8,128)(2,1)S(1)} %convolution_convert_fusion.5), channel_id=1, source_target_pairs={{0,8},{8,16},{16,24},{24,32},{32,40},{40,48},{48,56},{56,64},{64,7... | collective-permute-start | bytes 393224 | tf_op jit(solution)/shard_map/ppermute | solution.py:26
  229.0 17.5 %collective-permute-start.9 = (bf16[512,128]{1,0:T(8,128)(2,1)S(1)}, bf16[512,128]{1,0:T(8,128)(2,1)S(1)}, u32[]{:S(2)}, u32[]{:S(2)}) collective-permute-start(bf16[512,128]{1,0:T(8,128)(2,1)S(1)} %get-tuple-element.83), channel_id=1, source_target_pairs={{0,8},{16,24},{32,40},{48,56},{64,72},{80,88},{96,104},{112,120},{... | collective-permute-start | bytes 393224 | tf_op jit(solution)/shard_map/ppermute | solution.py:118
  230.9 15.6 %collective-permute-start.10 = (bf16[512,128]{1,0:T(8,128)(2,1)S(1)}, bf16[512,128]{1,0:T(8,128)(2,1)S(1)}, u32[]{:S(2)}, u32[]{:S(2)}) collective-permute-start(bf16[512,128]{1,0:T(8,128)(2,1)S(1)} %get-tuple-element.84), channel_id=1, source_target_pairs={{8,16},{24,32},{40,48},{56,64},{72,80},{88,96},{104,112},{120,128}... | collective-permute-start | bytes 393224 | tf_op jit(solution)/shard_map/ppermute | solution.py:118
  234.0 16.8 %collective-permute-start.12 = (bf16[512,128]{1,0:T(8,128)(2,1)S(1)}, bf16[512,128]{1,0:T(8,128)(2,1)S(1)}, u32[]{:S(2)}, u32[]{:S(2)}) collective-permute-start(bf16[512,128]{1,0:T(8,128)(2,1)S(1)} %get-tuple-element.78), channel_id=1, source_target_pairs={{32,64},{40,72},{48,80},{56,88},{96,128},{104,136},{112,144},{120,... | collective-permute-start | bytes 393224 | tf_op jit(solution)/shard_map/ppermute | solution.py:118
  236.7 15.2 %collective-permute-start.11 = (bf16[512,128]{1,0:T(8,128)(2,1)S(1)}, bf16[512,128]{1,0:T(8,128)(2,1)S(1)}, u32[]{:S(2)}, u32[]{:S(2)}) collective-permute-start(bf16[512,128]{1,0:T(8,128)(2,1)S(1)} %get-tuple-element.77), channel_id=1, source_target_pairs={{0,32},{8,40},{16,48},{24,56},{64,96},{72,104},{80,112},{88,120},{... | collective-permute-start | bytes 393224 | tf_op jit(solution)/shard_map/ppermute | solution.py:118
  252.9 26.3 %collective-permute-start.16 = (bf16[512,128]{1,0:T(8,128)(2,1)S(1)}, bf16[512,128]{1,0:T(8,128)(2,1)S(1)}, u32[]{:S(2)}, u32[]{:S(2)}) collective-permute-start(bf16[512,128]{1,0:T(8,128)(2,1)S(1)} %get-tuple-element.74), channel_id=1, source_target_pairs={{32,64},{40,72},{48,80},{56,88},{96,128},{104,136},{112,144},{120,... | collective-permute-start | bytes 393224 | tf_op jit(solution)/shard_map/ppermute | solution.py:118
  260.6 18.6 %collective-permute-start.15 = (bf16[512,128]{1,0:T(8,128)(2,1)S(1)}, bf16[512,128]{1,0:T(8,128)(2,1)S(1)}, u32[]{:S(2)}, u32[]{:S(2)}) collective-permute-start(bf16[512,128]{1,0:T(8,128)(2,1)S(1)} %get-tuple-element.73), channel_id=1, source_target_pairs={{0,32},{8,40},{16,48},{24,56},{64,96},{72,104},{80,112},{88,120},{... | collective-permute-start | bytes 393224 | tf_op jit(solution)/shard_map/ppermute | solution.py:118
  265.7 13.2 %collective-permute-start.14 = (bf16[512,128]{1,0:T(8,128)(2,1)S(1)}, bf16[512,128]{1,0:T(8,128)(2,1)S(1)}, u32[]{:S(2)}, u32[]{:S(2)}) collective-permute-start(bf16[512,128]{1,0:T(8,128)(2,1)S(1)} %get-tuple-element.82), channel_id=1, source_target_pairs={{8,16},{24,32},{40,48},{56,64},{72,80},{88,96},{104,112},{120,128}... | collective-permute-start | bytes 393224 | tf_op jit(solution)/shard_map/ppermute | solution.py:118
  272.9 6.0 %collective-permute-start.13 = (bf16[512,128]{1,0:T(8,128)(2,1)S(1)}, bf16[512,128]{1,0:T(8,128)(2,1)S(1)}, u32[]{:S(2)}, u32[]{:S(2)}) collective-permute-start(bf16[512,128]{1,0:T(8,128)(2,1)S(1)} %get-tuple-element.81), channel_id=1, source_target_pairs={{0,8},{16,24},{32,40},{48,56},{64,72},{80,88},{96,104},{112,120},{... | collective-permute-start | bytes 393224 | tf_op jit(solution)/shard_map/ppermute | solution.py:118

commit v4 on v3

--- a/solution.py
+++ b/solution.py
@@ -1,7 +1,11 @@
+import functools
+
 import jax
 import jax.numpy as jnp
 import numpy as np
 from jax import lax
+from jax.experimental import pallas as pl
+from jax.experimental.pallas import tpu as pltpu
 from jax.sharding import Mesh, PartitionSpec as P
 
 P_SIZE = 24
@@ -70,7 +74,7 @@
     return jnp.where(active[:, None], current / magnitude, 0.0).astype(jnp.bfloat16)
 
 
-def face_selector(planes):
+def face_selector(planes, width):
     grid = np.arange(planes * PLANE, dtype=np.int32).reshape(planes, P_SIZE, P_SIZE)
     last = P_SIZE - 1
     groups = [
@@ -78,7 +82,7 @@
         grid[:, :, last - 1], grid[:, :, last], grid[:, last - 1, :], grid[:, last, :],
     ]
     chosen = jnp.asarray(np.concatenate([g.reshape(-1) for g in groups]))
-    points = jnp.arange(planes * PLANE, dtype=jnp.int32)
+    points = jnp.arange(width, dtype=jnp.int32)
     return (chosen[:, None] == points[None, :]).astype(jnp.bfloat16)
 
 
@@ -102,13 +106,35 @@
     return chunks
 
 
+def cut_kernel(length, *refs):
+    out = refs[-1]
+    count, _, width = out.shape
+    piece = (width - length) // 2
+    middle = refs[0].shape[1] // 2
+    step = refs[0].shape[0]
+    for k, source in enumerate(refs[:-1]):
+        rows = pl.ds(k * step, step)
+        for s in range(count):
+            out[s, rows, :length] = source[:, s * length : (s + 1) * length]
+            low = middle - PLANE + s * piece
+            out[s, rows, length : length + piece] = source[:, low : low + piece]
+            out[s, rows, length + piece :] = source[:, low + PLANE : low + PLANE + piece]
+
+
 def slab_rows(chunks, length):
-    slabs = [
-        jnp.concatenate([c[:, s * length : (s + 1) * length] for c in chunks])
-        for s in range(HALVES * SLABS)
-    ]
-    rows = lax.all_to_all(jnp.stack(slabs), BOTH, 0, 0, tiled=True)
-    return rows.reshape(-1, length)
+    count = HALVES * SLABS
+    width = length + 2 * (PLANE // count)
+    functions = sum(c.shape[0] for c in chunks)
+    whole = pl.BlockSpec(memory_space=pltpu.VMEM)
+    slabs = pl.pallas_call(
+        functools.partial(cut_kernel, length),
+        out_shape=jax.ShapeDtypeStruct((count, functions, width), jnp.bfloat16),
+        in_specs=[whole] * len(chunks),
+        out_specs=whole,
+        compiler_params=pltpu.CompilerParams(vmem_limit_bytes=16 << 20),
+    )(*chunks)
+    rows = lax.all_to_all(slabs, BOTH, 0, 0, tiled=True)
+    return rows.reshape(-1, width)
 
 
 def pair_swap(value, by, odd):
@@ -187,17 +213,23 @@
     rows = slab_rows(chunks, length)
 
     above = lax.ppermute(
-        rows[:, :PLANE], BOTH, [(i + 1, i) for i in range(HALVES * SLABS - 1)]
-    )
-    faces = transposed_dot(face_selector(planes), rows, 1, 1).astype(jnp.bfloat16)
+        rows[:, :PLANE], "slab", [(i + 1, i) for i in range(SLABS - 1)]
+    )
+    faces = transposed_dot(face_selector(planes, rows.shape[1]), rows, 1, 1)
+    faces = faces.astype(jnp.bfloat16)
     width = 2 * planes * P_SIZE
     other_z = from_behind(faces[:width], "elem", -1)
     other_y = from_behind(faces[width : 2 * width], "elem", -EB)
 
-    padded = jnp.pad(rows.astype(jnp.float32), ((0, 0), (PLANE, PLANE)))
+    padded = jnp.pad(rows[:, :length].astype(jnp.float32), ((0, 0), (PLANE, PLANE)))
     applied = flat_hamiltonian(padded, length, slab_potential, side_masks(length))
-    last = rows[:, length - PLANE :]
-    h_self = transposed_dot(rows, applied.astype(jnp.bfloat16), 1, 1)
+    last = rows[:, length - PLANE : length]
+    piece = (rows.shape[1] - length) // 2
+    below_part, above_part = rows[:, length : length + piece], rows[:, length + piece :]
+    applied = jnp.concatenate(
+        [applied.astype(jnp.bfloat16), -above_part, -below_part], axis=1
+    )
+    h_self = transposed_dot(rows, applied, 1, 1)
     h_self = h_self - transposed_dot(last, above, 1, 1) - transposed_dot(above, last, 1, 1)
     weight = -0.5 / PLANE
     h_z = transposed_dot(faces[2 * width : 3 * width], other_z, 0, 0) * weight

time: 282 us -> 283 us (level)
  starting transfers between devices: 160 us -> 139 us
  waiting for transfers between devices: 69.9 us -> 86.3 us
  local copies, waits for them, and re-layouts: 3.16 us -> 7.86 us
    ppermute x2, starting transfers between devices: 24.1 us -> 4.39 us  [swap_halves(): return lax.ppermute(value, 'half', [(0, 1), (1, 0)])]
    ppermute x8, starting transfers between devices: 39.1 us -> 25.7 us  [pair_swap(): return lax.ppermute(value, 'elem', pairs + [(j, i) for i, j in pairs])]
    ppermute x6, starting transfers between devices: 56.2 us -> 66.3 us  [from_behind(): lax.ppermute(value, axis, [(i, (i + by) % devices) for i in range(devices)])]
    all_to_all x2, waiting for transfers between devices: 5.28 us -> 14.9 us  [sum_over_slabs(): pieces = lax.all_to_all(slices_of(partial), 'slab', 0, 0, tiled=True)]
    convert_element_type x1 -> x2, other arithmetic: 0.37 us -> 8.57 us  [the longest x1 6.53 us: device_body(): applied.astype(jnp.bfloat16)]
    ppermute x8, waiting for transfers between devices: 8.82 us -> 14.5 us  [pair_swap(): return lax.ppermute(value, 'elem', pairs + [(j, i) for i, j in pairs])]
    unnamed x8 -> x1, other arithmetic: 5.15 us -> 0.13 us
    all_to_all x2, waiting for transfers between devices: 4.59 us -> 0.01 us  [gather_slices(): blocks = lax.all_to_all(copies, 'slab', 0, 0, tiled=True)]
  transfers between devices with their start and end apart: 22 -> 22, of which waited for: 12 -> 11; matrix products, arithmetic and copies ran while one was open for 6% -> 9% of each run, Pallas kernels for 0% -> 0%
where the time goes in v4:
time: 283 us; the launch traced here: 282 us
  starting transfers between devices  139 us (49%)
  waiting for transfers between devices  86.3 us (30%)
  other arithmetic  32.1 us (11%)
  matrix products  13.6 us (5%)
  local copies, waits for them, and re-layouts  7.86 us (3%)
    ppermute x6, starting transfers between devices, from_behind(): lax.ppermute(value, axis, [(i, (i + by) % devices) for i in range(devices)])  66.3 us
    all_to_all x1, waiting for transfers between devices, slab_rows(): rows = lax.all_to_all(slabs, BOTH, 0, 0, tiled=True)  31.9 us
    ppermute x8, starting transfers between devices, pair_swap(): return lax.ppermute(value, 'elem', pairs + [(j, i) for i, j in pairs])  25.7 us
    all_to_all x1, starting transfers between devices, slab_rows(): rows = lax.all_to_all(slabs, BOTH, 0, 0, tiled=True)  17.4 us
    ppermute x6, waiting for transfers between devices, from_behind(): lax.ppermute(value, axis, [(i, (i + by) % devices) for i in range(devices)])  16.6 us
    all_to_all x2, waiting for transfers between devices, sum_over_slabs(): pieces = lax.all_to_all(slices_of(partial), 'slab', 0, 0, tiled=True)  14.9 us
    ppermute x8, waiting for transfers between devices, pair_swap(): return lax.ppermute(value, 'elem', pairs + [(j, i) for i, j in pairs])  14.5 us
    dot_general x21, matrix products, transposed_dot(): lax.dot_general(a, b, (((contract_a,), (contract_b,)), ((), ())), preferr...  13.6 us
  transfers between devices with their start and end apart: 22, of which 11 were waited for; matrix products, arithmetic and copies ran while one was open for 9% of the time, Pallas kernels for 0%

profile of v4, /device:TPU:6, one launch (start us, length us, event | category | flops | bytes accessed | tf_op | source)
XLA Modules:
  0.0 282.1 jit_solution(9437260909831197685)
XLA Ops:
  0.1 2.8 slice_bitcast_fusion
  3.0 4.7 %broadcast_multiply_fusion.3 = (f32[16,13824]{1,0:T(8,128)S(1)}, f32[16,13824]{1,0:T(8,128)S(1)}) fusion(f32[13824]{0:T(1024)S(1)} %reduce.3, f32[13824]{0:T(1024)S(1)} %get-tuple-element.59, f32[13824]{0:T(1024)S(1)} %get-tuple-element.60, f32[13824]{0:T(1024)S(1)} %get-tuple-element.58, f32[13824]{0:T(1024)S(1)} %get-tuple-element.57, ...), kind=kLoop, calls=%fused_computation.147 | loop fusion | flops 3760128 | bytes 3373056 | tf_op jit(solution)/shard_map/div | solution.py:68
  7.8 2.5 multiply_reduce_fusion.3
  10.9 1.3 select_convert_fusion.3.refs_0_
  12.3 1.4 broadcast_multiply_fusion.2
  13.7 1.5 multiply_reduce_fusion.2
  15.5 1.4 broadcast_multiply_fusion.1
  17.0 1.5 multiply_reduce_fusion.1
  18.8 1.4 broadcast_multiply_fusion
  20.2 1.5 multiply_reduce_fusion
  21.9 1.9 shard_map.55
  23.8 17.4 %all-to-all-start = ((bf16[8,64,1872]{2,1,0:T(8,128)(2,1)}), bf16[8,64,1872]{2,1,0:T(8,128)(2,1)S(1)}, u32[]{:S(2)}, u32[]{:S(2)}) async-start(bf16[8,64,1872]{2,1,0:T(8,128)(2,1)} %shard_map.55), calls=%async_computation | async-start | bytes 3932160 | tf_op jit(solution)/shard_map/all_to_all | solution.py:136
  41.4 31.9 %all-to-all-done = bf16[8,64,1872]{2,1,0:T(8,128)(2,1)S(1)} async-done(((bf16[8,64,1872]{2,1,0:T(8,128)(2,1)}), bf16[8,64,1872]{2,1,0:T(8,128)(2,1)S(1)}, u32[]{:S(2)}, u32[]{:S(2)}) %all-to-all-start) | async-done | bytes 1916960 | tf_op jit(solution)/shard_map/all_to_all | solution.py:136
  73.3 2.0 slice_convert_fusion
  75.6 1.8 collective-permute-start
  77.4 1.4 fusion.15
  78.9 0.8 copy-done.4
  79.7 0.7 fusion.110
  80.4 46.7 %collective-permute-start.3 = (bf16[144,512]{1,0:T(8,128)(2,1)}, bf16[144,512]{1,0:T(8,128)(2,1)}, u32[]{:S(2)}, u32[]{:S(2)}) collective-permute-start(bf16[144,512]{1,0:T(8,128)(2,1)} %get-tuple-element.42), channel_id=1, source_target_pairs={{0,736},{8,744},{16,752},{24,760},{32,0},{40,8},{48,16},{56,24},{6... | collective-permute-start | bytes 442376 | tf_op jit(solution)/shard_map/ppermute | solution.py:30
  127.1 1.9 collective-permute-start.2
  129.1 6.5 %fusion.8 = bf16[512,1728]{1,0:T(8,128)(2,1)} fusion(f32[512,1728]{1,0:T(8,128)S(1)} %copy-done, f32[1728]{0:T(1024)S(1)} %dynamic-slice_reduce_fusion, f32[1728]{0:T(1024)S(1)} %get-tuple-element.67, f32[1728]{0:T(1024)S(1)} %get-tuple-element.68, f32[1728]{0:T(1024)S(1)} %get-tuple-element.66, f32[1728]{0:T(1024)S(1)} %get-tuple-element.65), kind=kLoop, calls=%fused_computation.15 | loop fusion | flops 12386304 | bytes 5342976 | tf_op jit(solution)/shard_map/convert_element_type | solution.py:230
  135.7 3.9 %concatenate.8 = bf16[512,1872]{1,0:T(8,128)(2,1)} concatenate(bf16[512,1728]{1,0:T(8,128)(2,1)} %fusion.8, bf16[512,72]{1,0:T(8,128)(2,1)S(1)} %get-tuple-element.34, bf16[512,72]{1,0:T(8,128)(2,1)S(1)} %get-tuple-element.33), dimensions={1} | concatenate | bytes 3833856 | tf_op jit(solution)/shard_map/concatenate | solution.py:229
  139.6 2.8 %fusion.111 = f32[512,512]{1,0:T(8,128)S(1)} fusion(bf16[512,1872]{1,0:T(8,128)(2,1)S(1)} %bitcast.84, bf16[512,1872]{1,0:T(8,128)(2,1)} %concatenate.8), kind=kOutput, calls=%fused_computation.232 | convolution fusion | flops 981467136 | bytes 4882432 | tf_op jit(solution)/shard_map/dot_general | solution.py:90
  142.5 0.6 convolution_subtract_fusion.1
  143.1 1.4 fusion.18
  144.5 5.9 %all-to-all-start.1 = ((bf16[4,1,128,512]{3,2,1,0:T(8,128)(2,1)}), bf16[4,1,128,512]{3,2,1,0:T(8,128)(2,1)S(1)}, u32[]{:S(2)}, u32[]{:S(2)}) async-start(bf16[4,1,128,512]{3,2,1,0:T(8,128)(2,1)} %bitcast.8), calls=%async_computation.1 | async-start | bytes 1048576 | tf_op jit(solution)/shard_map/all_to_all | solution.py:180
  150.4 1.2 fusion.17
  151.7 1.2 fusion.16
  153.0 1.1 maximum_bitcast_fusion
  154.0 4.5 %all-to-all-done.1 = bf16[4,1,128,512]{3,2,1,0:T(8,128)(2,1)S(1)} async-done(((bf16[4,1,128,512]{3,2,1,0:T(8,128)(2,1)}), bf16[4,1,128,512]{3,2,1,0:T(8,128)(2,1)S(1)}, u32[]{:S(2)}, u32[]{:S(2)}) %all-to-all-start.1) | async-done | bytes 524320 | tf_op jit(solution)/shard_map/all_to_all | solution.py:180
  158.5 5.6 %all-to-all-start.3 = ((bf16[4,2,128,512]{3,2,1,0:T(8,128)(2,1)}), bf16[4,2,128,512]{3,2,1,0:T(8,128)(2,1)S(1)}, u32[]{:S(2)}, u32[]{:S(2)}) async-start(bf16[4,2,128,512]{3,2,1,0:T(8,128)(2,1)} %maximum_bitcast_fusion), calls=%async_computation.3 | async-start | bytes 2097152 | tf_op jit(solution)/shard_map/all_to_all | solution.py:180
  164.2 2.3 collective-permute-start.1
  166.4 10.5 %all-to-all-done.3 = bf16[4,2,128,512]{3,2,1,0:T(8,128)(2,1)S(1)} async-done(((bf16[4,2,128,512]{3,2,1,0:T(8,128)(2,1)}), bf16[4,2,128,512]{3,2,1,0:T(8,128)(2,1)S(1)}, u32[]{:S(2)}, u32[]{:S(2)}) %all-to-all-start.3) | async-done | bytes 1048608 | tf_op jit(solution)/shard_map/all_to_all | solution.py:180
  177.2 2.1 collective-permute-start.4
  179.3 0.8 broadcast_in_dim.44
  180.2 5.5 %all-to-all-start.2 = ((bf16[4,1,128,512]{3,2,1,0:T(8,128)(2,1)}), bf16[4,1,128,512]{3,2,1,0:T(8,128)(2,1)S(1)}, u32[]{:S(2)}, u32[]{:S(2)}) async-start(bf16[4,1,128,512]{3,2,1,0:T(8,128)(2,1)} %broadcast_in_dim.44), calls=%async_computation.2 | async-start | bytes 1048576 | tf_op jit(solution)/shard_map/all_to_all | solution.py:192
  185.7 8.4 %collective-permute-done.4 = bf16[2,128,512]{2,1,0:T(8,128)(2,1)S(1)} collective-permute-done((bf16[2,128,512]{2,1,0:T(8,128)(2,1)S(1)}, bf16[2,128,512]{2,1,0:T(8,128)(2,1)S(1)}, u32[]{:S(2)}, u32[]{:S(2)}) %collective-permute-start.4) | collective-permute-done | bytes 262176 | tf_op jit(solution)/shard_map/ppermute | solution.py:34
  194.2 1.1 broadcast_in_dim.45
  195.3 6.4 %all-to-all-start.4 = ((bf16[4,2,128,512]{3,2,1,0:T(8,128)(2,1)}), bf16[4,2,128,512]{3,2,1,0:T(8,128)(2,1)S(1)}, u32[]{:S(2)}, u32[]{:S(2)}) async-start(bf16[4,2,128,512]{3,2,1,0:T(8,128)(2,1)} %broadcast_in_dim.45), calls=%async_computation.4 | async-start | bytes 2097152 | tf_op jit(solution)/shard_map/all_to_all | solution.py:192
  201.7 11.1 %collective-permute-start.6 = (bf16[512,128]{1,0:T(8,128)(2,1)S(1)}, bf16[512,128]{1,0:T(8,128)(2,1)S(1)}, u32[]{:S(2)}, u32[]{:S(2)}) collective-permute-start(bf16[512,128]{1,0:T(8,128)(2,1)S(1)} %bitcast.96), channel_id=1, source_target_pairs={{0,736},{8,744},{16,752},{24,760},{32,0},{40,8},{48,16},{56,24},{6... | collective-permute-start | bytes 393224 | tf_op jit(solution)/shard_map/ppermute | solution.py:30
  212.8 1.9 collective-permute-start.5
  214.8 0.5 collective-permute-done.6
  215.3 1.9 collective-permute-done.5
  218.0 1.9 collective-permute-start.8
  219.9 0.3 convolution_convert_fusion.5
  220.3 2.8 %collective-permute-start.7 = (bf16[512,128]{1,0:T(8,128)(2,1)S(1)}, bf16[512,128]{1,0:T(8,128)(2,1)S(1)}, u32[]{:S(2)}, u32[]{:S(2)}) collective-permute-start(bf16[512,128]{1,0:T(8,128)(2,1)S(1)} %convolution_convert_fusion.5), channel_id=1, source_target_pairs={{0,8},{8,16},{16,24},{24,32},{32,40},{40,48},{48,56},{56,64},{64,7... | collective-permute-start | bytes 393224 | tf_op jit(solution)/shard_map/ppermute | solution.py:30
  223.4 13.4 %collective-permute-done.8 = bf16[512,128]{1,0:T(8,128)(2,1)S(1)} collective-permute-done((bf16[512,128]{1,0:T(8,128)(2,1)S(1)}, bf16[512,128]{1,0:T(8,128)(2,1)S(1)}, u32[]{:S(2)}, u32[]{:S(2)}) %collective-permute-start.8) | collective-permute-done | bytes 131104 | tf_op jit(solution)/shard_map/ppermute | solution.py:30
  236.8 0.7 collective-permute-done.7
  237.8 0.4 convolution_convert_fusion.3
  238.1 0.4 broadcast_select_fusion.3
  238.5 1.9 collective-permute-start.9
  240.4 2.0 collective-permute-start.10
  242.5 3.2 %collective-permute-start.12 = (bf16[512,128]{1,0:T(8,128)(2,1)S(1)}, bf16[512,128]{1,0:T(8,128)(2,1)S(1)}, u32[]{:S(2)}, u32[]{:S(2)}) collective-permute-start(bf16[512,128]{1,0:T(8,128)(2,1)S(1)} %get-tuple-element.48), channel_id=1, source_target_pairs={{32,64},{40,72},{48,80},{56,88},{96,128},{104,136},{112,144},{120,... | collective-permute-start | bytes 393224 | tf_op jit(solution)/shard_map/ppermute | solution.py:144
  245.6 1.9 collective-permute-start.11
  247.9 5.8 %collective-permute-done.10 = bf16[512,128]{1,0:T(8,128)(2,1)S(1)} collective-permute-done((bf16[512,128]{1,0:T(8,128)(2,1)S(1)}, bf16[512,128]{1,0:T(8,128)(2,1)S(1)}, u32[]{:S(2)}, u32[]{:S(2)}) %collective-permute-start.10) | collective-permute-done | bytes 131104 | tf_op jit(solution)/shard_map/ppermute | solution.py:144
  253.9 5.8 %collective-permute-done.12 = bf16[512,128]{1,0:T(8,128)(2,1)S(1)} collective-permute-done((bf16[512,128]{1,0:T(8,128)(2,1)S(1)}, bf16[512,128]{1,0:T(8,128)(2,1)S(1)}, u32[]{:S(2)}, u32[]{:S(2)}) %collective-permute-start.12) | collective-permute-done | bytes 131104 | tf_op jit(solution)/shard_map/ppermute | solution.py:144
  260.1 0.4 convolution_convert_fusion.1
  260.4 0.4 broadcast_select_fusion.1
  260.8 4.7 %collective-permute-start.16 = (bf16[512,128]{1,0:T(8,128)(2,1)S(1)}, bf16[512,128]{1,0:T(8,128)(2,1)S(1)}, u32[]{:S(2)}, u32[]{:S(2)}) collective-permute-start(bf16[512,128]{1,0:T(8,128)(2,1)S(1)} %get-tuple-element.44), channel_id=1, source_target_pairs={{32,64},{40,72},{48,80},{56,88},{96,128},{104,136},{112,144},{120,... | collective-permute-start | bytes 393224 | tf_op jit(solution)/shard_map/ppermute | solution.py:144
  265.6 1.9 collective-permute-start.15
  267.5 8.1 %collective-permute-start.14 = (bf16[512,128]{1,0:T(8,128)(2,1)S(1)}, bf16[512,128]{1,0:T(8,128)(2,1)S(1)}, u32[]{:S(2)}, u32[]{:S(2)}) collective-permute-start(bf16[512,128]{1,0:T(8,128)(2,1)S(1)} %get-tuple-element.52), channel_id=1, source_target_pairs={{8,16},{24,32},{40,48},{56,64},{72,80},{88,96},{104,112},{120,128}... | collective-permute-start | bytes 393224 | tf_op jit(solution)/shard_map/ppermute | solution.py:144
  275.6 1.9 collective-permute-start.13
  277.8 2.9 %collective-permute-done.14 = bf16[512,128]{1,0:T(8,128)(2,1)S(1)} collective-permute-done((bf16[512,128]{1,0:T(8,128)(2,1)S(1)}, bf16[512,128]{1,0:T(8,128)(2,1)S(1)}, u32[]{:S(2)}, u32[]{:S(2)}) %collective-permute-start.14) | collective-permute-done | bytes 131104 | tf_op jit(solution)/shard_map/ppermute | solution.py:144
  281.4 0.7 fusion.79
  (65 shorter events, 5.1 us)
Async XLA Ops:
  0.0 3.0 %copy-start.1 = (bf16[1,64,13824]{2,1,0:T(8,128)(2,1)S(1)}, bf16[1,64,13824]{2,1,0:T(8,128)(2,1)}, u32[]{:S(2)}) copy-start(bf16[1,64,13824]{2,1,0:T(8,128)(2,1)} %param.5) | copy-start | bytes 5308420
  0.0 2.9 %copy-start.6 = (f32[1,13824]{1,0:T(1,128)S(1)}, f32[1,13824]{1,0:T(1,128)}, u32[]{:S(2)}) copy-start(f32[1,13824]{1,0:T(1,128)} %param.6) | copy-start | bytes 165892
  12.3 3.2 %copy-start.2 = (bf16[16,13824]{1,0:T(8,128)(2,1)S(1)}, bf16[16,13824]{1,0:T(8,128)(2,1)}, u32[]{:S(2)}) copy-start(bf16[16,13824]{1,0:T(8,128)(2,1)} %get-tuple-element.14) | copy-start | bytes 1327108
  23.8 49.5 %all-to-all-start = ((bf16[8,64,1872]{2,1,0:T(8,128)(2,1)}), bf16[8,64,1872]{2,1,0:T(8,128)(2,1)S(1)}, u32[]{:S(2)}, u32[]{:S(2)}) async-start(bf16[8,64,1872]{2,1,0:T(8,128)(2,1)} %shard_map.55), calls=%async_computation | async-start | bytes 3932160 | tf_op jit(solution)/shard_map/all_to_all | solution.py:136
  73.3 4.2 %copy-start.7 = (s32[576]{0:T(1024)S(1)}, s32[576]{0:T(1024)}, u32[]{:S(2)}) copy-start(s32[576]{0:T(1024)} %constant.203.clone) | copy-start | bytes 6916
  75.6 53.4 %copy-start = (f32[512,1728]{1,0:T(8,128)S(1)}, f32[512,1728]{1,0:T(8,128)}, u32[]{:S(2)}) copy-start(f32[512,1728]{1,0:T(8,128)} %slice_convert_fusion) | copy-start | bytes 10616836
  75.6 66.8 %collective-permute-start = (bf16[512,576]{0,1:T(8,128)(2,1)S(1)}, bf16[512,576]{0,1:T(8,128)(2,1)S(1)}, u32[]{:S(2)}, u32[]{:S(2)}) collective-permute-start(bf16[512,576]{0,1:T(8,128)(2,1)S(1)} %copy.10), channel_id=1, source_target_pairs={{1,0},{2,1},{3,2},{5,4},{6,5},{7,6},{9,8},{10,9},{11,10},{13,12},{... | collective-permute-start | bytes 1769480 | tf_op jit(solution)/shard_map/ppermute | solution.py:215
  78.9 0.8 copy-start.4
  80.4 70.0 %collective-permute-start.3 = (bf16[144,512]{1,0:T(8,128)(2,1)}, bf16[144,512]{1,0:T(8,128)(2,1)}, u32[]{:S(2)}, u32[]{:S(2)}) collective-permute-start(bf16[144,512]{1,0:T(8,128)(2,1)} %get-tuple-element.42), channel_id=1, source_target_pairs={{0,736},{8,744},{16,752},{24,760},{32,0},{40,8},{48,16},{56,24},{6... | collective-permute-start | bytes 442376 | tf_op jit(solution)/shard_map/ppermute | solution.py:30
  127.1 24.6 %collective-permute-start.2 = (bf16[144,512]{1,0:T(8,128)(2,1)}, bf16[144,512]{1,0:T(8,128)(2,1)}, u32[]{:S(2)}, u32[]{:S(2)}) collective-permute-start(bf16[144,512]{1,0:T(8,128)(2,1)} %get-tuple-element.41), channel_id=1, source_target_pairs={{0,760},{8,0},{16,8},{24,16},{32,24},{40,32},{48,40},{56,48},{64,5... | collective-permute-start | bytes 442376 | tf_op jit(solution)/shard_map/ppermute | solution.py:30
  142.5 8.0 %copy-start.5 = (bf16[576,512]{1,0:T(8,128)(2,1)S(1)}, bf16[576,512]{1,0:T(8,128)(2,1)}, u32[]{:S(2)}) copy-start(bf16[576,512]{1,0:T(8,128)(2,1)} %copy-done.4) | copy-start | bytes 1769476
  144.5 14.0 %all-to-all-start.1 = ((bf16[4,1,128,512]{3,2,1,0:T(8,128)(2,1)}), bf16[4,1,128,512]{3,2,1,0:T(8,128)(2,1)S(1)}, u32[]{:S(2)}, u32[]{:S(2)}) async-start(bf16[4,1,128,512]{3,2,1,0:T(8,128)(2,1)} %bitcast.8), calls=%async_computation.1 | async-start | bytes 1048576 | tf_op jit(solution)/shard_map/all_to_all | solution.py:180
  158.5 18.4 %all-to-all-start.3 = ((bf16[4,2,128,512]{3,2,1,0:T(8,128)(2,1)}), bf16[4,2,128,512]{3,2,1,0:T(8,128)(2,1)S(1)}, u32[]{:S(2)}, u32[]{:S(2)}) async-start(bf16[4,2,128,512]{3,2,1,0:T(8,128)(2,1)} %maximum_bitcast_fusion), calls=%async_computation.3 | async-start | bytes 2097152 | tf_op jit(solution)/shard_map/all_to_all | solution.py:180
  164.1 37.6 %copy-start.3 = (bf16[1,512,128]{2,1,0:T(8,128)(2,1)S(1)}, bf16[1,512,128]{2,1,0:T(8,128)(2,1)}, u32[]{:S(2)}) copy-start(bf16[1,512,128]{2,1,0:T(8,128)(2,1)} %param.8) | copy-start | bytes 393220
  164.2 15.1 %collective-permute-start.1 = (bf16[1,128,512]{2,1,0:T(8,128)(2,1)S(1)}, bf16[1,128,512]{2,1,0:T(8,128)(2,1)S(1)}, u32[]{:S(2)}, u32[]{:S(2)}) collective-permute-start(bf16[1,128,512]{2,1,0:T(8,128)(2,1)S(1)} %bitcast.98), channel_id=1, source_target_pairs={{0,4},{4,0},{1,5},{5,1},{2,6},{6,2},{3,7},{7,3},{8,12},{12,8},{9,1... | collective-permute-start | bytes 393224 | tf_op jit(solution)/shard_map/ppermute | solution.py:34
  177.2 16.9 %collective-permute-start.4 = (bf16[2,128,512]{2,1,0:T(8,128)(2,1)S(1)}, bf16[2,128,512]{2,1,0:T(8,128)(2,1)S(1)}, u32[]{:S(2)}, u32[]{:S(2)}) collective-permute-start(bf16[2,128,512]{2,1,0:T(8,128)(2,1)S(1)} %reduce_sum.77), channel_id=1, source_target_pairs={{0,4},{4,0},{1,5},{5,1},{2,6},{6,2},{3,7},{7,3},{8,12},{12,8},{9,1... | collective-permute-start | bytes 786440 | tf_op jit(solution)/shard_map/ppermute | solution.py:34
  180.2 14.0 %all-to-all-start.2 = ((bf16[4,1,128,512]{3,2,1,0:T(8,128)(2,1)}), bf16[4,1,128,512]{3,2,1,0:T(8,128)(2,1)S(1)}, u32[]{:S(2)}, u32[]{:S(2)}) async-start(bf16[4,1,128,512]{3,2,1,0:T(8,128)(2,1)} %broadcast_in_dim.44), calls=%async_computation.2 | async-start | bytes 1048576 | tf_op jit(solution)/shard_map/all_to_all | solution.py:192
  195.3 22.3 %all-to-all-start.4 = ((bf16[4,2,128,512]{3,2,1,0:T(8,128)(2,1)}), bf16[4,2,128,512]{3,2,1,0:T(8,128)(2,1)S(1)}, u32[]{:S(2)}, u32[]{:S(2)}) async-start(bf16[4,2,128,512]{3,2,1,0:T(8,128)(2,1)} %broadcast_in_dim.45), calls=%async_computation.4 | async-start | bytes 2097152 | tf_op jit(solution)/shard_map/all_to_all | solution.py:192
  201.7 13.6 %collective-permute-start.6 = (bf16[512,128]{1,0:T(8,128)(2,1)S(1)}, bf16[512,128]{1,0:T(8,128)(2,1)S(1)}, u32[]{:S(2)}, u32[]{:S(2)}) collective-permute-start(bf16[512,128]{1,0:T(8,128)(2,1)S(1)} %bitcast.96), channel_id=1, source_target_pairs={{0,736},{8,744},{16,752},{24,760},{32,0},{40,8},{48,16},{56,24},{6... | collective-permute-start | bytes 393224 | tf_op jit(solution)/shard_map/ppermute | solution.py:30
  212.8 4.4 %collective-permute-start.5 = (bf16[512,128]{1,0:T(8,128)(2,1)S(1)}, bf16[512,128]{1,0:T(8,128)(2,1)S(1)}, u32[]{:S(2)}, u32[]{:S(2)}) collective-permute-start(bf16[512,128]{1,0:T(8,128)(2,1)S(1)} %bitcast.97), channel_id=1, source_target_pairs={{0,760},{8,0},{16,8},{24,16},{32,24},{40,32},{48,40},{56,48},{64,5... | collective-permute-start | bytes 393224 | tf_op jit(solution)/shard_map/ppermute | solution.py:30
  218.0 18.8 %collective-permute-start.8 = (bf16[512,128]{1,0:T(8,128)(2,1)S(1)}, bf16[512,128]{1,0:T(8,128)(2,1)S(1)}, u32[]{:S(2)}, u32[]{:S(2)}) collective-permute-start(bf16[512,128]{1,0:T(8,128)(2,1)S(1)} %convolution_convert_fusion.4), channel_id=1, source_target_pairs={{0,32},{8,40},{16,48},{24,56},{32,64},{40,72},{48,80},{56,88},{64,... | collective-permute-start | bytes 393224 | tf_op jit(solution)/shard_map/ppermute | solution.py:30
  220.3 17.2 %collective-permute-start.7 = (bf16[512,128]{1,0:T(8,128)(2,1)S(1)}, bf16[512,128]{1,0:T(8,128)(2,1)S(1)}, u32[]{:S(2)}, u32[]{:S(2)}) collective-permute-start(bf16[512,128]{1,0:T(8,128)(2,1)S(1)} %convolution_convert_fusion.5), channel_id=1, source_target_pairs={{0,8},{8,16},{16,24},{24,32},{32,40},{40,48},{48,56},{56,64},{64,7... | collective-permute-start | bytes 393224 | tf_op jit(solution)/shard_map/ppermute | solution.py:30
  238.5 9.4 %collective-permute-start.9 = (bf16[512,128]{1,0:T(8,128)(2,1)S(1)}, bf16[512,128]{1,0:T(8,128)(2,1)S(1)}, u32[]{:S(2)}, u32[]{:S(2)}) collective-permute-start(bf16[512,128]{1,0:T(8,128)(2,1)S(1)} %get-tuple-element.53), channel_id=1, source_target_pairs={{0,8},{16,24},{32,40},{48,56},{64,72},{80,88},{96,104},{112,120},{... | collective-permute-start | bytes 393224 | tf_op jit(solution)/shard_map/ppermute | solution.py:144
  240.4 13.2 %collective-permute-start.10 = (bf16[512,128]{1,0:T(8,128)(2,1)S(1)}, bf16[512,128]{1,0:T(8,128)(2,1)S(1)}, u32[]{:S(2)}, u32[]{:S(2)}) collective-permute-start(bf16[512,128]{1,0:T(8,128)(2,1)S(1)} %get-tuple-element.54), channel_id=1, source_target_pairs={{8,16},{24,32},{40,48},{56,64},{72,80},{88,96},{104,112},{120,128}... | collective-permute-start | bytes 393224 | tf_op jit(solution)/shard_map/ppermute | solution.py:144
  242.5 17.3 %collective-permute-start.12 = (bf16[512,128]{1,0:T(8,128)(2,1)S(1)}, bf16[512,128]{1,0:T(8,128)(2,1)S(1)}, u32[]{:S(2)}, u32[]{:S(2)}) collective-permute-start(bf16[512,128]{1,0:T(8,128)(2,1)S(1)} %get-tuple-element.48), channel_id=1, source_target_pairs={{32,64},{40,72},{48,80},{56,88},{96,128},{104,136},{112,144},{120,... | collective-permute-start | bytes 393224 | tf_op jit(solution)/shard_map/ppermute | solution.py:144
  245.6 14.1 %collective-permute-start.11 = (bf16[512,128]{1,0:T(8,128)(2,1)S(1)}, bf16[512,128]{1,0:T(8,128)(2,1)S(1)}, u32[]{:S(2)}, u32[]{:S(2)}) collective-permute-start(bf16[512,128]{1,0:T(8,128)(2,1)S(1)} %get-tuple-element.47), channel_id=1, source_target_pairs={{0,32},{8,40},{16,48},{24,56},{64,96},{72,104},{80,112},{88,120},{... | collective-permute-start | bytes 393224 | tf_op jit(solution)/shard_map/ppermute | solution.py:144
  260.8 20.2 %collective-permute-start.16 = (bf16[512,128]{1,0:T(8,128)(2,1)S(1)}, bf16[512,128]{1,0:T(8,128)(2,1)S(1)}, u32[]{:S(2)}, u32[]{:S(2)}) collective-permute-start(bf16[512,128]{1,0:T(8,128)(2,1)S(1)} %get-tuple-element.44), channel_id=1, source_target_pairs={{32,64},{40,72},{48,80},{56,88},{96,128},{104,136},{112,144},{120,... | collective-permute-start | bytes 393224 | tf_op jit(solution)/shard_map/ppermute | solution.py:144
  265.6 15.5 %collective-permute-start.15 = (bf16[512,128]{1,0:T(8,128)(2,1)S(1)}, bf16[512,128]{1,0:T(8,128)(2,1)S(1)}, u32[]{:S(2)}, u32[]{:S(2)}) collective-permute-start(bf16[512,128]{1,0:T(8,128)(2,1)S(1)} %get-tuple-element.43), channel_id=1, source_target_pairs={{0,32},{8,40},{16,48},{24,56},{64,96},{72,104},{80,112},{88,120},{... | collective-permute-start | bytes 393224 | tf_op jit(solution)/shard_map/ppermute | solution.py:144
  267.5 13.2 %collective-permute-start.14 = (bf16[512,128]{1,0:T(8,128)(2,1)S(1)}, bf16[512,128]{1,0:T(8,128)(2,1)S(1)}, u32[]{:S(2)}, u32[]{:S(2)}) collective-permute-start(bf16[512,128]{1,0:T(8,128)(2,1)S(1)} %get-tuple-element.52), channel_id=1, source_target_pairs={{8,16},{24,32},{40,48},{56,64},{72,80},{88,96},{104,112},{120,128}... | collective-permute-start | bytes 393224 | tf_op jit(solution)/shard_map/ppermute | solution.py:144
  275.6 5.1 %collective-permute-start.13 = (bf16[512,128]{1,0:T(8,128)(2,1)S(1)}, bf16[512,128]{1,0:T(8,128)(2,1)S(1)}, u32[]{:S(2)}, u32[]{:S(2)}) collective-permute-start(bf16[512,128]{1,0:T(8,128)(2,1)S(1)} %get-tuple-element.51), channel_id=1, source_target_pairs={{0,8},{16,24},{32,40},{48,56},{64,72},{80,88},{96,104},{112,120},{... | collective-permute-start | bytes 393224 | tf_op jit(solution)/shard_map/ppermute | solution.py:144

commit v5 on v4

--- a/solution.py
+++ b/solution.py
@@ -215,22 +215,20 @@
     above = lax.ppermute(
         rows[:, :PLANE], "slab", [(i + 1, i) for i in range(SLABS - 1)]
     )
-    faces = transposed_dot(face_selector(planes, rows.shape[1]), rows, 1, 1)
+    padded = jnp.pad(rows[:, :length].astype(jnp.float32), ((0, 0), (PLANE, PLANE)))
+    applied = flat_hamiltonian(padded, length, slab_potential, side_masks(length))
+    last = rows[:, length - PLANE : length]
+    edges = rows[:, length:]
+    swapped_edges = jnp.roll(edges, edges.shape[1] // 2, axis=1)
+    h_self = transposed_dot(rows[:, :length], applied.astype(jnp.bfloat16), 1, 1)
+    h_self = h_self - transposed_dot(edges, swapped_edges, 1, 1)
+    h_self = h_self - transposed_dot(last, above, 1, 1) - transposed_dot(above, last, 1, 1)
+
+    faces = transposed_dot(face_selector(planes, length), rows[:, :length], 1, 1)
     faces = faces.astype(jnp.bfloat16)
     width = 2 * planes * P_SIZE
     other_z = from_behind(faces[:width], "elem", -1)
     other_y = from_behind(faces[width : 2 * width], "elem", -EB)
-
-    padded = jnp.pad(rows[:, :length].astype(jnp.float32), ((0, 0), (PLANE, PLANE)))
-    applied = flat_hamiltonian(padded, length, slab_potential, side_masks(length))
-    last = rows[:, length - PLANE : length]
-    piece = (rows.shape[1] - length) // 2
-    below_part, above_part = rows[:, length : length + piece], rows[:, length + piece :]
-    applied = jnp.concatenate(
-        [applied.astype(jnp.bfloat16), -above_part, -below_part], axis=1
-    )
-    h_self = transposed_dot(rows, applied, 1, 1)
-    h_self = h_self - transposed_dot(last, above, 1, 1) - transposed_dot(above, last, 1, 1)
     weight = -0.5 / PLANE
     h_z = transposed_dot(faces[2 * width : 3 * width], other_z, 0, 0) * weight
     h_y = transposed_dot(faces[3 * width :], other_y, 0, 0) * weight

time: 283 us -> 294 us (1.039)
  waiting for transfers between devices: 86.3 us -> 98.9 us
  matrix products: 13.6 us -> 26.1 us
  other arithmetic: 32.1 us -> 25.4 us
  local copies, waits for them, and re-layouts: 7.86 us -> 2.6 us
    dot_general x21 -> x22, matrix products: 13.6 us -> 26.1 us  [transposed_dot(): lax.dot_general(a, b, (((contract_a,), (contract_b,)), ((), ())), preferr...]
    ppermute x8, waiting for transfers between devices: 14.5 us -> 23.6 us  [pair_swap(): return lax.ppermute(value, 'elem', pairs + [(j, i) for i, j in pairs])]
    convert_element_type x1 -> x0, other arithmetic: 6.53 us -> none  [device_body(): applied.astype(jnp.bfloat16)]
    ppermute x6, waiting for transfers between devices: 16.6 us -> 20.9 us  [from_behind(): lax.ppermute(value, axis, [(i, (i + by) % devices) for i in range(devices)])]
    concatenate x1 -> x0, local copies, waits for them, and re-layouts: 3.88 us -> none  [device_body(): jnp.concatenate([applied.astype(jnp.bfloat16), -above_part, -below_part],...]
  transfers between devices with their start and end apart: 22 -> 22, of which waited for: 11 -> 13; matrix products, arithmetic and copies ran while one was open for 9% -> 9% of each run, Pallas kernels for 0% -> 0%
where the time goes in v5:
time: 294 us; the launch traced here: 293 us
  starting transfers between devices  137 us (47%)
  waiting for transfers between devices  98.9 us (34%)
  matrix products  26.1 us (9%)
  other arithmetic  25.4 us (9%)
    ppermute x6, starting transfers between devices, from_behind(): lax.ppermute(value, axis, [(i, (i + by) % devices) for i in range(devices)])  64.9 us
    all_to_all x1, waiting for transfers between devices, slab_rows(): rows = lax.all_to_all(slabs, BOTH, 0, 0, tiled=True)  31.9 us
    dot_general x22, matrix products, transposed_dot(): lax.dot_general(a, b, (((contract_a,), (contract_b,)), ((), ())), preferr...  26.1 us
    ppermute x8, starting transfers between devices, pair_swap(): return lax.ppermute(value, 'elem', pairs + [(j, i) for i, j in pairs])  25.8 us
    ppermute x8, waiting for transfers between devices, pair_swap(): return lax.ppermute(value, 'elem', pairs + [(j, i) for i, j in pairs])  23.6 us
    ppermute x6, waiting for transfers between devices, from_behind(): lax.ppermute(value, axis, [(i, (i + by) % devices) for i in range(devices)])  20.9 us
    all_to_all x1, starting transfers between devices, slab_rows(): rows = lax.all_to_all(slabs, BOTH, 0, 0, tiled=True)  17.4 us
    all_to_all x2, waiting for transfers between devices, sum_over_slabs(): pieces = lax.all_to_all(slices_of(partial), 'slab', 0, 0, tiled=True)  13.8 us
  transfers between devices with their start and end apart: 22, of which 13 were waited for; matrix products, arithmetic and copies ran while one was open for 9% of the time, Pallas kernels for 0%

profile of v5, /device:TPU:6, one launch (start us, length us, event | category | flops | bytes accessed | tf_op | source)
XLA Modules:
  0.0 293.1 jit_solution(13067702398790851916)
XLA Ops:
  0.1 2.8 slice_bitcast_fusion
  3.0 4.7 %broadcast_multiply_fusion.3 = (f32[16,13824]{1,0:T(8,128)S(1)}, f32[16,13824]{1,0:T(8,128)S(1)}) fusion(f32[13824]{0:T(1024)S(1)} %reduce.3, f32[13824]{0:T(1024)S(1)} %get-tuple-element.59, f32[13824]{0:T(1024)S(1)} %get-tuple-element.60, f32[13824]{0:T(1024)S(1)} %get-tuple-element.58, f32[13824]{0:T(1024)S(1)} %get-tuple-element.57, ...), kind=kLoop, calls=%fused_computation.152 | loop fusion | flops 3760128 | bytes 3373056 | tf_op jit(solution)/shard_map/div | solution.py:68
  7.8 2.5 multiply_reduce_fusion.3
  10.9 1.3 select_convert_fusion.3.refs_0_
  12.3 1.4 broadcast_multiply_fusion.2
  13.7 1.5 multiply_reduce_fusion.2
  15.5 1.4 broadcast_multiply_fusion.1
  17.0 1.5 multiply_reduce_fusion.1
  18.8 1.4 broadcast_multiply_fusion
  20.2 1.5 multiply_reduce_fusion
  21.9 1.9 shard_map.55
  23.8 17.4 %all-to-all-start = ((bf16[8,64,1872]{2,1,0:T(8,128)(2,1)}), bf16[8,64,1872]{2,1,0:T(8,128)(2,1)S(1)}, u32[]{:S(2)}, u32[]{:S(2)}) async-start(bf16[8,64,1872]{2,1,0:T(8,128)(2,1)} %shard_map.55), calls=%async_computation | async-start | bytes 3932160 | tf_op jit(solution)/shard_map/all_to_all | solution.py:136
  41.4 31.9 %all-to-all-done = bf16[8,64,1872]{2,1,0:T(8,128)(2,1)S(1)} async-done(((bf16[8,64,1872]{2,1,0:T(8,128)(2,1)}), bf16[8,64,1872]{2,1,0:T(8,128)(2,1)S(1)}, u32[]{:S(2)}, u32[]{:S(2)}) %all-to-all-start) | async-done | bytes 1916960 | tf_op jit(solution)/shard_map/all_to_all | solution.py:136
  73.3 2.0 slice_convert_fusion
  75.4 1.3 fusion.20
  76.7 27.3 %collective-permute-start.2 = (bf16[144,512]{1,0:T(8,128)(2,1)S(1)}, bf16[144,512]{1,0:T(8,128)(2,1)}, u32[]{:S(2)}, u32[]{:S(2)}) collective-permute-start(bf16[144,512]{1,0:T(8,128)(2,1)S(1)} %get-tuple-element.41), channel_id=1, source_target_pairs={{0,760},{8,0},{16,8},{24,16},{32,24},{40,32},{48,40},{56,48},{64,5... | collective-permute-start | bytes 442376 | tf_op jit(solution)/shard_map/ppermute | solution.py:30
  104.1 21.5 %collective-permute-start.3 = (bf16[144,512]{1,0:T(8,128)(2,1)S(1)}, bf16[144,512]{1,0:T(8,128)(2,1)}, u32[]{:S(2)}, u32[]{:S(2)}) collective-permute-start(bf16[144,512]{1,0:T(8,128)(2,1)S(1)} %get-tuple-element.42), channel_id=1, source_target_pairs={{0,736},{8,744},{16,752},{24,760},{32,0},{40,8},{48,16},{56,24},{6... | collective-permute-start | bytes 442376 | tf_op jit(solution)/shard_map/ppermute | solution.py:30
  125.8 1.3 collective-permute-start
  127.1 15.1 %fusion.14 = f32[512,512]{1,0:T(8,128)S(1)} fusion(f32[512,1728]{1,0:T(8,128)} %slice_convert_fusion, f32[1728]{0:T(1024)S(1)} %dynamic-slice_reduce_fusion, f32[1728]{0:T(1024)S(1)} %get-tuple-element.67, f32[1728]{0:T(1024)S(1)} %get-tuple-element.68, f32[1728]{0:T(1024)S(1)} %get-tuple-element.66, f32[1728]{0:T(1024)S(1)} %get-tuple-element.65, ...), kind=kOutput, calls=%fused_computation.21 | convolution fusion | flops 918355968 | bytes 6463488 | tf_op jit(solution)/shard_map/dot_general | solution.py:90
  142.4 0.4 convolution_subtract_fusion.1
  142.9 0.6 fusion.75
  143.5 1.4 fusion.25
  144.9 5.9 %all-to-all-start.1 = ((bf16[4,1,128,512]{3,2,1,0:T(8,128)(2,1)}), bf16[4,1,128,512]{3,2,1,0:T(8,128)(2,1)S(1)}, u32[]{:S(2)}, u32[]{:S(2)}) async-start(bf16[4,1,128,512]{3,2,1,0:T(8,128)(2,1)} %bitcast.8), calls=%async_computation.1 | async-start | bytes 1048576 | tf_op jit(solution)/shard_map/all_to_all | solution.py:180
  150.8 1.2 fusion.23
  152.1 1.2 fusion.24
  153.3 1.1 maximum_bitcast_fusion
  154.4 3.9 %all-to-all-done.1 = bf16[4,1,128,512]{3,2,1,0:T(8,128)(2,1)S(1)} async-done(((bf16[4,1,128,512]{3,2,1,0:T(8,128)(2,1)}), bf16[4,1,128,512]{3,2,1,0:T(8,128)(2,1)S(1)}, u32[]{:S(2)}, u32[]{:S(2)}) %all-to-all-start.1) | async-done | bytes 524320 | tf_op jit(solution)/shard_map/all_to_all | solution.py:180
  158.3 5.6 %all-to-all-start.3 = ((bf16[4,2,128,512]{3,2,1,0:T(8,128)(2,1)}), bf16[4,2,128,512]{3,2,1,0:T(8,128)(2,1)S(1)}, u32[]{:S(2)}, u32[]{:S(2)}) async-start(bf16[4,2,128,512]{3,2,1,0:T(8,128)(2,1)} %maximum_bitcast_fusion), calls=%async_computation.3 | async-start | bytes 2097152 | tf_op jit(solution)/shard_map/all_to_all | solution.py:180
  164.0 2.3 collective-permute-start.1
  166.3 9.9 %all-to-all-done.3 = bf16[4,2,128,512]{3,2,1,0:T(8,128)(2,1)S(1)} async-done(((bf16[4,2,128,512]{3,2,1,0:T(8,128)(2,1)}), bf16[4,2,128,512]{3,2,1,0:T(8,128)(2,1)S(1)}, u32[]{:S(2)}, u32[]{:S(2)}) %all-to-all-start.3) | async-done | bytes 1048608 | tf_op jit(solution)/shard_map/all_to_all | solution.py:180
  176.4 2.1 collective-permute-start.4
  178.6 0.9 broadcast_in_dim.44
  179.5 5.5 %all-to-all-start.2 = ((bf16[4,1,128,512]{3,2,1,0:T(8,128)(2,1)}), bf16[4,1,128,512]{3,2,1,0:T(8,128)(2,1)S(1)}, u32[]{:S(2)}, u32[]{:S(2)}) async-start(bf16[4,1,128,512]{3,2,1,0:T(8,128)(2,1)} %broadcast_in_dim.44), calls=%async_computation.2 | async-start | bytes 1048576 | tf_op jit(solution)/shard_map/all_to_all | solution.py:192
  185.0 8.8 %collective-permute-done.4 = bf16[2,128,512]{2,1,0:T(8,128)(2,1)S(1)} collective-permute-done((bf16[2,128,512]{2,1,0:T(8,128)(2,1)S(1)}, bf16[2,128,512]{2,1,0:T(8,128)(2,1)S(1)}, u32[]{:S(2)}, u32[]{:S(2)}) %collective-permute-start.4) | collective-permute-done | bytes 262176 | tf_op jit(solution)/shard_map/ppermute | solution.py:34
  193.8 1.1 broadcast_in_dim.45
  194.9 6.1 %all-to-all-start.4 = ((bf16[4,2,128,512]{3,2,1,0:T(8,128)(2,1)}), bf16[4,2,128,512]{3,2,1,0:T(8,128)(2,1)S(1)}, u32[]{:S(2)}, u32[]{:S(2)}) async-start(bf16[4,2,128,512]{3,2,1,0:T(8,128)(2,1)} %broadcast_in_dim.45), calls=%async_computation.4 | async-start | bytes 2097152 | tf_op jit(solution)/shard_map/all_to_all | solution.py:192
  201.0 4.7 %collective-permute-start.5 = (bf16[512,128]{1,0:T(8,128)(2,1)S(1)}, bf16[512,128]{1,0:T(8,128)(2,1)S(1)}, u32[]{:S(2)}, u32[]{:S(2)}) collective-permute-start(bf16[512,128]{1,0:T(8,128)(2,1)S(1)} %bitcast.94), channel_id=1, source_target_pairs={{0,760},{8,0},{16,8},{24,16},{32,24},{40,32},{48,40},{56,48},{64,5... | collective-permute-start | bytes 393224 | tf_op jit(solution)/shard_map/ppermute | solution.py:30
  205.7 7.5 %collective-permute-start.6 = (bf16[512,128]{1,0:T(8,128)(2,1)S(1)}, bf16[512,128]{1,0:T(8,128)(2,1)S(1)}, u32[]{:S(2)}, u32[]{:S(2)}) collective-permute-start(bf16[512,128]{1,0:T(8,128)(2,1)S(1)} %bitcast.95), channel_id=1, source_target_pairs={{0,736},{8,744},{16,752},{24,760},{32,0},{40,8},{48,16},{56,24},{6... | collective-permute-start | bytes 393224 | tf_op jit(solution)/shard_map/ppermute | solution.py:30
  213.3 3.3 %collective-permute-done.6 = bf16[512,128]{1,0:T(8,128)(2,1)S(1)} collective-permute-done((bf16[512,128]{1,0:T(8,128)(2,1)S(1)}, bf16[512,128]{1,0:T(8,128)(2,1)S(1)}, u32[]{:S(2)}, u32[]{:S(2)}) %collective-permute-start.6) | collective-permute-done | bytes 131104 | tf_op jit(solution)/shard_map/ppermute | solution.py:30
  217.0 0.3 convolution_convert_fusion.5
  217.4 1.9 collective-permute-start.7
  219.3 0.3 convolution_convert_fusion.4
  219.7 1.9 collective-permute-start.8
  221.9 10.8 %collective-permute-done.7 = bf16[512,128]{1,0:T(8,128)(2,1)S(1)} collective-permute-done((bf16[512,128]{1,0:T(8,128)(2,1)S(1)}, bf16[512,128]{1,0:T(8,128)(2,1)S(1)}, u32[]{:S(2)}, u32[]{:S(2)}) %collective-permute-start.7) | collective-permute-done | bytes 131104 | tf_op jit(solution)/shard_map/ppermute | solution.py:30
  232.7 6.7 %collective-permute-done.8 = bf16[512,128]{1,0:T(8,128)(2,1)S(1)} collective-permute-done((bf16[512,128]{1,0:T(8,128)(2,1)S(1)}, bf16[512,128]{1,0:T(8,128)(2,1)S(1)}, u32[]{:S(2)}, u32[]{:S(2)}) %collective-permute-start.8) | collective-permute-done | bytes 131104 | tf_op jit(solution)/shard_map/ppermute | solution.py:30
  239.8 0.4 convolution_convert_fusion.3
  240.1 0.4 broadcast_select_fusion.3
  240.5 3.9 %collective-permute-start.10 = (bf16[512,128]{1,0:T(8,128)(2,1)S(1)}, bf16[512,128]{1,0:T(8,128)(2,1)S(1)}, u32[]{:S(2)}, u32[]{:S(2)}) collective-permute-start(bf16[512,128]{1,0:T(8,128)(2,1)S(1)} %get-tuple-element.54), channel_id=1, source_target_pairs={{8,16},{24,32},{40,48},{56,64},{72,80},{88,96},{104,112},{120,128}... | collective-permute-start | bytes 393224 | tf_op jit(solution)/shard_map/ppermute | solution.py:144
  244.4 1.9 collective-permute-start.9
  246.3 1.9 collective-permute-start.11
  248.3 4.4 %collective-permute-start.12 = (bf16[512,128]{1,0:T(8,128)(2,1)S(1)}, bf16[512,128]{1,0:T(8,128)(2,1)S(1)}, u32[]{:S(2)}, u32[]{:S(2)}) collective-permute-start(bf16[512,128]{1,0:T(8,128)(2,1)S(1)} %get-tuple-element.48), channel_id=1, source_target_pairs={{32,64},{40,72},{48,80},{56,88},{96,128},{104,136},{112,144},{120,... | collective-permute-start | bytes 393224 | tf_op jit(solution)/shard_map/ppermute | solution.py:144
  253.0 0.7 collective-permute-done.10
  254.0 2.8 collective-permute-done.11
  256.8 7.9 %collective-permute-done.12 = bf16[512,128]{1,0:T(8,128)(2,1)S(1)} collective-permute-done((bf16[512,128]{1,0:T(8,128)(2,1)S(1)}, bf16[512,128]{1,0:T(8,128)(2,1)S(1)}, u32[]{:S(2)}, u32[]{:S(2)}) %collective-permute-start.12) | collective-permute-done | bytes 131104 | tf_op jit(solution)/shard_map/ppermute | solution.py:144
  265.0 0.3 convolution_convert_fusion.1
  265.4 0.3 broadcast_select_fusion.1
  265.7 1.9 collective-permute-start.13
  267.7 7.8 %collective-permute-start.14 = (bf16[512,128]{1,0:T(8,128)(2,1)S(1)}, bf16[512,128]{1,0:T(8,128)(2,1)S(1)}, u32[]{:S(2)}, u32[]{:S(2)}) collective-permute-start(bf16[512,128]{1,0:T(8,128)(2,1)S(1)} %get-tuple-element.52), channel_id=1, source_target_pairs={{8,16},{24,32},{40,48},{56,64},{72,80},{88,96},{104,112},{120,128}... | collective-permute-start | bytes 393224 | tf_op jit(solution)/shard_map/ppermute | solution.py:144
  275.5 1.9 collective-permute-start.15
  277.4 1.9 collective-permute-start.16
  279.6 1.2 collective-permute-done.14
  281.2 2.1 collective-permute-done.15
  283.2 8.8 %collective-permute-done.16 = bf16[512,128]{1,0:T(8,128)(2,1)S(1)} collective-permute-done((bf16[512,128]{1,0:T(8,128)(2,1)S(1)}, bf16[512,128]{1,0:T(8,128)(2,1)S(1)}, u32[]{:S(2)}, u32[]{:S(2)}) %collective-permute-start.16) | collective-permute-done | bytes 131104 | tf_op jit(solution)/shard_map/ppermute | solution.py:144
  292.4 0.7 fusion.91
  (62 shorter events, 4.8 us)
Async XLA Ops:
  0.0 3.0 %copy-start = (bf16[1,64,13824]{2,1,0:T(8,128)(2,1)S(1)}, bf16[1,64,13824]{2,1,0:T(8,128)(2,1)}, u32[]{:S(2)}) copy-start(bf16[1,64,13824]{2,1,0:T(8,128)(2,1)} %param.5) | copy-start | bytes 5308420
  0.0 2.9 copy-start.5
  12.3 3.2 %copy-start.1 = (bf16[16,13824]{1,0:T(8,128)(2,1)S(1)}, bf16[16,13824]{1,0:T(8,128)(2,1)}, u32[]{:S(2)}) copy-start(bf16[16,13824]{1,0:T(8,128)(2,1)} %get-tuple-element.14) | copy-start | bytes 1327108
  23.8 49.5 %all-to-all-start = ((bf16[8,64,1872]{2,1,0:T(8,128)(2,1)}), bf16[8,64,1872]{2,1,0:T(8,128)(2,1)S(1)}, u32[]{:S(2)}, u32[]{:S(2)}) async-start(bf16[8,64,1872]{2,1,0:T(8,128)(2,1)} %shard_map.55), calls=%async_computation | async-start | bytes 3932160 | tf_op jit(solution)/shard_map/all_to_all | solution.py:136
  41.3 34.1 %copy-start.6 = (s32[576]{0:T(1024)S(1)}, s32[576]{0:T(1024)}, u32[]{:S(2)}) copy-start(s32[576]{0:T(1024)} %constant.203.clone) | copy-start | bytes 6916
  76.7 27.4 %copy-start.3 = (bf16[576,512]{1,0:T(8,128)(2,1)}, bf16[576,512]{1,0:T(8,128)(2,1)S(1)}, u32[]{:S(2)}) copy-start(bf16[576,512]{1,0:T(8,128)(2,1)S(1)} %fusion.20) | copy-start | bytes 1769476
  76.7 74.1 %collective-permute-start.2 = (bf16[144,512]{1,0:T(8,128)(2,1)S(1)}, bf16[144,512]{1,0:T(8,128)(2,1)}, u32[]{:S(2)}, u32[]{:S(2)}) collective-permute-start(bf16[144,512]{1,0:T(8,128)(2,1)S(1)} %get-tuple-element.41), channel_id=1, source_target_pairs={{0,760},{8,0},{16,8},{24,16},{32,24},{40,32},{48,40},{56,48},{64,5... | collective-permute-start | bytes 442376 | tf_op jit(solution)/shard_map/ppermute | solution.py:30
  104.1 48.0 %collective-permute-start.3 = (bf16[144,512]{1,0:T(8,128)(2,1)S(1)}, bf16[144,512]{1,0:T(8,128)(2,1)}, u32[]{:S(2)}, u32[]{:S(2)}) collective-permute-start(bf16[144,512]{1,0:T(8,128)(2,1)S(1)} %get-tuple-element.42), channel_id=1, source_target_pairs={{0,736},{8,744},{16,752},{24,760},{32,0},{40,8},{48,16},{56,24},{6... | collective-permute-start | bytes 442376 | tf_op jit(solution)/shard_map/ppermute | solution.py:30
  125.8 17.1 %collective-permute-start = (bf16[512,576]{0,1:T(8,128)(2,1)S(1)}, bf16[512,576]{0,1:T(8,128)(2,1)S(1)}, u32[]{:S(2)}, u32[]{:S(2)}) collective-permute-start(bf16[512,576]{0,1:T(8,128)(2,1)S(1)} %copy.10), channel_id=1, source_target_pairs={{1,0},{2,1},{3,2},{5,4},{6,5},{7,6},{9,8},{10,9},{11,10},{13,12},{... | collective-permute-start | bytes 1769480 | tf_op jit(solution)/shard_map/ppermute | solution.py:215
  142.9 8.0 %copy-start.4 = (bf16[576,512]{1,0:T(8,128)(2,1)S(1)}, bf16[576,512]{1,0:T(8,128)(2,1)}, u32[]{:S(2)}) copy-start(bf16[576,512]{1,0:T(8,128)(2,1)} %copy-done.3) | copy-start | bytes 1769476
  144.9 13.5 %all-to-all-start.1 = ((bf16[4,1,128,512]{3,2,1,0:T(8,128)(2,1)}), bf16[4,1,128,512]{3,2,1,0:T(8,128)(2,1)S(1)}, u32[]{:S(2)}, u32[]{:S(2)}) async-start(bf16[4,1,128,512]{3,2,1,0:T(8,128)(2,1)} %bitcast.8), calls=%async_computation.1 | async-start | bytes 1048576 | tf_op jit(solution)/shard_map/all_to_all | solution.py:180
  158.3 17.8 %all-to-all-start.3 = ((bf16[4,2,128,512]{3,2,1,0:T(8,128)(2,1)}), bf16[4,2,128,512]{3,2,1,0:T(8,128)(2,1)S(1)}, u32[]{:S(2)}, u32[]{:S(2)}) async-start(bf16[4,2,128,512]{3,2,1,0:T(8,128)(2,1)} %maximum_bitcast_fusion), calls=%async_computation.3 | async-start | bytes 2097152 | tf_op jit(solution)/shard_map/all_to_all | solution.py:180
  164.0 37.0 %copy-start.2 = (bf16[1,512,128]{2,1,0:T(8,128)(2,1)S(1)}, bf16[1,512,128]{2,1,0:T(8,128)(2,1)}, u32[]{:S(2)}) copy-start(bf16[1,512,128]{2,1,0:T(8,128)(2,1)} %param.8) | copy-start | bytes 393220
  164.0 14.6 %collective-permute-start.1 = (bf16[1,128,512]{2,1,0:T(8,128)(2,1)S(1)}, bf16[1,128,512]{2,1,0:T(8,128)(2,1)S(1)}, u32[]{:S(2)}, u32[]{:S(2)}) collective-permute-start(bf16[1,128,512]{2,1,0:T(8,128)(2,1)S(1)} %bitcast.96), channel_id=1, source_target_pairs={{0,4},{4,0},{1,5},{5,1},{2,6},{6,2},{3,7},{7,3},{8,12},{12,8},{9,1... | collective-permute-start | bytes 393224 | tf_op jit(solution)/shard_map/ppermute | solution.py:34
  176.4 17.3 %collective-permute-start.4 = (bf16[2,128,512]{2,1,0:T(8,128)(2,1)S(1)}, bf16[2,128,512]{2,1,0:T(8,128)(2,1)S(1)}, u32[]{:S(2)}, u32[]{:S(2)}) collective-permute-start(bf16[2,128,512]{2,1,0:T(8,128)(2,1)S(1)} %reduce_sum.77), channel_id=1, source_target_pairs={{0,4},{4,0},{1,5},{5,1},{2,6},{6,2},{3,7},{7,3},{8,12},{12,8},{9,1... | collective-permute-start | bytes 786440 | tf_op jit(solution)/shard_map/ppermute | solution.py:34
  179.5 14.4 %all-to-all-start.2 = ((bf16[4,1,128,512]{3,2,1,0:T(8,128)(2,1)}), bf16[4,1,128,512]{3,2,1,0:T(8,128)(2,1)S(1)}, u32[]{:S(2)}, u32[]{:S(2)}) async-start(bf16[4,1,128,512]{3,2,1,0:T(8,128)(2,1)} %broadcast_in_dim.44), calls=%async_computation.2 | async-start | bytes 1048576 | tf_op jit(solution)/shard_map/all_to_all | solution.py:192
  194.9 22.0 %all-to-all-start.4 = ((bf16[4,2,128,512]{3,2,1,0:T(8,128)(2,1)}), bf16[4,2,128,512]{3,2,1,0:T(8,128)(2,1)S(1)}, u32[]{:S(2)}, u32[]{:S(2)}) async-start(bf16[4,2,128,512]{3,2,1,0:T(8,128)(2,1)} %broadcast_in_dim.45), calls=%async_computation.4 | async-start | bytes 2097152 | tf_op jit(solution)/shard_map/all_to_all | solution.py:192
  201.0 12.3 %collective-permute-start.5 = (bf16[512,128]{1,0:T(8,128)(2,1)S(1)}, bf16[512,128]{1,0:T(8,128)(2,1)S(1)}, u32[]{:S(2)}, u32[]{:S(2)}) collective-permute-start(bf16[512,128]{1,0:T(8,128)(2,1)S(1)} %bitcast.94), channel_id=1, source_target_pairs={{0,760},{8,0},{16,8},{24,16},{32,24},{40,32},{48,40},{56,48},{64,5... | collective-permute-start | bytes 393224 | tf_op jit(solution)/shard_map/ppermute | solution.py:30
  205.7 10.9 %collective-permute-start.6 = (bf16[512,128]{1,0:T(8,128)(2,1)S(1)}, bf16[512,128]{1,0:T(8,128)(2,1)S(1)}, u32[]{:S(2)}, u32[]{:S(2)}) collective-permute-start(bf16[512,128]{1,0:T(8,128)(2,1)S(1)} %bitcast.95), channel_id=1, source_target_pairs={{0,736},{8,744},{16,752},{24,760},{32,0},{40,8},{48,16},{56,24},{6... | collective-permute-start | bytes 393224 | tf_op jit(solution)/shard_map/ppermute | solution.py:30
  217.4 15.3 %collective-permute-start.7 = (bf16[512,128]{1,0:T(8,128)(2,1)S(1)}, bf16[512,128]{1,0:T(8,128)(2,1)S(1)}, u32[]{:S(2)}, u32[]{:S(2)}) collective-permute-start(bf16[512,128]{1,0:T(8,128)(2,1)S(1)} %convolution_convert_fusion.5), channel_id=1, source_target_pairs={{0,8},{8,16},{16,24},{24,32},{32,40},{40,48},{48,56},{56,64},{64,7... | collective-permute-start | bytes 393224 | tf_op jit(solution)/shard_map/ppermute | solution.py:30
  219.7 19.8 %collective-permute-start.8 = (bf16[512,128]{1,0:T(8,128)(2,1)S(1)}, bf16[512,128]{1,0:T(8,128)(2,1)S(1)}, u32[]{:S(2)}, u32[]{:S(2)}) collective-permute-start(bf16[512,128]{1,0:T(8,128)(2,1)S(1)} %convolution_convert_fusion.4), channel_id=1, source_target_pairs={{0,32},{8,40},{16,48},{24,56},{32,64},{40,72},{48,80},{56,88},{64,... | collective-permute-start | bytes 393224 | tf_op jit(solution)/shard_map/ppermute | solution.py:30
  240.5 13.2 %collective-permute-start.10 = (bf16[512,128]{1,0:T(8,128)(2,1)S(1)}, bf16[512,128]{1,0:T(8,128)(2,1)S(1)}, u32[]{:S(2)}, u32[]{:S(2)}) collective-permute-start(bf16[512,128]{1,0:T(8,128)(2,1)S(1)} %get-tuple-element.54), channel_id=1, source_target_pairs={{8,16},{24,32},{40,48},{56,64},{72,80},{88,96},{104,112},{120,128}... | collective-permute-start | bytes 393224 | tf_op jit(solution)/shard_map/ppermute | solution.py:144
  244.4 9.3 %collective-permute-start.9 = (bf16[512,128]{1,0:T(8,128)(2,1)S(1)}, bf16[512,128]{1,0:T(8,128)(2,1)S(1)}, u32[]{:S(2)}, u32[]{:S(2)}) collective-permute-start(bf16[512,128]{1,0:T(8,128)(2,1)S(1)} %get-tuple-element.53), channel_id=1, source_target_pairs={{0,8},{16,24},{32,40},{48,56},{64,72},{80,88},{96,104},{112,120},{... | collective-permute-start | bytes 393224 | tf_op jit(solution)/shard_map/ppermute | solution.py:144
  246.3 10.5 %collective-permute-start.11 = (bf16[512,128]{1,0:T(8,128)(2,1)S(1)}, bf16[512,128]{1,0:T(8,128)(2,1)S(1)}, u32[]{:S(2)}, u32[]{:S(2)}) collective-permute-start(bf16[512,128]{1,0:T(8,128)(2,1)S(1)} %get-tuple-element.47), channel_id=1, source_target_pairs={{0,32},{8,40},{16,48},{24,56},{64,96},{72,104},{80,112},{88,120},{... | collective-permute-start | bytes 393224 | tf_op jit(solution)/shard_map/ppermute | solution.py:144
  248.3 16.5 %collective-permute-start.12 = (bf16[512,128]{1,0:T(8,128)(2,1)S(1)}, bf16[512,128]{1,0:T(8,128)(2,1)S(1)}, u32[]{:S(2)}, u32[]{:S(2)}) collective-permute-start(bf16[512,128]{1,0:T(8,128)(2,1)S(1)} %get-tuple-element.48), channel_id=1, source_target_pairs={{32,64},{40,72},{48,80},{56,88},{96,128},{104,136},{112,144},{120,... | collective-permute-start | bytes 393224 | tf_op jit(solution)/shard_map/ppermute | solution.py:144
  265.7 13.9 %collective-permute-start.13 = (bf16[512,128]{1,0:T(8,128)(2,1)S(1)}, bf16[512,128]{1,0:T(8,128)(2,1)S(1)}, u32[]{:S(2)}, u32[]{:S(2)}) collective-permute-start(bf16[512,128]{1,0:T(8,128)(2,1)S(1)} %get-tuple-element.51), channel_id=1, source_target_pairs={{0,8},{16,24},{32,40},{48,56},{64,72},{80,88},{96,104},{112,120},{... | collective-permute-start | bytes 393224 | tf_op jit(solution)/shard_map/ppermute | solution.py:144
  267.7 13.2 %collective-permute-start.14 = (bf16[512,128]{1,0:T(8,128)(2,1)S(1)}, bf16[512,128]{1,0:T(8,128)(2,1)S(1)}, u32[]{:S(2)}, u32[]{:S(2)}) collective-permute-start(bf16[512,128]{1,0:T(8,128)(2,1)S(1)} %get-tuple-element.52), channel_id=1, source_target_pairs={{8,16},{24,32},{40,48},{56,64},{72,80},{88,96},{104,112},{120,128}... | collective-permute-start | bytes 393224 | tf_op jit(solution)/shard_map/ppermute | solution.py:144
  275.5 7.8 %collective-permute-start.15 = (bf16[512,128]{1,0:T(8,128)(2,1)S(1)}, bf16[512,128]{1,0:T(8,128)(2,1)S(1)}, u32[]{:S(2)}, u32[]{:S(2)}) collective-permute-start(bf16[512,128]{1,0:T(8,128)(2,1)S(1)} %get-tuple-element.43), channel_id=1, source_target_pairs={{0,32},{8,40},{16,48},{24,56},{64,96},{72,104},{80,112},{88,120},{... | collective-permute-start | bytes 393224 | tf_op jit(solution)/shard_map/ppermute | solution.py:144
  277.4 14.7 %collective-permute-start.16 = (bf16[512,128]{1,0:T(8,128)(2,1)S(1)}, bf16[512,128]{1,0:T(8,128)(2,1)S(1)}, u32[]{:S(2)}, u32[]{:S(2)}) collective-permute-start(bf16[512,128]{1,0:T(8,128)(2,1)S(1)} %get-tuple-element.44), channel_id=1, source_target_pairs={{32,64},{40,72},{48,80},{56,88},{96,128},{104,136},{112,144},{120,... | collective-permute-start | bytes 393224 | tf_op jit(solution)/shard_map/ppermute | solution.py:144

commit v6 on v3

--- a/solution.py
+++ b/solution.py
@@ -1,7 +1,11 @@
+import functools
+
 import jax
 import jax.numpy as jnp
 import numpy as np
 from jax import lax
+from jax.experimental import pallas as pl
+from jax.experimental.pallas import tpu as pltpu
 from jax.sharding import Mesh, PartitionSpec as P
 
 P_SIZE = 24
@@ -11,6 +15,8 @@
 HALVES = 2
 SLABS = 4
 CHUNKS = 4
+MARGIN = 640
+TILE = 2 * PLANE
 BOTH = ("half", "slab")
 
 LOW_EDGE = 4.0
@@ -52,25 +58,82 @@
     return 6.0 * values - beside + potential * values
 
 
-def whole_hamiltonian(values, potential, masks):
-    padded = jnp.pad(values, ((0, 0), (PLANE, PLANE)))
-    return flat_hamiltonian(padded, values.shape[1], potential, masks)
-
-
-def filtered_basis(orbitals, potential, kept_count, start_index):
-    orbital_count = orbitals.shape[0]
-    masks = side_masks(G)
-    previous = orbitals.astype(jnp.float32)
-    current = (whole_hamiltonian(previous, potential, masks) - MIDDLE * previous) / SPREAD
-    current = (
-        2.0 * (whole_hamiltonian(current, potential, masks) - MIDDLE * current) / SPREAD - previous
-    )
-    magnitude = jnp.sqrt(jnp.mean(current * current, axis=1, keepdims=True) + 1e-06)
-    active = start_index + jnp.arange(orbital_count, dtype=jnp.int32) < kept_count
-    return jnp.where(active[:, None], current / magnitude, 0.0).astype(jnp.bfloat16)
-
-
-def face_selector(planes):
+def filter_kernel(length, kept_ref, orbital_ref, potential_ref, mask_ref, out_ref, zero_ref, one_ref, two_ref):
+    rows, points = orbital_ref.shape
+    count, _, width = out_ref.shape
+    piece = (width - length) // 2
+    for ref in (zero_ref, one_ref):
+        ref[:, :MARGIN] = jnp.zeros((rows, MARGIN), jnp.float32)
+        ref[:, MARGIN + points :] = jnp.zeros((rows, MARGIN), jnp.float32)
+    for low in range(0, points, TILE):
+        zero_ref[:, MARGIN + low : MARGIN + low + TILE] = orbital_ref[
+            :, low : low + TILE
+        ].astype(jnp.float32)
+
+    def shifted(ref, low, by):
+        return ref[:, MARGIN + low + by : MARGIN + low + by + TILE]
+
+    def stencil(ref, low):
+        beside = shifted(ref, low, PLANE) + shifted(ref, low, -PLANE)
+        for k, by in enumerate((1, -1, P_SIZE, -P_SIZE)):
+            beside = beside + mask_ref[k : k + 1, :] * shifted(ref, low, by)
+        centre = (6.0 - MIDDLE) + potential_ref[:, low : low + TILE]
+        return (centre * shifted(ref, low, 0) - beside) * (1.0 / SPREAD)
+
+    for low in range(0, points, TILE):
+        one_ref[:, MARGIN + low : MARGIN + low + TILE] = stencil(zero_ref, low)
+    squares = jnp.zeros((rows, TILE), jnp.float32)
+    for low in range(0, points, TILE):
+        value = 2.0 * stencil(one_ref, low) - shifted(zero_ref, low, 0)
+        two_ref[:, low : low + TILE] = value
+        squares = squares + value * value
+    mean = jnp.sum(squares, axis=1, keepdims=True) * (1.0 / points)
+    index = kept_ref[1] + pl.program_id(0) * rows
+    index = index + lax.broadcasted_iota(jnp.int32, (rows, 1), 0)
+    scale = jnp.where(index < kept_ref[0], 1.0 / jnp.sqrt(mean + 1e-06), 0.0)
+    middle = points // 2
+
+    def scaled_span(low, size):
+        return (two_ref[:, low : low + size] * scale).astype(jnp.bfloat16)
+
+    for s in range(count):
+        out_ref[s, :, :length] = scaled_span(s * length, length)
+        low = middle - PLANE + s * piece
+        out_ref[s, :, length : length + piece] = scaled_span(low, piece)
+        out_ref[s, :, length + piece :] = scaled_span(low + PLANE, piece)
+
+
+def owned_slabs(orbitals, potential, kept_count, start_index, length):
+    count = HALVES * SLABS
+    width = length + 2 * (PLANE // count)
+    functions, points = orbitals.shape
+    step = functions // CHUNKS
+    where = np.arange(TILE)
+    zpos, ypos = where % P_SIZE, where // P_SIZE % P_SIZE
+    masks = [zpos < P_SIZE - 1, zpos > 0, ypos < P_SIZE - 1, ypos > 0]
+    masks = jnp.asarray(np.stack(masks).astype(np.float32))
+    kept = jnp.stack([kept_count, start_index.astype(jnp.int32)])
+    return pl.pallas_call(
+        functools.partial(filter_kernel, length),
+        out_shape=jax.ShapeDtypeStruct((count, functions, width), jnp.bfloat16),
+        grid=(CHUNKS,),
+        in_specs=[
+            pl.BlockSpec(memory_space=pltpu.SMEM),
+            pl.BlockSpec((step, points), lambda c: (c, 0)),
+            pl.BlockSpec((1, points), lambda c: (0, 0)),
+            pl.BlockSpec((4, TILE), lambda c: (0, 0)),
+        ],
+        out_specs=pl.BlockSpec((count, step, width), lambda c: (0, c, 0)),
+        scratch_shapes=[
+            pltpu.VMEM((step, points + 2 * MARGIN), jnp.float32),
+            pltpu.VMEM((step, points + 2 * MARGIN), jnp.float32),
+            pltpu.VMEM((step, points), jnp.float32),
+        ],
+        compiler_params=pltpu.CompilerParams(vmem_limit_bytes=24 << 20),
+    )(kept, orbitals, potential[None], masks)
+
+
+def face_selector(planes, width):
     grid = np.arange(planes * PLANE, dtype=np.int32).reshape(planes, P_SIZE, P_SIZE)
     last = P_SIZE - 1
     groups = [
@@ -78,7 +141,7 @@
         grid[:, :, last - 1], grid[:, :, last], grid[:, last - 1, :], grid[:, last, :],
     ]
     chosen = jnp.asarray(np.concatenate([g.reshape(-1) for g in groups]))
-    points = jnp.arange(planes * PLANE, dtype=jnp.int32)
+    points = jnp.arange(width, dtype=jnp.int32)
     return (chosen[:, None] == points[None, :]).astype(jnp.bfloat16)
 
 
@@ -88,27 +151,9 @@
     )
 
 
-def owned_basis(orbitals, potential, kept_count, start_index):
-    step = orbitals.shape[0] // CHUNKS
-    chunks = []
-    tied = None
-    for chunk in range(CHUNKS):
-        source = orbitals[chunk * step : (chunk + 1) * step]
-        if tied is not None:
-            source, tied = lax.optimization_barrier((source, tied))
-            chunks[-1] = tied
-        tied = filtered_basis(source, potential, kept_count, start_index + chunk * step)
-        chunks.append(tied)
-    return chunks
-
-
-def slab_rows(chunks, length):
-    slabs = [
-        jnp.concatenate([c[:, s * length : (s + 1) * length] for c in chunks])
-        for s in range(HALVES * SLABS)
-    ]
-    rows = lax.all_to_all(jnp.stack(slabs), BOTH, 0, 0, tiled=True)
-    return rows.reshape(-1, length)
+def slab_rows(slabs):
+    rows = lax.all_to_all(slabs, BOTH, 0, 0, tiled=True)
+    return rows.reshape(-1, rows.shape[2])
 
 
 def pair_swap(value, by, odd):
@@ -181,23 +226,30 @@
     ahead = lax.optimization_barrier(jnp.concatenate([ahead_z, ahead_y]))
     ahead_z, ahead_y = ahead[: ahead.shape[0] // 2], ahead[ahead.shape[0] // 2 :]
 
-    chunks = owned_basis(
-        orbitals[0], potential[0], basis_count[0], band * orbitals.shape[1]
-    )
-    rows = slab_rows(chunks, length)
+    slabs = owned_slabs(
+        orbitals[0], potential[0], basis_count[0], band * orbitals.shape[1], length
+    )
+    rows = slab_rows(slabs)
 
     above = lax.ppermute(
-        rows[:, :PLANE], BOTH, [(i + 1, i) for i in range(HALVES * SLABS - 1)]
-    )
-    faces = transposed_dot(face_selector(planes), rows, 1, 1).astype(jnp.bfloat16)
+        rows[:, :PLANE], "slab", [(i + 1, i) for i in range(SLABS - 1)]
+    )
+    masks = side_masks(length)
+    padded = jnp.pad(rows[:, :length].astype(jnp.float32), ((0, 0), (PLANE, PLANE)))
+    applied = flat_hamiltonian(padded, length, slab_potential, masks)
+    applied = applied.astype(jnp.bfloat16)
+    applied, rows = lax.optimization_barrier((applied, rows))
+
+    faces = transposed_dot(face_selector(planes, length), rows[:, :length], 1, 1)
+    faces = faces.astype(jnp.bfloat16)
     width = 2 * planes * P_SIZE
     other_z = from_behind(faces[:width], "elem", -1)
     other_y = from_behind(faces[width : 2 * width], "elem", -EB)
-
-    padded = jnp.pad(rows.astype(jnp.float32), ((0, 0), (PLANE, PLANE)))
-    applied = flat_hamiltonian(padded, length, slab_potential, side_masks(length))
-    last = rows[:, length - PLANE :]
-    h_self = transposed_dot(rows, applied.astype(jnp.bfloat16), 1, 1)
+    last = rows[:, length - PLANE : length]
+    edges = rows[:, length:]
+    swapped_edges = jnp.roll(edges, edges.shape[1] // 2, axis=1)
+    h_self = transposed_dot(rows[:, :length], applied, 1, 1)
+    h_self = h_self - transposed_dot(edges, swapped_edges, 1, 1)
     h_self = h_self - transposed_dot(last, above, 1, 1) - transposed_dot(above, last, 1, 1)
     weight = -0.5 / PLANE
     h_z = transposed_dot(faces[2 * width : 3 * width], other_z, 0, 0) * weight

time: 282 us -> 317 us (1.12)
  Pallas kernels: 0 us -> 43.2 us
  waiting for transfers between devices: 69.9 us -> 109 us
  starting transfers between devices: 160 us -> 132 us
  other arithmetic: 29.4 us -> 9.13 us
  local copies, waits for them, and re-layouts: 3.16 us -> 7.05 us
    pallas_call x0 -> x1, Pallas kernels: none -> 43.2 us  [owned_slabs(): pl.pallas_call(functools.partial(filter_kernel, length), out_shape=jax.Sh...]
    ppermute x2, starting transfers between devices: 24.1 us -> 4.19 us  [swap_halves(): return lax.ppermute(value, 'half', [(0, 1), (1, 0)])]
    ppermute x8, waiting for transfers between devices: 8.82 us -> 22.8 us  [pair_swap(): return lax.ppermute(value, 'elem', pairs + [(j, i) for i, j in pairs])]
    ppermute x8, starting transfers between devices: 39.1 us -> 26.5 us  [pair_swap(): return lax.ppermute(value, 'elem', pairs + [(j, i) for i, j in pairs])]
    ppermute x1, waiting for transfers between devices: 0.01 us -> 9.92 us  [device_body(): lax.ppermute(rows[:, :PLANE], 'slab', [(i + 1, i) for i in range(SLABS -...]
    div x4 -> x0, other arithmetic: 8.99 us -> none  [filtered_basis(): (whole_hamiltonian(previous, potential, masks) - MIDDLE * previous) / SPREAD]
    all_to_all x2, waiting for transfers between devices: 5.28 us -> 13 us  [sum_over_slabs(): pieces = lax.all_to_all(slices_of(partial), 'slab', 0, 0, tiled=True)]
    reduce_sum x4 -> x0, other arithmetic: 7.1 us -> none  [filtered_basis(): jnp.mean(current * current, axis=1, keepdims=True) + 1e-06]
  transfers between devices with their start and end apart: 22 -> 22, of which waited for: 12 -> 13; matrix products, arithmetic and copies ran while one was open for 6% -> 4% of each run, Pallas kernels for 0% -> 0%
where the time goes in v6:
time: 317 us; the launch traced here: 316 us
  starting transfers between devices  132 us (42%)
  waiting for transfers between devices  109 us (34%)
  Pallas kernels  43.2 us (14%)
  matrix products  13.7 us (4%)
  other arithmetic  9.13 us (3%)
  local copies, waits for them, and re-layouts  7.05 us (2%)
    ppermute x6, starting transfers between devices, from_behind(): lax.ppermute(value, axis, [(i, (i + by) % devices) for i in range(devices)])  60.7 us
    pallas_call x1, Pallas kernels, owned_slabs(): pl.pallas_call(functools.partial(filter_kernel, length), out_shape=jax.Sh...  43.2 us
    all_to_all x1, waiting for transfers between devices, slab_rows(): rows = lax.all_to_all(slabs, BOTH, 0, 0, tiled=True)  31.2 us
    ppermute x8, starting transfers between devices, pair_swap(): return lax.ppermute(value, 'elem', pairs + [(j, i) for i, j in pairs])  26.5 us
    ppermute x8, waiting for transfers between devices, pair_swap(): return lax.ppermute(value, 'elem', pairs + [(j, i) for i, j in pairs])  22.8 us
    ppermute x6, waiting for transfers between devices, from_behind(): lax.ppermute(value, axis, [(i, (i + by) % devices) for i in range(devices)])  20.8 us
    all_to_all x1, starting transfers between devices, slab_rows(): rows = lax.all_to_all(slabs, BOTH, 0, 0, tiled=True)  17.4 us
    dot_general x22, matrix products, transposed_dot(): lax.dot_general(a, b, (((contract_a,), (contract_b,)), ((), ())), preferr...  13.7 us
  transfers between devices with their start and end apart: 22, of which 13 were waited for; matrix products, arithmetic and copies ran while one was open for 4% of the time, Pallas kernels for 0%

profile of v6, /device:TPU:6, one launch (start us, length us, event | category | flops | bytes accessed | tf_op | source)
XLA Modules:
  0.0 315.7 jit_solution(530024068379908235)
XLA Ops:
  0.7 1.5 copy-done
  2.2 0.8 copy-done.1
  3.0 0.7 copy-done.2
  3.7 43.2 %shard_map.64 = bf16[8,64,1872]{2,1,0:T(8,128)(2,1)} custom-call(s32[2]{0:T(128)S(1)} %pad_add_fusion.kept_ref, bf16[64,13824]{1,0:T(8,128)(2,1)S(1)} %bitcast.58, f32[1,13824]{1,0:T(1,128)S(1)} %copy-done.1, f32[4,1152]{1,0:T(4,128)S(1)} %copy-done.2), custom_call_target="tpu_custom_call" | custom-call | tf_op jit(solution)/shard_map/pallas_call | solution.py:116
  47.0 17.4 %all-to-all-start = ((bf16[8,64,1872]{2,1,0:T(8,128)(2,1)}), bf16[8,64,1872]{2,1,0:T(8,128)(2,1)S(1)}, u32[]{:S(2)}, u32[]{:S(2)}) async-start(bf16[8,64,1872]{2,1,0:T(8,128)(2,1)} %shard_map.64), calls=%async_computation | async-start | bytes 3932160 | tf_op jit(solution)/shard_map/all_to_all | solution.py:155
  64.4 0.8 dynamic-slice_reduce_fusion
  65.2 31.2 %all-to-all-done = bf16[8,64,1872]{2,1,0:T(8,128)(2,1)S(1)} async-done(((bf16[8,64,1872]{2,1,0:T(8,128)(2,1)}), bf16[8,64,1872]{2,1,0:T(8,128)(2,1)S(1)}, u32[]{:S(2)}, u32[]{:S(2)}) %all-to-all-start) | async-done | bytes 1916960 | tf_op jit(solution)/shard_map/all_to_all | solution.py:155
  96.8 6.5 %fusion.8 = bf16[512,1728]{1,0:T(8,128)(2,1)} fusion(f32[512,1728]{1,0:T(8,128)S(1)} %slice_convert_fusion, f32[1728]{0:T(1024)S(1)} %dynamic-slice_reduce_fusion, f32[1728]{0:T(1024)S(1)} %get-tuple-element.31, f32[1728]{0:T(1024)S(1)} %get-tuple-element.32, f32[1728]{0:T(1024)S(1)} %get-tuple-element.30, f32[1728]{0:T(1024)S(1)} %get-tuple-element.29), kind=kLoop, calls=%fused_computation.15 | loop fusion | flops 12386304 | bytes 5342976 | tf_op jit(solution)/shard_map/convert_element_type | solution.py:240
  103.4 1.3 fusion.19
  104.7 0.8 fusion.79
  105.5 27.3 %collective-permute-start.2 = (bf16[144,512]{1,0:T(8,128)(2,1)}, bf16[144,512]{1,0:T(8,128)(2,1)}, u32[]{:S(2)}, u32[]{:S(2)}) collective-permute-start(bf16[144,512]{1,0:T(8,128)(2,1)} %get-tuple-element.13), channel_id=1, source_target_pairs={{0,760},{8,0},{16,8},{24,16},{32,24},{40,32},{48,40},{56,48},{64,5... | collective-permute-start | bytes 442376 | tf_op jit(solution)/shard_map/ppermute | solution.py:32
  132.9 21.5 %collective-permute-start.3 = (bf16[144,512]{1,0:T(8,128)(2,1)}, bf16[144,512]{1,0:T(8,128)(2,1)}, u32[]{:S(2)}, u32[]{:S(2)}) collective-permute-start(bf16[144,512]{1,0:T(8,128)(2,1)} %get-tuple-element.14), channel_id=1, source_target_pairs={{0,736},{8,744},{16,752},{24,760},{32,0},{40,8},{48,16},{56,24},{6... | collective-permute-start | bytes 442376 | tf_op jit(solution)/shard_map/ppermute | solution.py:32
  154.6 1.5 collective-permute-start
  156.1 2.7 fusion.15
  158.8 0.4 convolution_subtract_fusion.1
  159.2 9.9 %collective-permute-done = bf16[512,576]{0,1:T(8,128)(2,1)S(1)} collective-permute-done((bf16[512,576]{0,1:T(8,128)(2,1)S(1)}, bf16[512,576]{0,1:T(8,128)(2,1)S(1)}, u32[]{:S(2)}, u32[]{:S(2)}) %collective-permute-start) | collective-permute-done | bytes 589856 | tf_op jit(solution)/shard_map/ppermute | solution.py:234
  169.1 0.6 fusion.41
  169.7 1.4 fusion.24
  171.1 6.7 %all-to-all-start.1 = ((bf16[4,1,128,512]{3,2,1,0:T(8,128)(2,1)}), bf16[4,1,128,512]{3,2,1,0:T(8,128)(2,1)S(1)}, u32[]{:S(2)}, u32[]{:S(2)}) async-start(bf16[4,1,128,512]{3,2,1,0:T(8,128)(2,1)} %bitcast.4), calls=%async_computation.1 | async-start | bytes 1048576 | tf_op jit(solution)/shard_map/all_to_all | solution.py:199
  177.8 1.2 fusion.22
  179.1 1.2 fusion.23
  180.4 1.1 maximum_bitcast_fusion
  181.4 3.6 %all-to-all-done.1 = bf16[4,1,128,512]{3,2,1,0:T(8,128)(2,1)S(1)} async-done(((bf16[4,1,128,512]{3,2,1,0:T(8,128)(2,1)}), bf16[4,1,128,512]{3,2,1,0:T(8,128)(2,1)S(1)}, u32[]{:S(2)}, u32[]{:S(2)}) %all-to-all-start.1) | async-done | bytes 524320 | tf_op jit(solution)/shard_map/all_to_all | solution.py:199
  185.0 5.6 %all-to-all-start.3 = ((bf16[4,2,128,512]{3,2,1,0:T(8,128)(2,1)}), bf16[4,2,128,512]{3,2,1,0:T(8,128)(2,1)S(1)}, u32[]{:S(2)}, u32[]{:S(2)}) async-start(bf16[4,2,128,512]{3,2,1,0:T(8,128)(2,1)} %maximum_bitcast_fusion), calls=%async_computation.3 | async-start | bytes 2097152 | tf_op jit(solution)/shard_map/all_to_all | solution.py:199
  190.7 2.2 collective-permute-start.1
  192.9 9.4 %all-to-all-done.3 = bf16[4,2,128,512]{3,2,1,0:T(8,128)(2,1)S(1)} async-done(((bf16[4,2,128,512]{3,2,1,0:T(8,128)(2,1)}), bf16[4,2,128,512]{3,2,1,0:T(8,128)(2,1)S(1)}, u32[]{:S(2)}, u32[]{:S(2)}) %all-to-all-start.3) | async-done | bytes 1048608 | tf_op jit(solution)/shard_map/all_to_all | solution.py:199
  202.5 2.0 collective-permute-start.4
  204.6 0.9 broadcast_in_dim.9
  205.5 5.5 %all-to-all-start.2 = ((bf16[4,1,128,512]{3,2,1,0:T(8,128)(2,1)}), bf16[4,1,128,512]{3,2,1,0:T(8,128)(2,1)S(1)}, u32[]{:S(2)}, u32[]{:S(2)}) async-start(bf16[4,1,128,512]{3,2,1,0:T(8,128)(2,1)} %broadcast_in_dim.9), calls=%async_computation.2 | async-start | bytes 1048576 | tf_op jit(solution)/shard_map/all_to_all | solution.py:211
  211.0 11.3 %collective-permute-done.4 = bf16[2,128,512]{2,1,0:T(8,128)(2,1)S(1)} collective-permute-done((bf16[2,128,512]{2,1,0:T(8,128)(2,1)S(1)}, bf16[2,128,512]{2,1,0:T(8,128)(2,1)S(1)}, u32[]{:S(2)}, u32[]{:S(2)}) %collective-permute-start.4) | collective-permute-done | bytes 262176 | tf_op jit(solution)/shard_map/ppermute | solution.py:36
  222.4 1.1 broadcast_in_dim.10
  223.5 4.5 %all-to-all-start.4 = ((bf16[4,2,128,512]{3,2,1,0:T(8,128)(2,1)}), bf16[4,2,128,512]{3,2,1,0:T(8,128)(2,1)S(1)}, u32[]{:S(2)}, u32[]{:S(2)}) async-start(bf16[4,2,128,512]{3,2,1,0:T(8,128)(2,1)} %broadcast_in_dim.10), calls=%async_computation.4 | async-start | bytes 2097152 | tf_op jit(solution)/shard_map/all_to_all | solution.py:211
  228.0 2.6 collective-permute-start.5
  230.6 5.4 %collective-permute-start.6 = (bf16[512,128]{1,0:T(8,128)(2,1)S(1)}, bf16[512,128]{1,0:T(8,128)(2,1)S(1)}, u32[]{:S(2)}, u32[]{:S(2)}) collective-permute-start(bf16[512,128]{1,0:T(8,128)(2,1)S(1)} %bitcast.83), channel_id=1, source_target_pairs={{0,736},{8,744},{16,752},{24,760},{32,0},{40,8},{48,16},{56,24},{6... | collective-permute-start | bytes 393224 | tf_op jit(solution)/shard_map/ppermute | solution.py:32
  236.1 5.1 %collective-permute-done.6 = bf16[512,128]{1,0:T(8,128)(2,1)S(1)} collective-permute-done((bf16[512,128]{1,0:T(8,128)(2,1)S(1)}, bf16[512,128]{1,0:T(8,128)(2,1)S(1)}, u32[]{:S(2)}, u32[]{:S(2)}) %collective-permute-start.6) | collective-permute-done | bytes 131104 | tf_op jit(solution)/shard_map/ppermute | solution.py:32
  241.3 0.3 fusion.75
  241.6 0.3 convolution_convert_fusion.5
  242.0 1.9 collective-permute-start.7
  243.9 0.3 convolution_convert_fusion.4
  244.3 1.9 collective-permute-start.8
  246.5 9.1 %collective-permute-done.7 = bf16[512,128]{1,0:T(8,128)(2,1)S(1)} collective-permute-done((bf16[512,128]{1,0:T(8,128)(2,1)S(1)}, bf16[512,128]{1,0:T(8,128)(2,1)S(1)}, u32[]{:S(2)}, u32[]{:S(2)}) %collective-permute-start.7) | collective-permute-done | bytes 131104 | tf_op jit(solution)/shard_map/ppermute | solution.py:32
  255.7 6.5 %collective-permute-done.8 = bf16[512,128]{1,0:T(8,128)(2,1)S(1)} collective-permute-done((bf16[512,128]{1,0:T(8,128)(2,1)S(1)}, bf16[512,128]{1,0:T(8,128)(2,1)S(1)}, u32[]{:S(2)}, u32[]{:S(2)}) %collective-permute-start.8) | collective-permute-done | bytes 131104 | tf_op jit(solution)/shard_map/ppermute | solution.py:32
  262.1 0.3 fusion.40
  262.4 0.4 convolution_convert_fusion.3
  262.8 0.4 broadcast_select_fusion.3
  263.1 3.8 %collective-permute-start.10 = (bf16[512,128]{1,0:T(8,128)(2,1)S(1)}, bf16[512,128]{1,0:T(8,128)(2,1)S(1)}, u32[]{:S(2)}, u32[]{:S(2)}) collective-permute-start(bf16[512,128]{1,0:T(8,128)(2,1)S(1)} %get-tuple-element.26), channel_id=1, source_target_pairs={{8,16},{24,32},{40,48},{56,64},{72,80},{88,96},{104,112},{120,128}... | collective-permute-start | bytes 393224 | tf_op jit(solution)/shard_map/ppermute | solution.py:163
  267.0 1.9 collective-permute-start.9
  268.9 1.9 collective-permute-start.11
  270.8 5.5 %collective-permute-start.12 = (bf16[512,128]{1,0:T(8,128)(2,1)S(1)}, bf16[512,128]{1,0:T(8,128)(2,1)S(1)}, u32[]{:S(2)}, u32[]{:S(2)}) collective-permute-start(bf16[512,128]{1,0:T(8,128)(2,1)S(1)} %get-tuple-element.20), channel_id=1, source_target_pairs={{32,64},{40,72},{48,80},{56,88},{96,128},{104,136},{112,144},{120,... | collective-permute-start | bytes 393224 | tf_op jit(solution)/shard_map/ppermute | solution.py:163
  276.6 0.3 convolution_add_fusion.3
  276.9 2.7 collective-permute-done.11
  279.6 7.9 %collective-permute-done.12 = bf16[512,128]{1,0:T(8,128)(2,1)S(1)} collective-permute-done((bf16[512,128]{1,0:T(8,128)(2,1)S(1)}, bf16[512,128]{1,0:T(8,128)(2,1)S(1)}, u32[]{:S(2)}, u32[]{:S(2)}) %collective-permute-start.12) | collective-permute-done | bytes 131104 | tf_op jit(solution)/shard_map/ppermute | solution.py:163
  287.6 0.3 fusion.39
  287.9 0.4 convolution_convert_fusion.1
  288.2 0.4 broadcast_select_fusion.1
  288.6 1.9 collective-permute-start.13
  290.5 7.5 %collective-permute-start.14 = (bf16[512,128]{1,0:T(8,128)(2,1)S(1)}, bf16[512,128]{1,0:T(8,128)(2,1)S(1)}, u32[]{:S(2)}, u32[]{:S(2)}) collective-permute-start(bf16[512,128]{1,0:T(8,128)(2,1)S(1)} %get-tuple-element.24), channel_id=1, source_target_pairs={{8,16},{24,32},{40,48},{56,64},{72,80},{88,96},{104,112},{120,128}... | collective-permute-start | bytes 393224 | tf_op jit(solution)/shard_map/ppermute | solution.py:163
  298.1 1.9 collective-permute-start.15
  300.0 1.9 collective-permute-start.16
  302.2 1.5 collective-permute-done.14
  304.0 1.8 collective-permute-done.15
  305.8 8.8 %collective-permute-done.16 = bf16[512,128]{1,0:T(8,128)(2,1)S(1)} collective-permute-done((bf16[512,128]{1,0:T(8,128)(2,1)S(1)}, bf16[512,128]{1,0:T(8,128)(2,1)S(1)}, u32[]{:S(2)}, u32[]{:S(2)}) %collective-permute-start.16) | collective-permute-done | bytes 131104 | tf_op jit(solution)/shard_map/ppermute | solution.py:163
  314.7 0.3 multiply_reduce_fusion
  315.0 0.7 fusion.57
  (38 shorter events, 2.5 us)
Async XLA Ops:
  0.7 1.5 copy-start
  2.2 0.8 copy-start.1
  3.0 0.7 copy-start.2
  47.0 49.5 %all-to-all-start = ((bf16[8,64,1872]{2,1,0:T(8,128)(2,1)}), bf16[8,64,1872]{2,1,0:T(8,128)(2,1)S(1)}, u32[]{:S(2)}, u32[]{:S(2)}) async-start(bf16[8,64,1872]{2,1,0:T(8,128)(2,1)} %shard_map.64), calls=%async_computation | async-start | bytes 3932160 | tf_op jit(solution)/shard_map/all_to_all | solution.py:155
  96.7 6.7 %copy-start.6 = (s32[576]{0:T(1024)S(1)}, s32[576]{0:T(1024)}, u32[]{:S(2)}) copy-start(s32[576]{0:T(1024)} %constant.125.clone) | copy-start | bytes 6916
  104.7 28.1 %copy-start.4 = (bf16[576,512]{1,0:T(8,128)(2,1)}, bf16[576,512]{1,0:T(8,128)(2,1)S(1)}, u32[]{:S(2)}) copy-start(bf16[576,512]{1,0:T(8,128)(2,1)S(1)} %fusion.19) | copy-start | bytes 1769476
  105.5 72.3 %collective-permute-start.2 = (bf16[144,512]{1,0:T(8,128)(2,1)}, bf16[144,512]{1,0:T(8,128)(2,1)}, u32[]{:S(2)}, u32[]{:S(2)}) collective-permute-start(bf16[144,512]{1,0:T(8,128)(2,1)} %get-tuple-element.13), channel_id=1, source_target_pairs={{0,760},{8,0},{16,8},{24,16},{32,24},{40,32},{48,40},{56,48},{64,5... | collective-permute-start | bytes 442376 | tf_op jit(solution)/shard_map/ppermute | solution.py:32
  132.9 46.2 %collective-permute-start.3 = (bf16[144,512]{1,0:T(8,128)(2,1)}, bf16[144,512]{1,0:T(8,128)(2,1)}, u32[]{:S(2)}, u32[]{:S(2)}) collective-permute-start(bf16[144,512]{1,0:T(8,128)(2,1)} %get-tuple-element.14), channel_id=1, source_target_pairs={{0,736},{8,744},{16,752},{24,760},{32,0},{40,8},{48,16},{56,24},{6... | collective-permute-start | bytes 442376 | tf_op jit(solution)/shard_map/ppermute | solution.py:32
  154.6 14.5 %collective-permute-start = (bf16[512,576]{0,1:T(8,128)(2,1)S(1)}, bf16[512,576]{0,1:T(8,128)(2,1)S(1)}, u32[]{:S(2)}, u32[]{:S(2)}) collective-permute-start(bf16[512,576]{0,1:T(8,128)(2,1)S(1)} %copy.11), channel_id=1, source_target_pairs={{1,0},{2,1},{3,2},{5,4},{6,5},{7,6},{9,8},{10,9},{11,10},{13,12},{... | collective-permute-start | bytes 1769480 | tf_op jit(solution)/shard_map/ppermute | solution.py:234
  159.2 18.7 %copy-start.5 = (bf16[576,512]{1,0:T(8,128)(2,1)S(1)}, bf16[576,512]{1,0:T(8,128)(2,1)}, u32[]{:S(2)}) copy-start(bf16[576,512]{1,0:T(8,128)(2,1)} %copy-done.4) | copy-start | bytes 1769476
  171.1 13.9 %all-to-all-start.1 = ((bf16[4,1,128,512]{3,2,1,0:T(8,128)(2,1)}), bf16[4,1,128,512]{3,2,1,0:T(8,128)(2,1)S(1)}, u32[]{:S(2)}, u32[]{:S(2)}) async-start(bf16[4,1,128,512]{3,2,1,0:T(8,128)(2,1)} %bitcast.4), calls=%async_computation.1 | async-start | bytes 1048576 | tf_op jit(solution)/shard_map/all_to_all | solution.py:199
  185.0 17.2 %all-to-all-start.3 = ((bf16[4,2,128,512]{3,2,1,0:T(8,128)(2,1)}), bf16[4,2,128,512]{3,2,1,0:T(8,128)(2,1)S(1)}, u32[]{:S(2)}, u32[]{:S(2)}) async-start(bf16[4,2,128,512]{3,2,1,0:T(8,128)(2,1)} %maximum_bitcast_fusion), calls=%async_computation.3 | async-start | bytes 2097152 | tf_op jit(solution)/shard_map/all_to_all | solution.py:199
  190.7 37.3 %copy-start.3 = (bf16[1,512,128]{2,1,0:T(8,128)(2,1)S(1)}, bf16[1,512,128]{2,1,0:T(8,128)(2,1)}, u32[]{:S(2)}) copy-start(bf16[1,512,128]{2,1,0:T(8,128)(2,1)} %param.9) | copy-start | bytes 393220
  190.7 13.9 %collective-permute-start.1 = (bf16[1,128,512]{2,1,0:T(8,128)(2,1)S(1)}, bf16[1,128,512]{2,1,0:T(8,128)(2,1)S(1)}, u32[]{:S(2)}, u32[]{:S(2)}) collective-permute-start(bf16[1,128,512]{2,1,0:T(8,128)(2,1)S(1)} %bitcast.84), channel_id=1, source_target_pairs={{0,4},{4,0},{1,5},{5,1},{2,6},{6,2},{3,7},{7,3},{8,12},{12,8},{9,1... | collective-permute-start | bytes 393224 | tf_op jit(solution)/shard_map/ppermute | solution.py:36
  202.5 19.8 %collective-permute-start.4 = (bf16[2,128,512]{2,1,0:T(8,128)(2,1)S(1)}, bf16[2,128,512]{2,1,0:T(8,128)(2,1)S(1)}, u32[]{:S(2)}, u32[]{:S(2)}) collective-permute-start(bf16[2,128,512]{2,1,0:T(8,128)(2,1)S(1)} %reduce_sum.37), channel_id=1, source_target_pairs={{0,4},{4,0},{1,5},{5,1},{2,6},{6,2},{3,7},{7,3},{8,12},{12,8},{9,1... | collective-permute-start | bytes 786440 | tf_op jit(solution)/shard_map/ppermute | solution.py:36
  205.5 16.9 %all-to-all-start.2 = ((bf16[4,1,128,512]{3,2,1,0:T(8,128)(2,1)}), bf16[4,1,128,512]{3,2,1,0:T(8,128)(2,1)S(1)}, u32[]{:S(2)}, u32[]{:S(2)}) async-start(bf16[4,1,128,512]{3,2,1,0:T(8,128)(2,1)} %broadcast_in_dim.9), calls=%async_computation.2 | async-start | bytes 1048576 | tf_op jit(solution)/shard_map/all_to_all | solution.py:211
  223.5 18.1 %all-to-all-start.4 = ((bf16[4,2,128,512]{3,2,1,0:T(8,128)(2,1)}), bf16[4,2,128,512]{3,2,1,0:T(8,128)(2,1)S(1)}, u32[]{:S(2)}, u32[]{:S(2)}) async-start(bf16[4,2,128,512]{3,2,1,0:T(8,128)(2,1)} %broadcast_in_dim.10), calls=%async_computation.4 | async-start | bytes 2097152 | tf_op jit(solution)/shard_map/all_to_all | solution.py:211
  228.0 8.1 %collective-permute-start.5 = (bf16[512,128]{1,0:T(8,128)(2,1)S(1)}, bf16[512,128]{1,0:T(8,128)(2,1)S(1)}, u32[]{:S(2)}, u32[]{:S(2)}) collective-permute-start(bf16[512,128]{1,0:T(8,128)(2,1)S(1)} %bitcast.82), channel_id=1, source_target_pairs={{0,760},{8,0},{16,8},{24,16},{32,24},{40,32},{48,40},{56,48},{64,5... | collective-permute-start | bytes 393224 | tf_op jit(solution)/shard_map/ppermute | solution.py:32
  230.6 10.6 %collective-permute-start.6 = (bf16[512,128]{1,0:T(8,128)(2,1)S(1)}, bf16[512,128]{1,0:T(8,128)(2,1)S(1)}, u32[]{:S(2)}, u32[]{:S(2)}) collective-permute-start(bf16[512,128]{1,0:T(8,128)(2,1)S(1)} %bitcast.83), channel_id=1, source_target_pairs={{0,736},{8,744},{16,752},{24,760},{32,0},{40,8},{48,16},{56,24},{6... | collective-permute-start | bytes 393224 | tf_op jit(solution)/shard_map/ppermute | solution.py:32
  242.0 13.7 %collective-permute-start.7 = (bf16[512,128]{1,0:T(8,128)(2,1)S(1)}, bf16[512,128]{1,0:T(8,128)(2,1)S(1)}, u32[]{:S(2)}, u32[]{:S(2)}) collective-permute-start(bf16[512,128]{1,0:T(8,128)(2,1)S(1)} %convolution_convert_fusion.5), channel_id=1, source_target_pairs={{0,8},{8,16},{16,24},{24,32},{32,40},{40,48},{48,56},{56,64},{64,7... | collective-permute-start | bytes 393224 | tf_op jit(solution)/shard_map/ppermute | solution.py:32
  244.3 17.8 %collective-permute-start.8 = (bf16[512,128]{1,0:T(8,128)(2,1)S(1)}, bf16[512,128]{1,0:T(8,128)(2,1)S(1)}, u32[]{:S(2)}, u32[]{:S(2)}) collective-permute-start(bf16[512,128]{1,0:T(8,128)(2,1)S(1)} %convolution_convert_fusion.4), channel_id=1, source_target_pairs={{0,32},{8,40},{16,48},{24,56},{32,64},{40,72},{48,80},{56,88},{64,... | collective-permute-start | bytes 393224 | tf_op jit(solution)/shard_map/ppermute | solution.py:32
  263.1 13.5 %collective-permute-start.10 = (bf16[512,128]{1,0:T(8,128)(2,1)S(1)}, bf16[512,128]{1,0:T(8,128)(2,1)S(1)}, u32[]{:S(2)}, u32[]{:S(2)}) collective-permute-start(bf16[512,128]{1,0:T(8,128)(2,1)S(1)} %get-tuple-element.26), channel_id=1, source_target_pairs={{8,16},{24,32},{40,48},{56,64},{72,80},{88,96},{104,112},{120,128}... | collective-permute-start | bytes 393224 | tf_op jit(solution)/shard_map/ppermute | solution.py:163
  267.0 9.6 %collective-permute-start.9 = (bf16[512,128]{1,0:T(8,128)(2,1)S(1)}, bf16[512,128]{1,0:T(8,128)(2,1)S(1)}, u32[]{:S(2)}, u32[]{:S(2)}) collective-permute-start(bf16[512,128]{1,0:T(8,128)(2,1)S(1)} %get-tuple-element.25), channel_id=1, source_target_pairs={{0,8},{16,24},{32,40},{48,56},{64,72},{80,88},{96,104},{112,120},{... | collective-permute-start | bytes 393224 | tf_op jit(solution)/shard_map/ppermute | solution.py:163
  268.9 10.7 %collective-permute-start.11 = (bf16[512,128]{1,0:T(8,128)(2,1)S(1)}, bf16[512,128]{1,0:T(8,128)(2,1)S(1)}, u32[]{:S(2)}, u32[]{:S(2)}) collective-permute-start(bf16[512,128]{1,0:T(8,128)(2,1)S(1)} %get-tuple-element.19), channel_id=1, source_target_pairs={{0,32},{8,40},{16,48},{24,56},{64,96},{72,104},{80,112},{88,120},{... | collective-permute-start | bytes 393224 | tf_op jit(solution)/shard_map/ppermute | solution.py:163
  270.8 16.7 %collective-permute-start.12 = (bf16[512,128]{1,0:T(8,128)(2,1)S(1)}, bf16[512,128]{1,0:T(8,128)(2,1)S(1)}, u32[]{:S(2)}, u32[]{:S(2)}) collective-permute-start(bf16[512,128]{1,0:T(8,128)(2,1)S(1)} %get-tuple-element.20), channel_id=1, source_target_pairs={{32,64},{40,72},{48,80},{56,88},{96,128},{104,136},{112,144},{120,... | collective-permute-start | bytes 393224 | tf_op jit(solution)/shard_map/ppermute | solution.py:163
  288.6 13.6 %collective-permute-start.13 = (bf16[512,128]{1,0:T(8,128)(2,1)S(1)}, bf16[512,128]{1,0:T(8,128)(2,1)S(1)}, u32[]{:S(2)}, u32[]{:S(2)}) collective-permute-start(bf16[512,128]{1,0:T(8,128)(2,1)S(1)} %get-tuple-element.23), channel_id=1, source_target_pairs={{0,8},{16,24},{32,40},{48,56},{64,72},{80,88},{96,104},{112,120},{... | collective-permute-start | bytes 393224 | tf_op jit(solution)/shard_map/ppermute | solution.py:163
  290.5 13.2 %collective-permute-start.14 = (bf16[512,128]{1,0:T(8,128)(2,1)S(1)}, bf16[512,128]{1,0:T(8,128)(2,1)S(1)}, u32[]{:S(2)}, u32[]{:S(2)}) collective-permute-start(bf16[512,128]{1,0:T(8,128)(2,1)S(1)} %get-tuple-element.24), channel_id=1, source_target_pairs={{8,16},{24,32},{40,48},{56,64},{72,80},{88,96},{104,112},{120,128}... | collective-permute-start | bytes 393224 | tf_op jit(solution)/shard_map/ppermute | solution.py:163
  298.1 7.8 %collective-permute-start.15 = (bf16[512,128]{1,0:T(8,128)(2,1)S(1)}, bf16[512,128]{1,0:T(8,128)(2,1)S(1)}, u32[]{:S(2)}, u32[]{:S(2)}) collective-permute-start(bf16[512,128]{1,0:T(8,128)(2,1)S(1)} %get-tuple-element.15), channel_id=1, source_target_pairs={{0,32},{8,40},{16,48},{24,56},{64,96},{72,104},{80,112},{88,120},{... | collective-permute-start | bytes 393224 | tf_op jit(solution)/shard_map/ppermute | solution.py:163
  300.0 14.7 %collective-permute-start.16 = (bf16[512,128]{1,0:T(8,128)(2,1)S(1)}, bf16[512,128]{1,0:T(8,128)(2,1)S(1)}, u32[]{:S(2)}, u32[]{:S(2)}) collective-permute-start(bf16[512,128]{1,0:T(8,128)(2,1)S(1)} %get-tuple-element.16), channel_id=1, source_target_pairs={{32,64},{40,72},{48,80},{56,88},{96,128},{104,136},{112,144},{120,... | collective-permute-start | bytes 393224 | tf_op jit(solution)/shard_map/ppermute | solution.py:163

commit v7 on v5

--- a/solution.py
+++ b/solution.py
@@ -97,10 +97,10 @@
     chunks = []
     tied = None
     for chunk in range(CHUNKS):
+        if tied is not None:
+            orbitals, tied = lax.optimization_barrier((orbitals, tied))
+            chunks[-1] = tied
         source = orbitals[chunk * step : (chunk + 1) * step]
-        if tied is not None:
-            source, tied = lax.optimization_barrier((source, tied))
-            chunks[-1] = tied
         tied = filtered_basis(source, potential, kept_count, start_index + chunk * step)
         chunks.append(tied)
     return chunks
@@ -163,8 +163,8 @@
         running = transposed_dot(h_self, current, 1, 0)
     else:
         ahead_z, ahead_y, running = given
+        behind_y = from_behind(back_y, "elem", EB)
         behind_z = from_behind(back_z, "elem", 1)
-        behind_y = from_behind(back_y, "elem", EB)
     running = running + transposed_dot(h_z, ahead_z, 1, 0)
     running = running + transposed_dot(h_y, ahead_y, 1, 0)
     running = running + behind_z.astype(jnp.float32) + behind_y.astype(jnp.float32)
@@ -215,20 +215,23 @@
     above = lax.ppermute(
         rows[:, :PLANE], "slab", [(i + 1, i) for i in range(SLABS - 1)]
     )
+    masks = side_masks(length)
     padded = jnp.pad(rows[:, :length].astype(jnp.float32), ((0, 0), (PLANE, PLANE)))
-    applied = flat_hamiltonian(padded, length, slab_potential, side_masks(length))
-    last = rows[:, length - PLANE : length]
-    edges = rows[:, length:]
-    swapped_edges = jnp.roll(edges, edges.shape[1] // 2, axis=1)
-    h_self = transposed_dot(rows[:, :length], applied.astype(jnp.bfloat16), 1, 1)
-    h_self = h_self - transposed_dot(edges, swapped_edges, 1, 1)
-    h_self = h_self - transposed_dot(last, above, 1, 1) - transposed_dot(above, last, 1, 1)
+    applied = flat_hamiltonian(padded, length, slab_potential, masks)
+    applied = applied.astype(jnp.bfloat16)
+    applied = lax.optimization_barrier(applied)
 
     faces = transposed_dot(face_selector(planes, length), rows[:, :length], 1, 1)
     faces = faces.astype(jnp.bfloat16)
     width = 2 * planes * P_SIZE
     other_z = from_behind(faces[:width], "elem", -1)
     other_y = from_behind(faces[width : 2 * width], "elem", -EB)
+    last = rows[:, length - PLANE : length]
+    edges = rows[:, length:]
+    swapped_edges = jnp.roll(edges, edges.shape[1] // 2, axis=1)
+    h_self = transposed_dot(rows[:, :length], applied, 1, 1)
+    h_self = h_self - transposed_dot(edges, swapped_edges, 1, 1)
+    h_self = h_self - transposed_dot(last, above, 1, 1) - transposed_dot(above, last, 1, 1)
     weight = -0.5 / PLANE
     h_z = transposed_dot(faces[2 * width : 3 * width], other_z, 0, 0) * weight
     h_y = transposed_dot(faces[3 * width :], other_y, 0, 0) * weight

time: 294 us -> 292 us (level)
  matrix products: 26.1 us -> 13.6 us
  waiting for transfers between devices: 98.9 us -> 109 us
    dot_general x22, matrix products: 26.1 us -> 13.6 us  [transposed_dot(): lax.dot_general(a, b, (((contract_a,), (contract_b,)), ((), ())), preferr...]
    ppermute x1, waiting for transfers between devices: 0.01 us -> 10.1 us  [device_body(): lax.ppermute(rows[:, :PLANE], 'slab', [(i + 1, i) for i in range(SLABS -...]
    convert_element_type x0 -> x1, other arithmetic: none -> 6.56 us  [device_body(): applied = applied.astype(jnp.bfloat16)]
    div x4, other arithmetic: 8.99 us -> 5.7 us  [filtered_basis(): (whole_hamiltonian(previous, potential, masks) - MIDDLE * previous) / SPREAD]
  transfers between devices with their start and end apart: 22 -> 22, of which waited for: 13 -> 14; matrix products, arithmetic and copies ran while one was open for 9% -> 7% of each run, Pallas kernels for 0% -> 0%
where the time goes in v7:
time: 292 us; the launch traced here: 291 us
  starting transfers between devices  136 us (47%)
  waiting for transfers between devices  109 us (37%)
  other arithmetic  26.2 us (9%)
  matrix products  13.6 us (5%)
  local copies, waits for them, and re-layouts  4.24 us (1%)
    ppermute x6, starting transfers between devices, from_behind(): lax.ppermute(value, axis, [(i, (i + by) % devices) for i in range(devices)])  64.8 us
    all_to_all x1, waiting for transfers between devices, slab_rows(): rows = lax.all_to_all(slabs, BOTH, 0, 0, tiled=True)  31.2 us
    ppermute x8, starting transfers between devices, pair_swap(): return lax.ppermute(value, 'elem', pairs + [(j, i) for i, j in pairs])  25.7 us
    ppermute x8, waiting for transfers between devices, pair_swap(): return lax.ppermute(value, 'elem', pairs + [(j, i) for i, j in pairs])  23.6 us
    ppermute x6, waiting for transfers between devices, from_behind(): lax.ppermute(value, axis, [(i, (i + by) % devices) for i in range(devices)])  20.9 us
    all_to_all x1, starting transfers between devices, slab_rows(): rows = lax.all_to_all(slabs, BOTH, 0, 0, tiled=True)  17.4 us
    dot_general x22, matrix products, transposed_dot(): lax.dot_general(a, b, (((contract_a,), (contract_b,)), ((), ())), preferr...  13.6 us
    all_to_all x2, waiting for transfers between devices, sum_over_slabs(): pieces = lax.all_to_all(slices_of(partial), 'slab', 0, 0, tiled=True)  13.2 us
  transfers between devices with their start and end apart: 22, of which 14 were waited for; matrix products, arithmetic and copies ran while one was open for 7% of the time, Pallas kernels for 0%

profile of v7, /device:TPU:6, one launch (start us, length us, event | category | flops | bytes accessed | tf_op | source)
XLA Modules:
  0.0 291.2 jit_solution(7761719475917086671)
XLA Ops:
  0.1 1.2 bitcast_convert_fusion
  1.3 0.9 reduce.3
  2.3 1.4 broadcast_multiply_fusion.3
  3.7 1.5 multiply_reduce_fusion.3
  6.2 1.4 broadcast_multiply_fusion.2
  7.6 1.5 multiply_reduce_fusion.2
  9.4 1.4 broadcast_multiply_fusion.1
  10.8 2.5 multiply_reduce_fusion.1
  13.3 1.3 select_convert_fusion.1.refs_2_
  14.7 1.4 broadcast_multiply_fusion
  16.1 1.5 multiply_reduce_fusion
  17.9 1.7 shard_map.55
  19.6 17.4 %all-to-all-start = ((bf16[8,64,1872]{2,1,0:T(8,128)(2,1)}), bf16[8,64,1872]{2,1,0:T(8,128)(2,1)S(1)}, u32[]{:S(2)}, u32[]{:S(2)}) async-start(bf16[8,64,1872]{2,1,0:T(8,128)(2,1)} %shard_map.55), calls=%async_computation | async-start | bytes 3932160 | tf_op jit(solution)/shard_map/all_to_all | solution.py:136
  37.0 0.8 dynamic-slice_reduce_fusion
  37.9 31.2 %all-to-all-done = bf16[8,64,1872]{2,1,0:T(8,128)(2,1)S(1)} async-done(((bf16[8,64,1872]{2,1,0:T(8,128)(2,1)}), bf16[8,64,1872]{2,1,0:T(8,128)(2,1)S(1)}, u32[]{:S(2)}, u32[]{:S(2)}) %all-to-all-start) | async-done | bytes 1916960 | tf_op jit(solution)/shard_map/all_to_all | solution.py:136
  69.7 1.3 fusion.19
  71.0 0.8 fusion.123
  71.8 27.3 %collective-permute-start.2 = (bf16[144,512]{1,0:T(8,128)(2,1)}, bf16[144,512]{1,0:T(8,128)(2,1)}, u32[]{:S(2)}, u32[]{:S(2)}) collective-permute-start(bf16[144,512]{1,0:T(8,128)(2,1)} %get-tuple-element.37), channel_id=1, source_target_pairs={{0,760},{8,0},{16,8},{24,16},{32,24},{40,32},{48,40},{56,48},{64,5... | collective-permute-start | bytes 442376 | tf_op jit(solution)/shard_map/ppermute | solution.py:30
  99.1 21.5 %collective-permute-start.3 = (bf16[144,512]{1,0:T(8,128)(2,1)}, bf16[144,512]{1,0:T(8,128)(2,1)}, u32[]{:S(2)}, u32[]{:S(2)}) collective-permute-start(bf16[144,512]{1,0:T(8,128)(2,1)} %get-tuple-element.38), channel_id=1, source_target_pairs={{0,736},{8,744},{16,752},{24,760},{32,0},{40,8},{48,16},{56,24},{6... | collective-permute-start | bytes 442376 | tf_op jit(solution)/shard_map/ppermute | solution.py:30
  120.6 6.6 %fusion.8 = bf16[512,1728]{1,0:T(8,128)(2,1)} fusion(f32[512,1728]{1,0:T(8,128)S(1)} %slice_convert_fusion, f32[1728]{0:T(1024)S(1)} %dynamic-slice_reduce_fusion, f32[1728]{0:T(1024)S(1)} %get-tuple-element.63, f32[1728]{0:T(1024)S(1)} %get-tuple-element.64, f32[1728]{0:T(1024)S(1)} %get-tuple-element.62, f32[1728]{0:T(1024)S(1)} %get-tuple-element.61), kind=kLoop, calls=%fused_computation.15 | loop fusion | flops 12386304 | bytes 5342976 | tf_op jit(solution)/shard_map/convert_element_type | solution.py:221
  127.4 1.3 collective-permute-start
  128.8 2.6 fusion.15
  131.4 0.4 convolution_subtract_fusion.1
  131.8 10.1 %collective-permute-done = bf16[512,576]{0,1:T(8,128)(2,1)S(1)} collective-permute-done((bf16[512,576]{0,1:T(8,128)(2,1)S(1)}, bf16[512,576]{0,1:T(8,128)(2,1)S(1)}, u32[]{:S(2)}, u32[]{:S(2)}) %collective-permute-start) | collective-permute-done | bytes 589856 | tf_op jit(solution)/shard_map/ppermute | solution.py:215
  142.0 0.6 fusion.74
  142.6 1.4 fusion.24
  144.0 6.7 %all-to-all-start.1 = ((bf16[4,1,128,512]{3,2,1,0:T(8,128)(2,1)}), bf16[4,1,128,512]{3,2,1,0:T(8,128)(2,1)S(1)}, u32[]{:S(2)}, u32[]{:S(2)}) async-start(bf16[4,1,128,512]{3,2,1,0:T(8,128)(2,1)} %bitcast.6), calls=%async_computation.1 | async-start | bytes 1048576 | tf_op jit(solution)/shard_map/all_to_all | solution.py:180
  150.7 1.2 fusion.22
  151.9 1.2 fusion.23
  153.2 1.1 maximum_bitcast_fusion
  154.3 3.6 %all-to-all-done.1 = bf16[4,1,128,512]{3,2,1,0:T(8,128)(2,1)S(1)} async-done(((bf16[4,1,128,512]{3,2,1,0:T(8,128)(2,1)}), bf16[4,1,128,512]{3,2,1,0:T(8,128)(2,1)S(1)}, u32[]{:S(2)}, u32[]{:S(2)}) %all-to-all-start.1) | async-done | bytes 524320 | tf_op jit(solution)/shard_map/all_to_all | solution.py:180
  157.9 5.6 %all-to-all-start.3 = ((bf16[4,2,128,512]{3,2,1,0:T(8,128)(2,1)}), bf16[4,2,128,512]{3,2,1,0:T(8,128)(2,1)S(1)}, u32[]{:S(2)}, u32[]{:S(2)}) async-start(bf16[4,2,128,512]{3,2,1,0:T(8,128)(2,1)} %maximum_bitcast_fusion), calls=%async_computation.3 | async-start | bytes 2097152 | tf_op jit(solution)/shard_map/all_to_all | solution.py:180
  163.5 2.0 collective-permute-start.1
  165.5 9.6 %all-to-all-done.3 = bf16[4,2,128,512]{3,2,1,0:T(8,128)(2,1)S(1)} async-done(((bf16[4,2,128,512]{3,2,1,0:T(8,128)(2,1)}), bf16[4,2,128,512]{3,2,1,0:T(8,128)(2,1)S(1)}, u32[]{:S(2)}, u32[]{:S(2)}) %all-to-all-start.3) | async-done | bytes 1048608 | tf_op jit(solution)/shard_map/all_to_all | solution.py:180
  175.4 2.0 collective-permute-start.4
  177.5 0.8 broadcast_in_dim.44
  178.3 5.5 %all-to-all-start.2 = ((bf16[4,1,128,512]{3,2,1,0:T(8,128)(2,1)}), bf16[4,1,128,512]{3,2,1,0:T(8,128)(2,1)S(1)}, u32[]{:S(2)}, u32[]{:S(2)}) async-start(bf16[4,1,128,512]{3,2,1,0:T(8,128)(2,1)} %broadcast_in_dim.44), calls=%async_computation.2 | async-start | bytes 1048576 | tf_op jit(solution)/shard_map/all_to_all | solution.py:192
  183.8 9.7 %collective-permute-done.4 = bf16[2,128,512]{2,1,0:T(8,128)(2,1)S(1)} collective-permute-done((bf16[2,128,512]{2,1,0:T(8,128)(2,1)S(1)}, bf16[2,128,512]{2,1,0:T(8,128)(2,1)S(1)}, u32[]{:S(2)}, u32[]{:S(2)}) %collective-permute-start.4) | collective-permute-done | bytes 262176 | tf_op jit(solution)/shard_map/ppermute | solution.py:34
  193.6 1.1 broadcast_in_dim.45
  194.7 4.5 %all-to-all-start.4 = ((bf16[4,2,128,512]{3,2,1,0:T(8,128)(2,1)}), bf16[4,2,128,512]{3,2,1,0:T(8,128)(2,1)S(1)}, u32[]{:S(2)}, u32[]{:S(2)}) async-start(bf16[4,2,128,512]{3,2,1,0:T(8,128)(2,1)} %broadcast_in_dim.45), calls=%async_computation.4 | async-start | bytes 2097152 | tf_op jit(solution)/shard_map/all_to_all | solution.py:192
  199.2 2.5 collective-permute-start.5
  201.7 9.7 %collective-permute-start.6 = (bf16[512,128]{1,0:T(8,128)(2,1)S(1)}, bf16[512,128]{1,0:T(8,128)(2,1)S(1)}, u32[]{:S(2)}, u32[]{:S(2)}) collective-permute-start(bf16[512,128]{1,0:T(8,128)(2,1)S(1)} %bitcast.97), channel_id=1, source_target_pairs={{0,736},{8,744},{16,752},{24,760},{32,0},{40,8},{48,16},{56,24},{6... | collective-permute-start | bytes 393224 | tf_op jit(solution)/shard_map/ppermute | solution.py:30
  211.4 3.3 %collective-permute-done.6 = bf16[512,128]{1,0:T(8,128)(2,1)S(1)} collective-permute-done((bf16[512,128]{1,0:T(8,128)(2,1)S(1)}, bf16[512,128]{1,0:T(8,128)(2,1)S(1)}, u32[]{:S(2)}, u32[]{:S(2)}) %collective-permute-start.6) | collective-permute-done | bytes 131104 | tf_op jit(solution)/shard_map/ppermute | solution.py:30
  215.5 1.9 collective-permute-start.7
  217.8 1.9 collective-permute-start.8
  220.1 10.8 %collective-permute-done.7 = bf16[512,128]{1,0:T(8,128)(2,1)S(1)} collective-permute-done((bf16[512,128]{1,0:T(8,128)(2,1)S(1)}, bf16[512,128]{1,0:T(8,128)(2,1)S(1)}, u32[]{:S(2)}, u32[]{:S(2)}) %collective-permute-start.7) | collective-permute-done | bytes 131104 | tf_op jit(solution)/shard_map/ppermute | solution.py:30
  230.9 6.7 %collective-permute-done.8 = bf16[512,128]{1,0:T(8,128)(2,1)S(1)} collective-permute-done((bf16[512,128]{1,0:T(8,128)(2,1)S(1)}, bf16[512,128]{1,0:T(8,128)(2,1)S(1)}, u32[]{:S(2)}, u32[]{:S(2)}) %collective-permute-start.8) | collective-permute-done | bytes 131104 | tf_op jit(solution)/shard_map/ppermute | solution.py:30
  237.9 0.4 convolution_convert_fusion.3
  238.2 0.4 broadcast_select_fusion.3
  238.6 3.9 %collective-permute-start.10 = (bf16[512,128]{1,0:T(8,128)(2,1)S(1)}, bf16[512,128]{1,0:T(8,128)(2,1)S(1)}, u32[]{:S(2)}, u32[]{:S(2)}) collective-permute-start(bf16[512,128]{1,0:T(8,128)(2,1)S(1)} %get-tuple-element.50), channel_id=1, source_target_pairs={{8,16},{24,32},{40,48},{56,64},{72,80},{88,96},{104,112},{120,128}... | collective-permute-start | bytes 393224 | tf_op jit(solution)/shard_map/ppermute | solution.py:144
  242.5 1.9 collective-permute-start.9
  244.4 1.9 collective-permute-start.11
  246.3 4.5 %collective-permute-start.12 = (bf16[512,128]{1,0:T(8,128)(2,1)S(1)}, bf16[512,128]{1,0:T(8,128)(2,1)S(1)}, u32[]{:S(2)}, u32[]{:S(2)}) collective-permute-start(bf16[512,128]{1,0:T(8,128)(2,1)S(1)} %get-tuple-element.44), channel_id=1, source_target_pairs={{32,64},{40,72},{48,80},{56,88},{96,128},{104,136},{112,144},{120,... | collective-permute-start | bytes 393224 | tf_op jit(solution)/shard_map/ppermute | solution.py:144
  251.1 0.7 collective-permute-done.10
  252.1 2.8 collective-permute-done.11
  254.9 7.9 %collective-permute-done.12 = bf16[512,128]{1,0:T(8,128)(2,1)S(1)} collective-permute-done((bf16[512,128]{1,0:T(8,128)(2,1)S(1)}, bf16[512,128]{1,0:T(8,128)(2,1)S(1)}, u32[]{:S(2)}, u32[]{:S(2)}) %collective-permute-start.12) | collective-permute-done | bytes 131104 | tf_op jit(solution)/shard_map/ppermute | solution.py:144
  263.9 1.9 collective-permute-start.13
  265.8 7.8 %collective-permute-start.14 = (bf16[512,128]{1,0:T(8,128)(2,1)S(1)}, bf16[512,128]{1,0:T(8,128)(2,1)S(1)}, u32[]{:S(2)}, u32[]{:S(2)}) collective-permute-start(bf16[512,128]{1,0:T(8,128)(2,1)S(1)} %get-tuple-element.48), channel_id=1, source_target_pairs={{8,16},{24,32},{40,48},{56,64},{72,80},{88,96},{104,112},{120,128}... | collective-permute-start | bytes 393224 | tf_op jit(solution)/shard_map/ppermute | solution.py:144
  273.6 1.9 collective-permute-start.15
  275.5 1.9 collective-permute-start.16
  277.8 1.3 collective-permute-done.14
  279.3 2.0 collective-permute-done.15
  281.4 8.8 %collective-permute-done.16 = bf16[512,128]{1,0:T(8,128)(2,1)S(1)} collective-permute-done((bf16[512,128]{1,0:T(8,128)(2,1)S(1)}, bf16[512,128]{1,0:T(8,128)(2,1)S(1)}, u32[]{:S(2)}, u32[]{:S(2)}) %collective-permute-start.16) | collective-permute-done | bytes 131104 | tf_op jit(solution)/shard_map/ppermute | solution.py:144
  290.5 0.7 fusion.90
  (59 shorter events, 6.4 us)
Async XLA Ops:
  0.0 2.3 copy-start
  19.6 49.5 %all-to-all-start = ((bf16[8,64,1872]{2,1,0:T(8,128)(2,1)}), bf16[8,64,1872]{2,1,0:T(8,128)(2,1)S(1)}, u32[]{:S(2)}, u32[]{:S(2)}) async-start(bf16[8,64,1872]{2,1,0:T(8,128)(2,1)} %shard_map.55), calls=%async_computation | async-start | bytes 3932160 | tf_op jit(solution)/shard_map/all_to_all | solution.py:136
  69.0 0.7 copy-start.4
  71.0 49.6 %copy-start.2 = (bf16[576,512]{1,0:T(8,128)(2,1)}, bf16[576,512]{1,0:T(8,128)(2,1)S(1)}, u32[]{:S(2)}) copy-start(bf16[576,512]{1,0:T(8,128)(2,1)S(1)} %fusion.19) | copy-start | bytes 1769476
  71.8 78.8 %collective-permute-start.2 = (bf16[144,512]{1,0:T(8,128)(2,1)}, bf16[144,512]{1,0:T(8,128)(2,1)}, u32[]{:S(2)}, u32[]{:S(2)}) collective-permute-start(bf16[144,512]{1,0:T(8,128)(2,1)} %get-tuple-element.37), channel_id=1, source_target_pairs={{0,760},{8,0},{16,8},{24,16},{32,24},{40,32},{48,40},{56,48},{64,5... | collective-permute-start | bytes 442376 | tf_op jit(solution)/shard_map/ppermute | solution.py:30
  99.1 52.8 %collective-permute-start.3 = (bf16[144,512]{1,0:T(8,128)(2,1)}, bf16[144,512]{1,0:T(8,128)(2,1)}, u32[]{:S(2)}, u32[]{:S(2)}) collective-permute-start(bf16[144,512]{1,0:T(8,128)(2,1)} %get-tuple-element.38), channel_id=1, source_target_pairs={{0,736},{8,744},{16,752},{24,760},{32,0},{40,8},{48,16},{56,24},{6... | collective-permute-start | bytes 442376 | tf_op jit(solution)/shard_map/ppermute | solution.py:30
  127.4 14.5 %collective-permute-start = (bf16[512,576]{0,1:T(8,128)(2,1)S(1)}, bf16[512,576]{0,1:T(8,128)(2,1)S(1)}, u32[]{:S(2)}, u32[]{:S(2)}) collective-permute-start(bf16[512,576]{0,1:T(8,128)(2,1)S(1)} %copy.10), channel_id=1, source_target_pairs={{1,0},{2,1},{3,2},{5,4},{6,5},{7,6},{9,8},{10,9},{11,10},{13,12},{... | collective-permute-start | bytes 1769480 | tf_op jit(solution)/shard_map/ppermute | solution.py:215
  142.6 8.1 %copy-start.3 = (bf16[576,512]{1,0:T(8,128)(2,1)S(1)}, bf16[576,512]{1,0:T(8,128)(2,1)}, u32[]{:S(2)}) copy-start(bf16[576,512]{1,0:T(8,128)(2,1)} %copy-done.2) | copy-start | bytes 1769476
  144.0 13.9 %all-to-all-start.1 = ((bf16[4,1,128,512]{3,2,1,0:T(8,128)(2,1)}), bf16[4,1,128,512]{3,2,1,0:T(8,128)(2,1)S(1)}, u32[]{:S(2)}, u32[]{:S(2)}) async-start(bf16[4,1,128,512]{3,2,1,0:T(8,128)(2,1)} %bitcast.6), calls=%async_computation.1 | async-start | bytes 1048576 | tf_op jit(solution)/shard_map/all_to_all | solution.py:180
  157.9 17.2 %all-to-all-start.3 = ((bf16[4,2,128,512]{3,2,1,0:T(8,128)(2,1)}), bf16[4,2,128,512]{3,2,1,0:T(8,128)(2,1)S(1)}, u32[]{:S(2)}, u32[]{:S(2)}) async-start(bf16[4,2,128,512]{3,2,1,0:T(8,128)(2,1)} %maximum_bitcast_fusion), calls=%async_computation.3 | async-start | bytes 2097152 | tf_op jit(solution)/shard_map/all_to_all | solution.py:180
  163.5 13.9 %collective-permute-start.1 = (bf16[1,128,512]{2,1,0:T(8,128)(2,1)S(1)}, bf16[1,128,512]{2,1,0:T(8,128)(2,1)S(1)}, u32[]{:S(2)}, u32[]{:S(2)}) collective-permute-start(bf16[1,128,512]{2,1,0:T(8,128)(2,1)S(1)} %bitcast.98), channel_id=1, source_target_pairs={{0,4},{4,0},{1,5},{5,1},{2,6},{6,2},{3,7},{7,3},{8,12},{12,8},{9,1... | collective-permute-start | bytes 393224 | tf_op jit(solution)/shard_map/ppermute | solution.py:34
  175.4 18.2 %collective-permute-start.4 = (bf16[2,128,512]{2,1,0:T(8,128)(2,1)S(1)}, bf16[2,128,512]{2,1,0:T(8,128)(2,1)S(1)}, u32[]{:S(2)}, u32[]{:S(2)}) collective-permute-start(bf16[2,128,512]{2,1,0:T(8,128)(2,1)S(1)} %reduce_sum.77), channel_id=1, source_target_pairs={{0,4},{4,0},{1,5},{5,1},{2,6},{6,2},{3,7},{7,3},{8,12},{12,8},{9,1... | collective-permute-start | bytes 786440 | tf_op jit(solution)/shard_map/ppermute | solution.py:34
  178.3 15.3 %all-to-all-start.2 = ((bf16[4,1,128,512]{3,2,1,0:T(8,128)(2,1)}), bf16[4,1,128,512]{3,2,1,0:T(8,128)(2,1)S(1)}, u32[]{:S(2)}, u32[]{:S(2)}) async-start(bf16[4,1,128,512]{3,2,1,0:T(8,128)(2,1)} %broadcast_in_dim.44), calls=%async_computation.2 | async-start | bytes 1048576 | tf_op jit(solution)/shard_map/all_to_all | solution.py:192
  183.8 15.4 %copy-start.1 = (bf16[1,512,128]{2,1,0:T(8,128)(2,1)S(1)}, bf16[1,512,128]{2,1,0:T(8,128)(2,1)}, u32[]{:S(2)}) copy-start(bf16[1,512,128]{2,1,0:T(8,128)(2,1)} %param.8) | copy-start | bytes 393220
  194.7 20.4 %all-to-all-start.4 = ((bf16[4,2,128,512]{3,2,1,0:T(8,128)(2,1)}), bf16[4,2,128,512]{3,2,1,0:T(8,128)(2,1)S(1)}, u32[]{:S(2)}, u32[]{:S(2)}) async-start(bf16[4,2,128,512]{3,2,1,0:T(8,128)(2,1)} %broadcast_in_dim.45), calls=%async_computation.4 | async-start | bytes 2097152 | tf_op jit(solution)/shard_map/all_to_all | solution.py:192
  199.2 12.2 %collective-permute-start.5 = (bf16[512,128]{1,0:T(8,128)(2,1)S(1)}, bf16[512,128]{1,0:T(8,128)(2,1)S(1)}, u32[]{:S(2)}, u32[]{:S(2)}) collective-permute-start(bf16[512,128]{1,0:T(8,128)(2,1)S(1)} %bitcast.96), channel_id=1, source_target_pairs={{0,760},{8,0},{16,8},{24,16},{32,24},{40,32},{48,40},{56,48},{64,5... | collective-permute-start | bytes 393224 | tf_op jit(solution)/shard_map/ppermute | solution.py:30
  201.7 13.1 %collective-permute-start.6 = (bf16[512,128]{1,0:T(8,128)(2,1)S(1)}, bf16[512,128]{1,0:T(8,128)(2,1)S(1)}, u32[]{:S(2)}, u32[]{:S(2)}) collective-permute-start(bf16[512,128]{1,0:T(8,128)(2,1)S(1)} %bitcast.97), channel_id=1, source_target_pairs={{0,736},{8,744},{16,752},{24,760},{32,0},{40,8},{48,16},{56,24},{6... | collective-permute-start | bytes 393224 | tf_op jit(solution)/shard_map/ppermute | solution.py:30
  215.5 15.4 %collective-permute-start.7 = (bf16[512,128]{1,0:T(8,128)(2,1)S(1)}, bf16[512,128]{1,0:T(8,128)(2,1)S(1)}, u32[]{:S(2)}, u32[]{:S(2)}) collective-permute-start(bf16[512,128]{1,0:T(8,128)(2,1)S(1)} %convolution_convert_fusion.5), channel_id=1, source_target_pairs={{0,8},{8,16},{16,24},{24,32},{32,40},{40,48},{48,56},{56,64},{64,7... | collective-permute-start | bytes 393224 | tf_op jit(solution)/shard_map/ppermute | solution.py:30
  217.8 19.7 %collective-permute-start.8 = (bf16[512,128]{1,0:T(8,128)(2,1)S(1)}, bf16[512,128]{1,0:T(8,128)(2,1)S(1)}, u32[]{:S(2)}, u32[]{:S(2)}) collective-permute-start(bf16[512,128]{1,0:T(8,128)(2,1)S(1)} %convolution_convert_fusion.4), channel_id=1, source_target_pairs={{0,32},{8,40},{16,48},{24,56},{32,64},{40,72},{48,80},{56,88},{64,... | collective-permute-start | bytes 393224 | tf_op jit(solution)/shard_map/ppermute | solution.py:30
  238.6 13.2 %collective-permute-start.10 = (bf16[512,128]{1,0:T(8,128)(2,1)S(1)}, bf16[512,128]{1,0:T(8,128)(2,1)S(1)}, u32[]{:S(2)}, u32[]{:S(2)}) collective-permute-start(bf16[512,128]{1,0:T(8,128)(2,1)S(1)} %get-tuple-element.50), channel_id=1, source_target_pairs={{8,16},{24,32},{40,48},{56,64},{72,80},{88,96},{104,112},{120,128}... | collective-permute-start | bytes 393224 | tf_op jit(solution)/shard_map/ppermute | solution.py:144
  242.5 9.3 %collective-permute-start.9 = (bf16[512,128]{1,0:T(8,128)(2,1)S(1)}, bf16[512,128]{1,0:T(8,128)(2,1)S(1)}, u32[]{:S(2)}, u32[]{:S(2)}) collective-permute-start(bf16[512,128]{1,0:T(8,128)(2,1)S(1)} %get-tuple-element.49), channel_id=1, source_target_pairs={{0,8},{16,24},{32,40},{48,56},{64,72},{80,88},{96,104},{112,120},{... | collective-permute-start | bytes 393224 | tf_op jit(solution)/shard_map/ppermute | solution.py:144
  244.4 10.5 %collective-permute-start.11 = (bf16[512,128]{1,0:T(8,128)(2,1)S(1)}, bf16[512,128]{1,0:T(8,128)(2,1)S(1)}, u32[]{:S(2)}, u32[]{:S(2)}) collective-permute-start(bf16[512,128]{1,0:T(8,128)(2,1)S(1)} %get-tuple-element.43), channel_id=1, source_target_pairs={{0,32},{8,40},{16,48},{24,56},{64,96},{72,104},{80,112},{88,120},{... | collective-permute-start | bytes 393224 | tf_op jit(solution)/shard_map/ppermute | solution.py:144
  246.3 16.6 %collective-permute-start.12 = (bf16[512,128]{1,0:T(8,128)(2,1)S(1)}, bf16[512,128]{1,0:T(8,128)(2,1)S(1)}, u32[]{:S(2)}, u32[]{:S(2)}) collective-permute-start(bf16[512,128]{1,0:T(8,128)(2,1)S(1)} %get-tuple-element.44), channel_id=1, source_target_pairs={{32,64},{40,72},{48,80},{56,88},{96,128},{104,136},{112,144},{120,... | collective-permute-start | bytes 393224 | tf_op jit(solution)/shard_map/ppermute | solution.py:144
  263.9 13.9 %collective-permute-start.13 = (bf16[512,128]{1,0:T(8,128)(2,1)S(1)}, bf16[512,128]{1,0:T(8,128)(2,1)S(1)}, u32[]{:S(2)}, u32[]{:S(2)}) collective-permute-start(bf16[512,128]{1,0:T(8,128)(2,1)S(1)} %get-tuple-element.47), channel_id=1, source_target_pairs={{0,8},{16,24},{32,40},{48,56},{64,72},{80,88},{96,104},{112,120},{... | collective-permute-start | bytes 393224 | tf_op jit(solution)/shard_map/ppermute | solution.py:144
  265.8 13.2 %collective-permute-start.14 = (bf16[512,128]{1,0:T(8,128)(2,1)S(1)}, bf16[512,128]{1,0:T(8,128)(2,1)S(1)}, u32[]{:S(2)}, u32[]{:S(2)}) collective-permute-start(bf16[512,128]{1,0:T(8,128)(2,1)S(1)} %get-tuple-element.48), channel_id=1, source_target_pairs={{8,16},{24,32},{40,48},{56,64},{72,80},{88,96},{104,112},{120,128}... | collective-permute-start | bytes 393224 | tf_op jit(solution)/shard_map/ppermute | solution.py:144
  273.6 7.8 %collective-permute-start.15 = (bf16[512,128]{1,0:T(8,128)(2,1)S(1)}, bf16[512,128]{1,0:T(8,128)(2,1)S(1)}, u32[]{:S(2)}, u32[]{:S(2)}) collective-permute-start(bf16[512,128]{1,0:T(8,128)(2,1)S(1)} %get-tuple-element.39), channel_id=1, source_target_pairs={{0,32},{8,40},{16,48},{24,56},{64,96},{72,104},{80,112},{88,120},{... | collective-permute-start | bytes 393224 | tf_op jit(solution)/shard_map/ppermute | solution.py:144
  275.5 14.7 %collective-permute-start.16 = (bf16[512,128]{1,0:T(8,128)(2,1)S(1)}, bf16[512,128]{1,0:T(8,128)(2,1)S(1)}, u32[]{:S(2)}, u32[]{:S(2)}) collective-permute-start(bf16[512,128]{1,0:T(8,128)(2,1)S(1)} %get-tuple-element.40), channel_id=1, source_target_pairs={{32,64},{40,72},{48,80},{56,88},{96,128},{104,136},{112,144},{120,... | collective-permute-start | bytes 393224 | tf_op jit(solution)/shard_map/ppermute | solution.py:144
